TPU v7x, 32 devices: a whole 2x2x4 slice. The times are simulated.
32 devices in a mesh: fold: 2 (over x), slab: 2 (over core), strip: 8 (over z, y).
Axes of the slice: x: 2, y: 2, z: 4, core: 2. Of those that a mesh axis runs over, the one named last changes fastest.
Arguments:
- volume: bfloat16 [128, 8, 128, 256], P('fold', 'slab', 'strip'), parts along dimension 0, may hold values from -6 to 6
- target: bfloat16 [512, 4, 64, 128], P('fold', 'slab', 'strip'), parts along dimension 0, may hold values from -6 to 6
- strided_weight: bfloat16 [128, 1728], replicated, may hold values from -0.15625 to 0.15625
- dilated_weight: bfloat16 [256, 3456], replicated, may hold values from -0.109375 to 0.109375
Outputs:
- prediction: bfloat16 [512, 4, 64, 128], P('fold', 'slab', 'strip'), parts along dimension 0
- strided_grad: float32 [256, 1728], P(('fold', 'strip')), parts along dimension 0
- dilated_grad: float32 [512, 3456], P(('fold', 'strip')), parts along dimension 0
There are 2 independent parts, one for each index of `fold`. A program takes and returns all parts, laid end to end along the dimension named above; an argument that names none is the same for every part. Nothing has to cross between parts.
All inputs are finite; a program needn't handle non-finite values.
Results may differ from a plain program's by a relative error of at most 0.005.
Values may be sent and summed in bfloat16 or wider, within the bound.
No kernel may reach another device: no remote copies, remote signals or barrier semaphores. Data moves between devices by JAX's collectives and lax.ppermute only.
A program may use at most 128 MiB of HBM per device.

v0:
```python
import math

import jax
import jax.numpy as jnp
from jax import lax
from jax.sharding import PartitionSpec as P

DILATION_FACTOR = 2


def passed_along(value, axis, steps):
    count = lax.axis_size(axis)
    initial, last = (max(0, -steps), min(count, count - steps))
    return lax.ppermute(value, axis, [(source, source + steps) for source in range(initial, last)])


def with_halo(value, sides, width):
    for axis, dim in sides:
        devices, length = (lax.axis_size(axis), value.shape[dim])
        up = [(i, (i + 1) % devices) for i in range(devices - 1)]
        down = [(j, i) for i, j in up]
        last = lax.slice_in_dim(value, length - width, length, axis=dim)
        initial = lax.slice_in_dim(value, 0, width, axis=dim)
        before = lax.ppermute(last, axis, up)
        after = lax.ppermute(initial, axis, down)
        value = jnp.concatenate([before, value, after], axis=dim)
    return value


def silu_slope(value):
    sigma = jax.nn.sigmoid(value)
    return sigma * (1.0 + value * (1.0 - sigma))


def tap_list():
    return [
        (inline_stride, crossline_stride, time_stride)
        for inline_stride in range(3)
        for crossline_stride in range(3)
        for time_stride in range(3)
    ]


def time_moved(field, offset):
    length = field.shape[3]
    if offset == 0:
        return field
    if offset > 0:
        padded = jnp.pad(field, ((0, 0), (0, 0), (0, 0), (offset, 0)))
        return padded[:, :, :, :length]
    padded = jnp.pad(field, ((0, 0), (0, 0), (0, 0), (0, -offset)))
    return padded[:, :, :, -offset:]


def strided_columns(extended, row_halfspan, column_halfspan, depth_halfspan):
    channel_count = extended.shape[0]
    even_time = extended[:, :, :, 0::2]
    odd_time = extended[:, :, :, 1::2]
    variants = [time_moved(odd_time, 1), even_time, odd_time]
    pieces = []
    for inline_stride, crossline_stride, time_stride in tap_list():
        source = variants[time_stride]
        pieces.append(
            lax.slice(
                source,
                (0, inline_stride, crossline_stride, 0),
                (
                    channel_count,
                    inline_stride + 2 * row_halfspan - 1,
                    crossline_stride + 2 * column_halfspan - 1,
                    depth_halfspan,
                ),
                (1, 2, 2, 1),
            )
        )
    return jnp.concatenate(pieces, axis=0).reshape(
        27 * channel_count, row_halfspan * column_halfspan * depth_halfspan
    )


def dilated_columns(padded, row_halfspan, column_halfspan, depth_halfspan, tap_spacing, flipped):
    channel_count = padded.shape[0]
    variants = [time_moved(padded, -(step - 1) * tap_spacing) for step in range(3)]
    pieces = []
    for inline_stride, crossline_stride, time_stride in tap_list():
        if flipped:
            inline_stride, crossline_stride, time_stride = (
                2 - inline_stride,
                2 - crossline_stride,
                2 - time_stride,
            )
        source = variants[time_stride]
        pieces.append(
            lax.slice(
                source,
                (0, inline_stride * tap_spacing, crossline_stride * tap_spacing, 0),
                (
                    channel_count,
                    inline_stride * tap_spacing + row_halfspan,
                    crossline_stride * tap_spacing + column_halfspan,
                    depth_halfspan,
                ),
            )
        )
    return jnp.concatenate(pieces, axis=0).reshape(
        27 * channel_count, row_halfspan * column_halfspan * depth_halfspan
    )


def local(volume, target, strided_weight, dilated_weight):
    channels_in, rows_in, cols_in, depth = volume.shape
    mid_channels = strided_weight.shape[0]
    out_channels = dilated_weight.shape[0]
    row_halfspan, column_halfspan, depth_halfspan = (rows_in // 2, cols_in // 2, depth // 2)
    tap_spacing = DILATION_FACTOR
    lower_plane = passed_along(volume[:, -1:, :, :], "slab", 1)
    extended = jnp.concatenate([lower_plane, volume], axis=1)
    left_plane = passed_along(extended[:, :, -1:, :], "strip", 1)
    extended = jnp.concatenate([left_plane, extended], axis=2)
    input_cols = strided_columns(extended, row_halfspan, column_halfspan, depth_halfspan)
    preact = jnp.dot(strided_weight, input_cols, preferred_element_type=jnp.float32)
    hidden_state = (
        jax.nn.silu(preact)
        .astype(jnp.bfloat16)
        .reshape(mid_channels, row_halfspan, column_halfspan, depth_halfspan)
    )
    hidden_state_padded = with_halo(hidden_state, (("slab", 1), ("strip", 2)), DILATION_FACTOR)
    hidden_cols = dilated_columns(
        hidden_state_padded, row_halfspan, column_halfspan, depth_halfspan, tap_spacing, False
    )
    output = jnp.dot(dilated_weight, hidden_cols, preferred_element_type=jnp.float32)
    prediction = output.astype(jnp.bfloat16).reshape(
        out_channels, row_halfspan, column_halfspan, depth_halfspan
    )
    cell_count = (
        row_halfspan
        * column_halfspan
        * depth_halfspan
        * lax.axis_size("slab")
        * lax.axis_size("strip")
    )
    loss_scale = 1.0 / math.sqrt(cell_count)
    residual_state = (
        (output - target.astype(jnp.float32).reshape(out_channels, -1)) * loss_scale
    ).astype(jnp.bfloat16)
    dims = (((1,), (1,)), ((), ()))
    dilated_grad = lax.dot_general(
        residual_state, hidden_cols, dims, preferred_element_type=jnp.float32
    )
    residual_state_padded = with_halo(
        residual_state.reshape(out_channels, row_halfspan, column_halfspan, depth_halfspan),
        (("slab", 1), ("strip", 2)),
        DILATION_FACTOR,
    )
    residual_cols = dilated_columns(
        residual_state_padded, row_halfspan, column_halfspan, depth_halfspan, tap_spacing, True
    )
    weight_taps = (
        dilated_weight.reshape(out_channels, 27, mid_channels)
        .transpose(1, 0, 2)
        .reshape(27 * out_channels, mid_channels)
    )
    hidden_grad = lax.dot_general(
        weight_taps, residual_cols, (((0,), (0,)), ((), ())), preferred_element_type=jnp.float32
    )
    preact_grad = (hidden_grad * silu_slope(preact)).astype(jnp.bfloat16)
    strided_grad = lax.dot_general(
        preact_grad, input_cols, dims, preferred_element_type=jnp.float32
    )
    strided_grad, dilated_grad = lax.psum((strided_grad, dilated_grad), ("slab", "strip"))
    position = lax.axis_index("strip")
    strip_count = lax.axis_size("strip")
    rows_first = mid_channels // strip_count
    rows_second = out_channels // strip_count
    strided_grad = lax.dynamic_slice_in_dim(strided_grad, position * rows_first, rows_first, 0)
    dilated_grad = lax.dynamic_slice_in_dim(dilated_grad, position * rows_second, rows_second, 0)
    return (prediction, strided_grad, dilated_grad)


def solution(mesh):
    return jax.shard_map(
        local,
        mesh=mesh,
        in_specs=(P("fold", "slab", "strip", None), P("fold", "slab", "strip", None), P(), P()),
        out_specs=(
            P("fold", "slab", "strip", None),
            P(("fold", "strip"), None),
            P(("fold", "strip"), None),
        ),
        check_vma=False,
    )
```

profile of v0, /device:TPU:0, one launch (start us, length us, event | category | flops | bytes accessed | tf_op | source)
XLA Modules:
  0.0 458.8 jit_solution(15833876541508158338)
XLA Ops:
  7.2 1.1 slice.388
  8.5 2.4 collective-permute-start
  10.9 1.5 collective-permute-done
  12.5 2.8 constant_dynamic-update-slice_fusion
  15.2 4.3 collective-permute-start.1
  19.5 4.0 collective-permute-done.1
  23.5 1.8 pad_maximum_fusion.1
  25.3 57.6 %slice.306 = bf16[64,5,17,128]{3,0,2,1:T(8,128)(2,1)S(1)} slice(bf16[64,5,17,256]{3,0,2,1:T(8,128)(2,1)} %pad_maximum_fusion.1), slice={[0:64:1], [0:5:1], [0:17:1], [1:256:2]} | slice | bytes 2785280 | tf_op jit(solution)/shard_map/slice | solution.py:58
  82.8 57.6 %slice.309 = bf16[64,5,17,128]{3,0,2,1:T(8,128)(2,1)S(1)} slice(bf16[64,5,17,256]{3,0,2,1:T(8,128)(2,1)} %pad_maximum_fusion.1), slice={[0:64:1], [0:5:1], [0:17:1], [0:256:2]} | slice | bytes 2785280 | tf_op jit(solution)/shard_map/slice | solution.py:57
  142.1 18.9 %copy.21 = bf16[1728,2,8,128]{3,2,1,0:T(8,128)(2,1)S(1)} copy(bf16[1728,2,8,128]{3,0,2,1:T(8,128)(2,1)S(1)} %slice_dynamic-update-slice_fusion) | data formatting | bytes 14155776 | tf_op jit(solution)/shard_map/concatenate | solution.py:76
  161.0 4.0 multiply_convert_fusion
  165.0 1.3 collective-permute-start.3
  166.3 3.1 collective-permute-start.2
  169.4 1.5 collective-permute-done.2
  171.9 4.4 collective-permute-start.4
  176.3 1.5 collective-permute-start.5
  177.8 1.9 copy.22
  179.6 14.3 %collective-permute-done.4 = bf16[128,6,2,128]{0,3,2,1:T(8,128)(2,1)S(1)} collective-permute-done((bf16[128,6,2,128]{0,3,2,1:T(8,128)(2,1)}, bf16[128,6,2,128]{0,3,2,1:T(8,128)(2,1)S(1)}, u32[]{:S(2)}, u32[]{:S(2)}) %collective-permute-start.4) | collective-permute-done | bytes 393248 | tf_op jit(solution)/shard_map/ppermute | solution.py:24
  194.3 4.3 pad_slice_fusion.19
  203.0 5.4 %fusion.12 = (bf16[256,2048]{0,1:T(8,128)(2,1)S(1)}, bf16[256,2048]{0,1:T(8,128)(2,1)}) fusion(f32[256,2,8,128]{0,3,2,1:T(8,128)S(1)} %copy-done.15, bf16[3456,2048]{0,1:T(8,128)(2,1)S(1)} %constant_dynamic-update-slice_fusion.2, bf16[256,3456]{1,0:T(8,128)(2,1)S(1)} %copy-done.16), kind=kOutput, calls=%fused_computation.17 | convolution fusion | flops 3625975808 | bytes 20119552 | tf_op jit(solution)/shard_map/dot_general | solution.py:131
  208.4 1.3 collective-permute-start.7
  209.7 3.2 collective-permute-start.6
  212.8 3.9 copy.23
  216.7 3.8 copy.24
  220.7 4.3 collective-permute-start.8
  225.1 1.5 collective-permute-start.9
  226.6 9.0 %fusion.19 = f32[256,3456]{1,0:T(8,128)} fusion(bf16[256,2048]{0,1:T(8,128)(2,1)S(1)} %get-tuple-element.61, bf16[3456,2048]{0,1:T(8,128)(2,1)} %copy-done.2), kind=kOutput, calls=%fused_computation.173 | convolution fusion | flops 3623878656 | bytes 18743296 | tf_op jit(solution)/shard_map/dot_general | solution.py:147
  235.5 22.6 %collective-permute-done.8 = bf16[256,6,2,128]{0,3,2,1:T(8,128)(2,1)S(1)} collective-permute-done((bf16[256,6,2,128]{0,3,2,1:T(8,128)(2,1)S(1)}, bf16[256,6,2,128]{0,3,2,1:T(8,128)(2,1)S(1)}, u32[]{:S(2)}, u32[]{:S(2)}) %collective-permute-start.8) | collective-permute-done | bytes 786464 | tf_op jit(solution)/shard_map/ppermute | solution.py:24
  259.9 2.9 pad_maximum_fusion
  262.9 10.8 %pad_slice_fusion.1 = (bf16[256,2,8,128]{0,3,2,1:T(8,128)(2,1)S(1)}, bf16[256,2,8,128]{0,3,2,1:T(8,128)(2,1)}, bf16[256,2,8,128]{0,3,2,1:T(8,128)(2,1)}, bf16[25...) fusion(bf16[256,6,12,128]{0,3,2,1:T(8,128)(2,1)S(1)} %pad_maxim, ...), kind=kLoop, calls=%fused_computation.18 | loop fusion | bytes 23592960 | tf_op jit(solution)/shard_map/slice | solution.py:94
  273.7 2.5 constant_dynamic-update-slice_fusion.55
  276.2 2.6 pad_maximum_fusion.6
  278.7 1.1 constant_dynamic-update-slice_fusion.54
  279.9 1.1 constant_dynamic-update-slice_fusion.53
  281.0 1.1 constant_dynamic-update-slice_fusion.52
  282.1 1.2 constant_dynamic-update-slice_fusion.51
  283.3 1.1 constant_dynamic-update-slice_fusion.50
  284.4 1.1 constant_dynamic-update-slice_fusion.49
  285.4 1.3 pad_maximum_fusion.3
  286.8 1.1 constant_dynamic-update-slice_fusion.48
  287.9 1.1 constant_dynamic-update-slice_fusion.47
  289.0 1.1 constant_dynamic-update-slice_fusion.46
  290.1 1.1 constant_dynamic-update-slice_fusion.45
  291.2 1.1 constant_dynamic-update-slice_fusion.44
  292.4 1.2 constant_dynamic-update-slice_fusion.43
  293.6 1.1 constant_dynamic-update-slice_fusion.42
  294.7 1.2 constant_dynamic-update-slice_fusion.41
  295.9 1.1 constant_dynamic-update-slice_fusion.40
  297.0 1.1 constant_dynamic-update-slice_fusion.39
  298.1 1.2 constant_dynamic-update-slice_fusion.38
  299.3 1.2 constant_dynamic-update-slice_fusion.37
  300.5 1.2 constant_dynamic-update-slice_fusion.36
  301.7 1.1 constant_dynamic-update-slice_fusion.35
  302.8 1.2 constant_dynamic-update-slice_fusion.34
  304.0 1.1 constant_dynamic-update-slice_fusion.33
  305.1 1.2 constant_dynamic-update-slice_fusion.32
  306.3 1.1 constant_dynamic-update-slice_fusion.31
  307.4 1.1 constant_dynamic-update-slice_fusion.30
  308.5 1.1 constant_dynamic-update-slice_fusion.29
  309.6 21.0 %fusion = f32[128,1728]{1,0:T(8,128)} fusion(bf16[216,8,16,128]{3,2,1,0:T(8,128)(2,1)} %bitcast.112, bf16[6912,2048]{0,1:T(8,128)(2,1)} %constant_dynamic-update-slice_fusion.29, bf16[6912,128]{1,0:T(8,128)(2,1)} %bitcast.162, f32[128,2048]{0,1:T(8,128)S(1)} %copy-done.19), kind=kOutput, calls=%fused_computation | convolution fusion | flops 4532207616 | bytes 39092224 | tf_op jit(solution)/shard_map/dot_general | solution.py:167
  330.6 1.8 copy.25
  332.4 115.8 %all-reduce.8.cloned.1.call-done = (f32[128,1728]{1,0:T(8,128)}, f32[256,3456]{1,0:T(8,128)}) async-done(((f32[128,1728]{1,0:T(8,128)}, f32[256,3456]{1,0:T(8,128)}), (f32[128,1728]{1,0:T(8,128)}, f32[256,3456]{1,0:T(8,128)})) %all-reduce.8.cloned.1.call-update) | async-done | bytes 4423696 | tf_op jit(solution)/shard_map/psum | solution.py:170
  448.2 1.6 constant_dynamic-slice_fusion.1
  449.7 1.8 constant_dynamic-slice_fusion
  (110 shorter events, 9.2 us)
Async XLA Ops:
  7.2 153.8 %copy-start = (bf16[128,1728]{0,1:T(8,128)(2,1)S(1)}, bf16[128,1728]{0,1:T(8,128)(2,1)}, u32[]{:S(2)}) copy-start(bf16[128,1728]{0,1:T(8,128)(2,1)} %param.6) | copy-start | bytes 1327108
  7.2 441.0 %all-reduce.8.cloned.1.call-start = ((), (), s32[]{:S(2)}) async-start(), calls=%async_computation | async-start | bytes 8912896 | tf_op jit(solution)/shard_map/psum | solution.py:170
  8.5 3.9 collective-permute-start
  15.2 8.2 %collective-permute-start.1 = (bf16[64,5,1,256]{3,0,2,1:T(8,128)(2,1)S(1)}, bf16[64,5,1,256]{3,0,2,1:T(8,128)(2,1)S(1)}, u32[]{:S(2)}, u32[]{:S(2)}) collective-permute-start(bf16[64,5,1,256]{3,0,2,1:T(8,128)(2,1)S(1)} %slice.389), channel_id=1, source_target_pairs={{0,1},{1,2},{2,3},{3,4},{4,5},{5,6},{6,7},{8,9},{9,10},{10,11},{11... | collective-permute-start | bytes 491528 | tf_op jit(solution)/shard_map/ppermute | solution.py:14
  161.0 9.9 %copy-start.3 = (bf16[1728,2,8,128]{3,2,1,0:T(8,128)(2,1)}, bf16[1728,2,8,128]{3,2,1,0:T(8,128)(2,1)S(1)}, u32[]{:S(2)}) copy-start(bf16[1728,2,8,128]{3,2,1,0:T(8,128)(2,1)S(1)} %copy.21) | copy-start | bytes 21233668
  161.0 16.8 %copy-start.17 = (bf16[256,2,8,128]{3,2,1,0:T(8,128)(2,1)S(1)}, bf16[256,2,8,128]{3,2,1,0:T(8,128)(2,1)}, u32[]{:S(2)}) copy-start(bf16[256,2,8,128]{3,2,1,0:T(8,128)(2,1)} %param.5) | copy-start | bytes 3145732
  165.0 4.4 collective-permute-start.3
  166.3 4.6 collective-permute-start.2
  171.9 22.0 %collective-permute-start.4 = (bf16[128,6,2,128]{0,3,2,1:T(8,128)(2,1)}, bf16[128,6,2,128]{0,3,2,1:T(8,128)(2,1)S(1)}, u32[]{:S(2)}, u32[]{:S(2)}) collective-permute-start(bf16[128,6,2,128]{0,3,2,1:T(8,128)(2,1)} %get-tuple-element.69), channel_id=1, source_target_pairs={{0,1},{1,2},{2,3},{3,4},{4,5},{5,6},{6,7},{8,9},{9,10},{10,11},{11... | collective-permute-start | bytes 1179656 | tf_op jit(solution)/shard_map/ppermute | solution.py:24
  176.3 17.6 %collective-permute-start.5 = (bf16[128,6,2,128]{0,3,2,1:T(8,128)(2,1)}, bf16[128,6,2,128]{0,3,2,1:T(8,128)(2,1)S(1)}, u32[]{:S(2)}, u32[]{:S(2)}) collective-permute-start(bf16[128,6,2,128]{0,3,2,1:T(8,128)(2,1)} %get-tuple-element.70), channel_id=1, source_target_pairs={{1,0},{2,1},{3,2},{4,3},{5,4},{6,5},{7,6},{9,8},{10,9},{11,10},{12... | collective-permute-start | bytes 1179656 | tf_op jit(solution)/shard_map/ppermute | solution.py:25
  200.9 1.8 copy-start.15
  200.9 2.1 copy-start.16
  203.0 5.4 %copy-start.2 = (bf16[3456,2048]{0,1:T(8,128)(2,1)}, bf16[3456,2048]{0,1:T(8,128)(2,1)S(1)}, u32[]{:S(2)}) copy-start(bf16[3456,2048]{0,1:T(8,128)(2,1)S(1)} %constant_dynamic-update-slice_fusion.2) | copy-start | bytes 42467332
  208.4 12.2 %collective-permute-start.7 = (bf16[256,2,8,128]{0,3,2,1:T(8,128)(2,1)S(1)}, bf16[256,2,8,128]{0,3,2,1:T(8,128)(2,1)S(1)}, u32[]{:S(2)}, u32[]{:S(2)}) collective-permute-start(bf16[256,2,8,128]{0,3,2,1:T(8,128)(2,1)S(1)} %bitcast.95), channel_id=1, source_target_pairs={{8,0},{9,1},{10,2},{11,3},{12,4},{13,5},{14,6},{15,7},{24,16},{25,... | collective-permute-start | bytes 3145736 | tf_op jit(solution)/shard_map/ppermute | solution.py:25
  209.7 10.9 %collective-permute-start.6 = (bf16[256,2,8,128]{0,3,2,1:T(8,128)(2,1)S(1)}, bf16[256,2,8,128]{0,3,2,1:T(8,128)(2,1)S(1)}, u32[]{:S(2)}, u32[]{:S(2)}) collective-permute-start(bf16[256,2,8,128]{0,3,2,1:T(8,128)(2,1)S(1)} %bitcast.96), channel_id=1, source_target_pairs={{0,8},{1,9},{2,10},{3,11},{4,12},{5,13},{6,14},{7,15},{16,24},{17,... | collective-permute-start | bytes 3145736 | tf_op jit(solution)/shard_map/ppermute | solution.py:24
  220.7 37.4 %collective-permute-start.8 = (bf16[256,6,2,128]{0,3,2,1:T(8,128)(2,1)S(1)}, bf16[256,6,2,128]{0,3,2,1:T(8,128)(2,1)S(1)}, u32[]{:S(2)}, u32[]{:S(2)}) collective-permute-start(bf16[256,6,2,128]{0,3,2,1:T(8,128)(2,1)S(1)} %get-tuple-element.41), channel_id=1, source_target_pairs={{0,1},{1,2},{2,3},{3,4},{4,5},{5,6},{6,7},{8,9},{9,10},{10,11},{11... | collective-permute-start | bytes 2359304 | tf_op jit(solution)/shard_map/ppermute | solution.py:24
  225.1 33.1 %collective-permute-start.9 = (bf16[256,6,2,128]{0,3,2,1:T(8,128)(2,1)S(1)}, bf16[256,6,2,128]{0,3,2,1:T(8,128)(2,1)S(1)}, u32[]{:S(2)}, u32[]{:S(2)}) collective-permute-start(bf16[256,6,2,128]{0,3,2,1:T(8,128)(2,1)S(1)} %get-tuple-element.42), channel_id=1, source_target_pairs={{1,0},{2,1},{3,2},{4,3},{5,4},{6,5},{7,6},{9,8},{10,9},{11,10},{12... | collective-permute-start | bytes 2359304 | tf_op jit(solution)/shard_map/ppermute | solution.py:25
  258.1 0.9 copy-start.12
  259.0 0.9 copy-start.14
  273.7 6.2 %copy-start.11 = (bf16[256,2,8,128]{0,3,2,1:T(8,128)(2,1)S(1)}, bf16[256,2,8,128]{0,3,2,1:T(8,128)(2,1)}, u32[]{:S(2)}) copy-start(bf16[256,2,8,128]{0,3,2,1:T(8,128)(2,1)} %get-tuple-element.33) | copy-start | bytes 3145732
  273.7 7.3 %copy-start.10 = (bf16[256,2,8,128]{0,3,2,1:T(8,128)(2,1)S(1)}, bf16[256,2,8,128]{0,3,2,1:T(8,128)(2,1)}, u32[]{:S(2)}) copy-start(bf16[256,2,8,128]{0,3,2,1:T(8,128)(2,1)} %get-tuple-element.18) | copy-start | bytes 3145732
  276.1 7.1 %copy-start.9 = (bf16[256,2,8,128]{0,3,2,1:T(8,128)(2,1)S(1)}, bf16[256,2,8,128]{0,3,2,1:T(8,128)(2,1)}, u32[]{:S(2)}) copy-start(bf16[256,2,8,128]{0,3,2,1:T(8,128)(2,1)} %get-tuple-element.26) | copy-start | bytes 3145732
  276.2 8.2 %copy-start.8 = (bf16[256,2,8,128]{0,3,2,1:T(8,128)(2,1)S(1)}, bf16[256,2,8,128]{0,3,2,1:T(8,128)(2,1)}, u32[]{:S(2)}) copy-start(bf16[256,2,8,128]{0,3,2,1:T(8,128)(2,1)} %get-tuple-element.19) | copy-start | bytes 3145732
  278.7 6.7 %copy-start.13 = (bf16[256,6,2,128]{0,3,2,1:T(8,128)(2,1)S(1)}, bf16[256,6,2,128]{0,3,2,1:T(8,128)(2,1)}, u32[]{:S(2)}) copy-start(bf16[256,6,2,128]{0,3,2,1:T(8,128)(2,1)} %copy-done.12) | copy-start | bytes 2359300
  283.3 4.6 %copy-start.7 = (bf16[256,2,8,128]{0,3,2,1:T(8,128)(2,1)S(1)}, bf16[256,2,8,128]{0,3,2,1:T(8,128)(2,1)}, u32[]{:S(2)}) copy-start(bf16[256,2,8,128]{0,3,2,1:T(8,128)(2,1)} %get-tuple-element.27) | copy-start | bytes 3145732
  284.4 4.7 %copy-start.6 = (bf16[256,2,8,128]{0,3,2,1:T(8,128)(2,1)S(1)}, bf16[256,2,8,128]{0,3,2,1:T(8,128)(2,1)}, u32[]{:S(2)}) copy-start(bf16[256,2,8,128]{0,3,2,1:T(8,128)(2,1)} %get-tuple-element.20) | copy-start | bytes 3145732
  285.4 5.8 %copy-start.5 = (bf16[256,2,8,128]{0,3,2,1:T(8,128)(2,1)S(1)}, bf16[256,2,8,128]{0,3,2,1:T(8,128)(2,1)}, u32[]{:S(2)}) copy-start(bf16[256,2,8,128]{0,3,2,1:T(8,128)(2,1)} %get-tuple-element.28) | copy-start | bytes 3145732
  285.4 7.0 %copy-start.4 = (bf16[256,2,8,128]{0,3,2,1:T(8,128)(2,1)S(1)}, bf16[256,2,8,128]{0,3,2,1:T(8,128)(2,1)}, u32[]{:S(2)}) copy-start(bf16[256,2,8,128]{0,3,2,1:T(8,128)(2,1)} %get-tuple-element.21) | copy-start | bytes 3145732
  301.7 7.9 %copy-start.19 = (f32[128,2048]{0,1:T(8,128)S(1)}, f32[128,2048]{0,1:T(8,128)}, u32[]{:S(2)}) copy-start(f32[128,2048]{0,1:T(8,128)} %get-tuple-element.72) | copy-start | bytes 3145732
  309.6 21.0 %copy-start.18 = (bf16[256,2048]{0,1:T(8,128)(2,1)S(1)}, bf16[256,2048]{0,1:T(8,128)(2,1)}, u32[]{:S(2)}) copy-start(bf16[256,2048]{0,1:T(8,128)(2,1)} %get-tuple-element.62) | copy-start | bytes 3145732
  309.6 141.9 %copy-start.1 = (bf16[128,1728]{0,1:T(8,128)(2,1)S(1)}, bf16[128,1728]{0,1:T(8,128)(2,1)}, u32[]{:S(2)}) copy-start(bf16[128,1728]{0,1:T(8,128)(2,1)} %param.6) | copy-start | bytes 1327108
Sparse Core Ops, SparseCore 0:
  330.8 117.3 all-reduce.7
where the time goes:
time: 468 us; the launch traced here: 459 us
  local copies, waits for them, and re-layouts  207 us (44%)
  waiting for transfers between devices  160 us (34%)
  matrix products  39.4 us (8%)
  starting transfers between devices  27.2 us (6%)
  between operations  15.2 us (3%)
  other arithmetic  10.5 us (2%)
    psum x1, waiting for transfers between devices, local(): lax.psum((strided_grad, dilated_grad), ('slab', 'strip'))  116 us
    slice x1, local copies, waits for them, and re-layouts, strided_columns(): even_time = extended[:, :, :, 0::2]  57.6 us
    slice x1, local copies, waits for them, and re-layouts, strided_columns(): odd_time = extended[:, :, :, 1::2]  57.6 us
    unnamed x122, local copies, waits for them, and re-layouts  43.1 us
    ppermute x4, waiting for transfers between devices, with_halo(): before = lax.ppermute(last, axis, up)  38.3 us
    dot_general x1, matrix products, local(): lax.dot_general(preact_grad, input_cols, dims, preferred_element_type=jnp...  21 us
    concatenate x2, local copies, waits for them, and re-layouts, strided_columns(): jnp.concatenate(pieces, axis=0)  18.9 us
    slice x2, local copies, waits for them, and re-layouts, dilated_columns(): lax.slice(source, (0, inline_stride * tap_spacing, crossline_stride * tap...  15.1 us
  transfers between devices with their start and end apart: 11, of which 6 were waited for; matrix products, arithmetic and copies ran while one was open for 4% of the time, Pallas kernels for 0%

commit v1 on v0

v1 whole, which is shorter than its diff:
```python
import math

import jax
import jax.numpy as jnp
from jax import lax
from jax.experimental import pallas as pl
from jax.experimental.pallas import tpu as pltpu
from jax.sharding import PartitionSpec as P


BF16 = jnp.bfloat16
F32 = jnp.float32
VMEM = pltpu.VMEM
VMEM_LIMIT = 24 * 1024 * 1024


def vmem_call(body, out_shape, n_in, scratch=()):
    spec = pl.BlockSpec(memory_space=pltpu.VMEM)
    return pl.pallas_call(
        body,
        out_shape=out_shape,
        in_specs=[spec] * n_in,
        out_specs=jax.tree.map(lambda _: spec, out_shape),
        scratch_shapes=list(scratch),
        compiler_params=pltpu.CompilerParams(vmem_limit_bytes=VMEM_LIMIT),
    )


def selection(depth):
    half = depth // 2
    source = lax.broadcasted_iota(jnp.int32, (depth, 3 * half), 0)
    lane = lax.broadcasted_iota(jnp.int32, (depth, 3 * half), 1)
    even = (lane < half) & (source == 2 * lane)
    odd = (lane >= half) & (lane < 2 * half) & (source == 2 * (lane - half) + 1)
    late = (lane >= 2 * half) & (source == 2 * (lane - 2 * half) - 1)
    return jnp.where(even | odd | late, 1.0, 0.0).astype(BF16)


def thirds(values):
    half = values.shape[1] // 3
    return [values[:, k * half : (k + 1) * half] for k in range(3)]


def spread(plane, pick, scratch):
    for k, part in enumerate(thirds(jnp.dot(plane, pick, preferred_element_type=F32))):
        scratch[k] = part


def put_column(vp_ref, values, channels, row, col, pairs):
    half = values[0].shape[1]
    taps = (values[2], values[0], values[1])
    for b in range(3):
        for h in range(2):
            rest = col + 1 - b - 2 * h
            if rest % 4 or not 0 <= rest // 4 < pairs:
                continue
            for c in range(3):
                start = ((row * 3 + b) * 3 + c) * channels
                vp_ref[rest // 4, start : start + channels, h * half : (h + 1) * half] = taps[c]


def split_body(vol_ref, tgt_ref, vp_ref, tp_ref, wide_ref, tall_ref):
    channels, rows, cols, depth = vol_ref.shape
    pairs = cols // 4
    half = depth // 2
    pick = selection(depth)
    for row in range(rows):
        slot = row % 2
        plane = vol_ref[:, row].reshape(channels * cols, depth)
        spread(plane, pick, wide_ref.at[slot])
        for col in range(cols):
            values = [
                wide_ref[slot, k, pl.ds(col, channels, stride=cols), :].astype(BF16)
                for k in range(3)
            ]
            put_column(vp_ref, values, channels, row + 1, col, pairs)
    outs, orows, ocols, _ = tgt_ref.shape
    for row in range(orows):
        slot = row % 2
        tall_ref[slot] = tgt_ref[:, row].astype(F32).reshape(outs * ocols, half)
        for col in range(ocols):
            values = tall_ref[slot, pl.ds(col, outs, stride=ocols), :].astype(BF16)
            tp_ref[row, col // 2, :, (col % 2) * half : (col % 2 + 1) * half] = values


def preact_body(own_ref, hrow_ref, hcol_ref, w_ref, vp_ref, h_ref, hl_ref, hr_ref, slope_ref, wide_ref):
    channels, cols, depth = hrow_ref.shape
    rows_ext = hcol_ref.shape[0]
    orows, pairs, _, _ = h_ref.shape
    vp_ref[:, 9 * channels :] = own_ref[:, 9 * channels :]
    pick = selection(depth)
    spread(hrow_ref[...].reshape(channels * cols, depth), pick, wide_ref)
    for col in range(cols):
        values = [
            wide_ref[k, pl.ds(col, channels, stride=cols), :].astype(BF16) for k in range(3)
        ]
        put_column(vp_ref, values, channels, 0, col, pairs)
    for row in range(rows_ext):
        values = jnp.dot(hcol_ref[row], pick, preferred_element_type=F32).astype(BF16)
        put_column(vp_ref, thirds(values), channels, row, -1, pairs)
    plane = 9 * channels
    for i in range(orows):
        for m in (0, pairs - 1, *range(1, pairs - 1)):
            window = vp_ref[m, 2 * i * plane : (2 * i + 3) * plane, :]
            pre = jnp.dot(w_ref[...], window, preferred_element_type=F32)
            sigma = jax.nn.sigmoid(pre)
            hidden = (pre * sigma).astype(BF16)
            h_ref[i, m] = hidden
            if m == 0:
                hl_ref[i] = hidden
            if m == pairs - 1:
                hr_ref[i] = hidden
            slope_ref[i, m] = sigma * (1.0 + pre * (1.0 - sigma))


def shifted(values, steps):
    half = values.shape[1] // 2
    lane = lax.broadcasted_iota(jnp.int32, (values.shape[0], half), 1)
    keep = lane >= steps if steps > 0 else lane < half + steps
    parts = [
        jnp.where(keep, pltpu.roll(values[:, k * half : (k + 1) * half], steps % half, 1), 0.0)
        for k in range(2)
    ]
    return jnp.concatenate(parts, axis=1)


def forward_body(
    scale, step, h_ref, hl_ref, hr_ref, o_ref, ol_ref, or_ref, w2_ref, wg_ref, tp_ref,
    hs_ref, pred_ref, res_ref, gown_ref, ghalo_ref, gother_ref, rs_ref,
):
    orows, pairs, mid, lanes = h_ref.shape
    outs = w2_ref.shape[0]
    for r in range(orows):
        for src, (whole, left, right) in enumerate(
            ((h_ref, hl_ref, hr_ref), (o_ref, ol_ref, or_ref))
        ):
            for x in range(pairs + 2):
                tile = left[r] if x == 0 else right[r] if x == pairs + 1 else whole[r, x - 1]
                wide = tile.astype(F32)
                base = src * 3 * mid
                hs_ref[r, x, base : base + mid, :] = shifted(wide, step).astype(BF16)
                hs_ref[r, x, base + mid : base + 2 * mid, :] = tile
                hs_ref[r, x, base + 2 * mid : base + 3 * mid, :] = shifted(wide, -step).astype(BF16)
    for r in range(orows):
        for m in range(pairs):
            window = hs_ref[r, m : m + 3].reshape(3 * 6 * mid, lanes)
            out = jnp.dot(w2_ref[...], window, preferred_element_type=F32)
            pred_ref[r, m] = out.astype(BF16)
            res = ((out - tp_ref[r, m].astype(F32)) * scale).astype(BF16)
            res_ref[r, m] = res
            wide = res.astype(F32)
            rs_ref[r, m, 0:outs, :] = shifted(wide, -step).astype(BF16)
            rs_ref[r, m, outs : 2 * outs, :] = res
            rs_ref[r, m, 2 * outs : 3 * outs, :] = shifted(wide, step).astype(BF16)
    block = 3 * outs
    for r in range(orows):
        for x in range(pairs + 2):
            low, high = max(x - 2, 0), min(x, pairs - 1)
            first = low - (x - 2)
            window = rs_ref[r, low : high + 1].reshape((high - low + 1) * block, lanes)
            weights = wg_ref[:, first * block : (first + high - low + 1) * block]
            grad = jnp.dot(weights, window, preferred_element_type=F32)
            gother_ref[r, x] = grad[mid:].astype(BF16)
            if x == 0:
                ghalo_ref[0, r] = grad[:mid]
            elif x == pairs + 1:
                ghalo_ref[1, r] = grad[:mid]
            else:
                gown_ref[r, x - 1] = grad[:mid]


NT = (((1,), (1,)), ((), ()))


def dilated_grad_body(res_ref, hs_ref, own_ref, other_ref):
    orows, pairs, outs, lanes = res_ref.shape
    mid = hs_ref.shape[2] // 6
    for b in range(3):
        for src, ref in enumerate((own_ref, other_ref)):
            base = src * 3 * mid
            total = None
            for r in range(orows):
                for m in range(pairs):
                    window = hs_ref[r, m + b, base : base + 3 * mid, :]
                    part = lax.dot_general(res_ref[r, m], window, NT, preferred_element_type=F32)
                    total = part if total is None else total + part
            ref[:, b * 3 * mid : (b + 1) * 3 * mid] = total


def strided_grad_body(gown_ref, gx_ref, gl_ref, gr_ref, slope_ref, vp_ref, out_ref):
    orows, pairs, mid, lanes = gown_ref.shape
    plane = vp_ref.shape[1] // (2 * orows + 1)
    total = None
    for i in range(orows):
        for m in range(pairs):
            grad = gown_ref[i, m] + gx_ref[i, m + 1].astype(F32)
            if m == 0:
                grad = grad + gl_ref[i].astype(F32)
            if m == pairs - 1:
                grad = grad + gr_ref[i].astype(F32)
            pg = (grad * slope_ref[i, m]).astype(BF16)
            window = vp_ref[m, 2 * i * plane : (2 * i + 3) * plane, :]
            part = lax.dot_general(pg, window, NT, preferred_element_type=F32)
            total = part if total is None else total + part
    out_ref[...] = total


def prediction_body(pred_ref, out_ref, tall_ref):
    orows, pairs, outs, lanes = pred_ref.shape
    half = lanes // 2
    cols = 2 * pairs
    for r in range(orows):
        slot = r % 2
        for col in range(cols):
            values = pred_ref[r, col // 2, :, (col % 2) * half : (col % 2 + 1) * half]
            tall_ref[slot, pl.ds(col, outs, stride=cols), :] = values.astype(F32)
        out_ref[:, r] = tall_ref[slot].reshape(outs, cols, half).astype(BF16)


def sds(shape, dtype):
    return jax.ShapeDtypeStruct(shape, dtype)


def shift_along(value, axis, steps):
    count = lax.axis_size(axis)
    pairs = [(i, i + steps) for i in range(count) if 0 <= i + steps < count]
    return lax.ppermute(value, axis, pairs)


def swap(value):
    return lax.ppermute(value, "slab", [(0, 1), (1, 0)])


def local(volume, target, strided_weight, dilated_weight):
    channels, rows_in, cols_in, depth = volume.shape
    mid = strided_weight.shape[0]
    outs = dilated_weight.shape[0]
    orows, ocols, half = rows_in // 2, cols_in // 2, depth // 2
    pairs, lanes = ocols // 2, 2 * half
    strips = lax.axis_size("strip")
    slab = lax.axis_index("slab")
    step = 2
    assert lax.axis_size("slab") == 2 and orows == step and ocols % 2 == 0
    cells = orows * ocols * half * lax.axis_size("slab") * strips
    scale = 1.0 / math.sqrt(cells)

    lower = shift_along(volume[:, -1], "slab", 1)
    last = jnp.concatenate([lower[None, :, -1, :], volume[:, :, -1, :].transpose(1, 0, 2)], axis=0)
    left = shift_along(last, "strip", 1)

    planes = dilated_weight.reshape(outs, 3, 9 * mid)
    w_own = planes[:, 1].reshape(outs, 3, 3 * mid)
    w_other = lax.dynamic_index_in_dim(planes, 2 - 2 * slab, 1, False).reshape(outs, 3, 3 * mid)
    both = jnp.stack([w_own, w_other], axis=2)
    w2 = both.reshape(outs, 18 * mid)
    wg = (
        both.reshape(outs, 3, 2, 3, mid)[:, ::-1]
        .transpose(2, 4, 1, 3, 0)
        .reshape(2 * mid, 9 * outs)
    )

    vp, tp = vmem_call(
        split_body,
        (
            sds((pairs, (rows_in + 1) * 9 * channels, lanes), BF16),
            sds((orows, pairs, outs, lanes), BF16),
        ),
        2,
        [VMEM((2, 3, channels * cols_in, half), F32), VMEM((2, outs * ocols, half), F32)],
    )(volume, target)
    vp, hidden, hid_l, hid_r, slope = vmem_call(
        preact_body,
        (
            sds(vp.shape, BF16),
            sds((orows, pairs, mid, lanes), BF16),
            sds((orows, mid, lanes), BF16),
            sds((orows, mid, lanes), BF16),
            sds((orows, pairs, mid, lanes), F32),
        ),
        4,
        [VMEM((3, channels * cols_in, half), F32)],
    )(vp, lower, left, strided_weight)

    from_left = shift_along(hid_r, "strip", 1)
    from_right = shift_along(hid_l, "strip", -1)
    other = swap(hidden)
    other_left = swap(from_left)
    other_right = swap(from_right)

    def forward(*refs):
        forward_body(scale, step, *refs)

    hs, pred, residual, gown, ghalo, gother = vmem_call(
        forward,
        (
            sds((orows, pairs + 2, 6 * mid, lanes), BF16),
            sds((orows, pairs, outs, lanes), BF16),
            sds((orows, pairs, outs, lanes), BF16),
            sds((orows, pairs, mid, lanes), F32),
            sds((2, orows, mid, lanes), F32),
            sds((orows, pairs + 2, mid, lanes), BF16),
        ),
        9,
        [VMEM((orows, pairs, 3 * outs, lanes), BF16)],
    )(hidden, from_left, from_right, other, other_left, other_right, w2, wg, tp)

    gx = swap(gother)
    to_left = (ghalo[0] + gx[:, 0].astype(F32)).astype(BF16)
    to_right = (ghalo[1] + gx[:, -1].astype(F32)).astype(BF16)
    grad_l = shift_along(to_right, "strip", 1)
    grad_r = shift_along(to_left, "strip", -1)

    dg_own, dg_other = vmem_call(
        dilated_grad_body, (sds((outs, 9 * mid), F32), sds((outs, 9 * mid), F32)), 2
    )(residual, hs)
    prediction = vmem_call(
        prediction_body,
        sds((outs, orows, ocols, half), BF16),
        1,
        [VMEM((2, outs * ocols, half), F32)],
    )(pred)
    sg = vmem_call(strided_grad_body, sds((mid, 27 * channels), F32), 6)(
        gown, gx, grad_l, grad_r, slope, vp
    )

    def halves(grad):
        rows = grad.shape[0] // strips
        return grad.reshape(strips, 2, rows // 2, grad.shape[1])

    def combined(grad):
        parts = halves(grad)
        mine = lax.dynamic_index_in_dim(parts, slab, 1, False)
        theirs = lax.dynamic_index_in_dim(parts, 1 - slab, 1, False)
        return mine + swap(theirs.astype(BF16)).astype(F32)

    rows = outs // strips
    dg = jnp.concatenate(
        [combined(dg_own).astype(BF16), dg_other.astype(BF16).reshape(strips, rows, 9 * mid)], axis=1
    )
    dg = lax.all_to_all(dg, "strip", 0, 0, tiled=True)
    dg = jnp.sum(dg.astype(F32), axis=0)
    sgc = lax.all_to_all(combined(sg).astype(BF16), "strip", 0, 0, tiled=True)
    sgc = jnp.sum(sgc.astype(F32), axis=0)
    dg_x, sg_x = swap(dg), swap(sgc)
    first = slab == 0
    half_rows = rows // 2
    dg0, dg1 = jnp.where(first, dg, dg_x), jnp.where(first, dg_x, dg)
    middle = jnp.concatenate([dg0[:half_rows], dg1[:half_rows]], axis=0)
    dilated_grad = jnp.concatenate([dg1[half_rows:], middle, dg0[half_rows:]], axis=1)
    strided_grad = jnp.concatenate(
        [jnp.where(first, sgc, sg_x), jnp.where(first, sg_x, sgc)], axis=0
    )
    return prediction, strided_grad, dilated_grad


def solution(mesh):
    return jax.shard_map(
        local,
        mesh=mesh,
        in_specs=(P("fold", "slab", "strip", None), P("fold", "slab", "strip", None), P(), P()),
        out_specs=(
            P("fold", "slab", "strip", None),
            P(("fold", "strip"), None),
            P(("fold", "strip"), None),
        ),
        check_vma=False,
    )
```

time: 468 us -> 133 us (0.28); the launches traced: 459 us -> 133 us
  local copies, waits for them, and re-layouts: 207 us -> 42.2 us
  waiting for transfers between devices: 160 us -> 32.5 us
  matrix products: 39.4 us -> 0 us
  Pallas kernels: 0 us -> 20.8 us
  between operations: 15.2 us -> 1.12 us
  other arithmetic: 10.5 us -> 5.79 us
    slice x7 -> x8, local copies, waits for them, and re-layouts: 132 us -> 2.66 us  [the longest x1 1.5 us: local(): volume[:, :, -1, :].transpose(1, 0, 2)]
    psum x1 -> x0, waiting for transfers between devices: 116 us -> none  [local(): lax.psum((strided_grad, dilated_grad), ('slab', 'strip'))]
    dot_general x4 -> x0, matrix products: 39.4 us -> none  [the longest x1 21 us: local(): lax.dot_general(preact_grad, input_cols, dims, preferred_element_type=jnp...]
    ppermute x10 -> x14, waiting for transfers between devices: 43.8 us -> 4.6 us  [the longest x8 3.54 us: swap(): return lax.ppermute(value, 'slab', [(0, 1), (1, 0)])]
    all_to_all x0 -> x2, waiting for transfers between devices: none -> 27.9 us  [the longest x1 20.2 us: local(): dg = lax.all_to_all(dg, 'strip', 0, 0, tiled=True)]
    concatenate x5 -> x0, local copies, waits for them, and re-layouts: 23 us -> none  [the longest x2 18.9 us: strided_columns(): jnp.concatenate(pieces, axis=0)]
    pallas_call x0 -> x6, Pallas kernels: none -> 20.8 us  [the longest x1 6.6 us: local(): vmem_call(forward, (sds((orows, pairs + 2, 6 * mid, lanes), BF16), sds((o...]
    unnamed x122 -> x54, local copies, waits for them, and re-layouts: 43.1 us -> 27.7 us
  transfers between devices with their start and end apart: 11 -> 16, of which waited for: 6 -> 7; matrix products, arithmetic and copies ran while one was open for 4% -> 17% of each run, Pallas kernels for 0% -> 7%
where the time goes in v1:
time: 133 us
  local copies, waits for them, and re-layouts  42.2 us (32%)
  waiting for transfers between devices  32.5 us (24%)
  starting transfers between devices  30.2 us (23%)
  Pallas kernels  20.8 us (16%)
  other arithmetic  5.79 us (4%)
    unnamed x54, local copies, waits for them, and re-layouts  27.7 us
    all_to_all x1, waiting for transfers between devices, local(): dg = lax.all_to_all(dg, 'strip', 0, 0, tiled=True)  20.2 us
    ppermute x6, starting transfers between devices, shift_along(): return lax.ppermute(value, axis, pairs)  17.4 us
    all_to_all x1, waiting for transfers between devices, local(): sgc = lax.all_to_all(combined(sg).astype(BF16), 'strip', 0, 0, tiled=True)  7.68 us
    all_to_all x1, starting transfers between devices, local(): sgc = lax.all_to_all(combined(sg).astype(BF16), 'strip', 0, 0, tiled=True)  7.63 us
    pallas_call x1, Pallas kernels, local(): vmem_call(forward, (sds((orows, pairs + 2, 6 * mid, lanes), BF16), sds((o...  6.6 us
    reshape x2, local copies, waits for them, and re-layouts, local(): wg = both.reshape(outs, 3, 2, 3, mid)[:, ::-1].transpose(2, 4, 1, 3, 0).r...  5.21 us
    pallas_call x1, Pallas kernels, local(): vmem_call(split_body, (sds((pairs, (rows_in + 1) * 9 * channels, lanes),...  4.08 us
  transfers between devices with their start and end apart: 16, of which 7 were waited for; matrix products, arithmetic and copies ran while one was open for 17% of the time, Pallas kernels for 7%

profile of v1, /device:TPU:0, one launch (start us, length us, event | category | flops | bytes accessed | tf_op | source)
XLA Modules:
  0.0 132.6 jit_solution(8029075738561009392)
XLA Ops:
  0.6 1.0 slice-done
  1.7 0.2 copy.43
  1.8 2.4 %collective-permute-start = (bf16[64,16,256]{2,0,1:T(8,128)(2,1)S(1)}, bf16[64,16,256]{2,0,1:T(8,128)(2,1)S(1)}, u32[]{:S(2)}, u32[]{:S(2)}) collective-permute-start(bf16[64,16,256]{2,0,1:T(8,128)(2,1)S(1)} %bitcast.61), channel_id=1, source_target_pairs={{0,8},{1,9},{2,10},{3,11},{4,12},{5,13},{6,14},{7,15},{16,24},{17,... | collective-permute-start | bytes 1572872 | tf_op jit(solution)/shard_map/ppermute | solution.py:227
  4.2 1.5 %slice.38 = bf16[64,4,1,256]{3,2,1,0:T(2,128)(2,1)S(1)} slice(bf16[64,4,16,256]{3,2,1,0:T(8,128)(2,1)} %vol_ref.1), slice={[0:64], [0:4], [15:16], [0:256]} | slice | bytes 262144 | tf_op jit(solution)/shard_map/slice | solution.py:248
  5.8 0.8 copy-done.23
  6.7 4.3 %collective-permute-start.1 = (bf16[5,64,256]{2,1,0:T(8,128)(2,1)S(1)}, bf16[5,64,256]{2,1,0:T(8,128)(2,1)S(1)}, u32[]{:S(2)}, u32[]{:S(2)}) collective-permute-start(bf16[5,64,256]{2,1,0:T(8,128)(2,1)S(1)} %pad_maximum_fusion.4), channel_id=1, source_target_pairs={{0,1},{1,2},{2,3},{3,4},{4,5},{5,6},{6,7},{8,9},{9,10},{10,11},{11... | collective-permute-start | bytes 491528 | tf_op jit(solution)/shard_map/ppermute | solution.py:227
  11.0 4.1 %copy.29 = bf16[256,3456]{0,1:T(8,128)(2,1)} copy(bf16[256,3456]{1,0:T(8,128)(2,1)} %param.7) | data formatting | bytes 3538944 | tf_op args[3]
  15.0 4.1 %shard_map.67 = (bf16[4,2880,256]{2,1,0:T(8,128)(2,1)S(1)}, bf16[2,4,256,256]{3,2,1,0:T(8,128)(2,1)S(1)}) custom-call(bf16[64,4,16,256]{3,2,1,0:T(8,128)(2,1)S(1)} %copy-done.6, bf16[256,2,8,128]{3,2,1,0:T(8,128)(2,1)S(1)} %copy-done.7), custom_call_target="tpu_custom_call" | custom-call | tf_op jit(solution)/shard_map/pallas_call | solution.py:262
  19.1 2.5 %copy-done.2 = bf16[4,2880,256]{2,1,0:T(8,128)(2,1)} copy-done((bf16[4,2880,256]{2,1,0:T(8,128)(2,1)}, bf16[4,2880,256]{2,1,0:T(8,128)(2,1)S(1)}, u32[]{:S(2)}) %copy-start.2) | copy-done | bytes 5898264
  21.6 1.0 copy-done.8
  22.6 1.3 copy.28.w_ref
  23.9 0.3 copy.27.hrow_ref
  24.2 0.7 copy-done.16
  24.9 2.7 %copy-done.3 = bf16[4,2880,256]{2,1,0:T(8,128)(2,1)S(1)} copy-done((bf16[4,2880,256]{2,1,0:T(8,128)(2,1)S(1)}, bf16[4,2880,256]{2,1,0:T(8,128)(2,1)}, u32[]{:S(2)}) %copy-start.3) | copy-done | bytes 5898264
  27.5 0.9 copy-done.17
  28.5 2.9 %shard_map.68 = (bf16[4,2880,256]{2,1,0:T(8,128)(2,1)S(1)}, bf16[2,4,128,256]{3,2,1,0:T(8,128)(2,1)}, bf16[2,128,256]{2,1,0:T(8,128)(2,1)S(1)}, bf16[2,128,256]{2,1,0:T(8,128)(2,1)S(1)}, f32[2,4,128,256]{3,2,1,0:T(8,128)S(1)}) custom-call(bf16[4,2880,256]{2,1,0:T(8,128)(2,1)S(1)} %copy-done.3, bf16[64,16,256]{2,1,0:T(8,128)(2,1)S(1)} %copy.27.hrow_ref, ...), custom_call_target="tpu_custom_call" | custom-call | tf_op jit(solution)/shard_map/pallas_call | solution.py:271
  31.4 2.5 %copy-done = bf16[4,2880,256]{2,1,0:T(8,128)(2,1)} copy-done((bf16[4,2880,256]{2,1,0:T(8,128)(2,1)}, bf16[4,2880,256]{2,1,0:T(8,128)(2,1)S(1)}, u32[]{:S(2)}) %copy-start) | copy-done | bytes 5898264
  33.9 0.1 fusion.6
  34.0 0.1 pad_maximum_fusion.1
  34.1 0.8 copy-done.18
  34.9 0.2 copy-done.19
  35.1 3.4 %collective-permute-start.2 = (bf16[2,128,256]{2,1,0:T(8,128)(2,1)S(1)}, bf16[2,128,256]{2,1,0:T(8,128)(2,1)S(1)}, u32[]{:S(2)}, u32[]{:S(2)}) collective-permute-start(bf16[2,128,256]{2,1,0:T(8,128)(2,1)S(1)} %get-tuple-element.20), channel_id=1, source_target_pairs={{0,1},{1,2},{2,3},{3,4},{4,5},{5,6},{6,7},{8,9},{9,10},{10,11},{11... | collective-permute-start | bytes 393224 | tf_op jit(solution)/shard_map/ppermute | solution.py:227
  38.5 1.5 %collective-permute-start.3 = (bf16[2,128,256]{2,1,0:T(8,128)(2,1)S(1)}, bf16[2,128,256]{2,1,0:T(8,128)(2,1)}, u32[]{:S(2)}, u32[]{:S(2)}) collective-permute-start(bf16[2,128,256]{2,1,0:T(8,128)(2,1)S(1)} %get-tuple-element.21), channel_id=1, source_target_pairs={{1,0},{2,1},{3,2},{4,3},{5,4},{6,5},{7,6},{9,8},{10,9},{11,10},{12... | collective-permute-start | bytes 393224 | tf_op jit(solution)/shard_map/ppermute | solution.py:227
  40.0 0.1 reverse_bitcast_fusion
  40.1 2.2 %copy.36 = bf16[2,128,3,3,256]{4,3,2,1,0:T(4,128)(2,1)} copy(bf16[2,128,3,3,256]{4,1,3,2,0:T(8,128)(2,1)S(1)} %reverse_bitcast_fusion) | data formatting | bytes 2359296 | tf_op jit(solution)/shard_map/reshape | solution.py:259
  42.2 3.1 %reshape.44.refs_7_ = bf16[256,2304]{1,0:T(8,128)(2,1)S(1)} reshape(bf16[2,128,3,3,256]{4,3,2,1,0:T(4,128)(2,1)} %copy.36) | data formatting | bytes 2359296 | tf_op jit(solution)/shard_map/reshape | solution.py:259
  45.3 0.3 collective-permute-start.5
  45.6 0.5 collective-permute-done.3.refs_2_
  46.1 1.4 %pad_maximum_fusion = bf16[256,3,2,384]{0,3,1,2:T(8,128)(2,1)S(1)} fusion(bf16[256,3,1,384]{0,3,1,2:T(8,128)(2,1)} %bitcast.57, bf16[256,3,1,384]{0,3,1,2:T(8,128)(2,1)} %bitcast.55), kind=kLoop, calls=%fused_computation.1 | loop fusion | flops 589824 | bytes 2359296 | tf_op jit(solution)/shard_map/stack | solution.py:254
  47.5 2.9 %copy.30 = bf16[256,3,2,384]{3,2,1,0:T(2,128)(2,1)} copy(bf16[256,3,2,384]{0,3,1,2:T(8,128)(2,1)S(1)} %pad_maximum_fusion) | data formatting | bytes 2359296 | tf_op jit(solution)/shard_map/stack | solution.py:254
  50.4 3.1 %reshape.37.refs_6_ = bf16[256,2304]{1,0:T(8,128)(2,1)S(1)} reshape(bf16[256,3,2,384]{3,2,1,0:T(2,128)(2,1)} %copy.30) | data formatting | bytes 2359296 | tf_op jit(solution)/shard_map/reshape | solution.py:255
  53.6 1.2 copy-done.9
  54.8 6.6 %shard_map.69 = (bf16[2,6,768,256]{3,2,1,0:T(8,128)(2,1)S(1)}, bf16[2,4,256,256]{3,2,1,0:T(8,128)(2,1)S(1)}, bf16[2,4,256,256]{3,2,1,0:T(8,128)(2,1)S(1)}, f32[2...) custom-call(bf16[2,4,128,256]{3,2,1,0:T(8,128)(2,1)} %get-tuple-element.19.refs_0_, ...), custom_call_target="tpu_custom_call" | custom-call | tf_op jit(solution)/shard_map/pallas_call | solution.py:293
  61.5 2.2 %copy-done.4 = bf16[2,6,768,256]{3,2,1,0:T(8,128)(2,1)} copy-done((bf16[2,6,768,256]{3,2,1,0:T(8,128)(2,1)}, bf16[2,6,768,256]{3,2,1,0:T(8,128)(2,1)S(1)}, u32[]{:S(2)}) %copy-start.4) | copy-done | bytes 4718616
  63.7 1.0 copy-done.14
  64.8 0.6 collective-permute-start.7
  65.4 1.9 %collective-permute-done.7 = bf16[2,6,128,256]{3,2,0,1:T(8,128)(2,1)S(1)} collective-permute-done((bf16[2,6,128,256]{3,2,0,1:T(8,128)(2,1)S(1)}, bf16[2,6,128,256]{3,2,0,1:T(8,128)(2,1)S(1)}, u32[]{:S(2)}, u32[]{:S(2)}) %collective-permute-start.7) | collective-permute-done | bytes 786464 | tf_op jit(solution)/shard_map/ppermute | solution.py:231
  67.3 0.8 fusion.3
  68.1 4.3 %collective-permute-start.8 = (bf16[2,128,256]{2,1,0:T(8,128)(2,1)}, bf16[2,128,256]{2,1,0:T(8,128)(2,1)S(1)}, u32[]{:S(2)}, u32[]{:S(2)}) collective-permute-start(bf16[2,128,256]{2,1,0:T(8,128)(2,1)} %get-tuple-element.36), channel_id=1, source_target_pairs={{0,1},{1,2},{2,3},{3,4},{4,5},{5,6},{6,7},{8,9},{9,10},{10,11},{11... | collective-permute-start | bytes 393224 | tf_op jit(solution)/shard_map/ppermute | solution.py:227
  72.5 1.5 %collective-permute-start.9 = (bf16[2,128,256]{2,1,0:T(8,128)(2,1)}, bf16[2,128,256]{2,1,0:T(8,128)(2,1)S(1)}, u32[]{:S(2)}, u32[]{:S(2)}) collective-permute-start(bf16[2,128,256]{2,1,0:T(8,128)(2,1)} %get-tuple-element.35), channel_id=1, source_target_pairs={{1,0},{2,1},{3,2},{4,3},{5,4},{6,5},{7,6},{9,8},{10,9},{11,10},{12... | collective-permute-start | bytes 393224 | tf_op jit(solution)/shard_map/ppermute | solution.py:227
  74.0 2.3 %copy-done.5 = bf16[2,6,768,256]{3,2,1,0:T(8,128)(2,1)S(1)} copy-done((bf16[2,6,768,256]{3,2,1,0:T(8,128)(2,1)S(1)}, bf16[2,6,768,256]{3,2,1,0:T(8,128)(2,1)}, u32[]{:S(2)}) %copy-start.5) | copy-done | bytes 4718616
  76.3 3.4 %shard_map.72 = (f32[256,1152]{1,0:T(8,128)S(1)}, f32[256,1152]{1,0:T(8,128)S(1)}) custom-call(bf16[2,4,256,256]{3,2,1,0:T(8,128)(2,1)S(1)} %copy-done.15, bf16[2,6,768,256]{3,2,1,0:T(8,128)(2,1)S(1)} %copy-done.5), custom_call_target="tpu_custom_call" | custom-call | tf_op jit(solution)/shard_map/pallas_call | solution.py:313
  79.8 0.5 collective-permute-done.9.gr_ref
  80.3 0.6 copy-done.11
  81.0 2.7 %copy-done.1 = bf16[4,2880,256]{2,1,0:T(8,128)(2,1)S(1)} copy-done((bf16[4,2880,256]{2,1,0:T(8,128)(2,1)S(1)}, bf16[4,2880,256]{2,1,0:T(8,128)(2,1)}, u32[]{:S(2)}) %copy-start.1) | copy-done | bytes 5898264
  83.6 2.2 %shard_map.71 = f32[128,1728]{1,0:T(8,128)S(1)} custom-call(f32[2,4,128,256]{3,2,1,0:T(8,128)S(1)} %copy-done.11, bf16[2,6,128,256]{3,2,1,0:T(8,128)(2,1)S(1)} %copy.34.gx_ref, bf16[2,128,256]{2,1,0:T(8,128)(2,1)S(1)} %collective-permute-done.8.gl_ref, bf16[2,128,256]{2,1,0:T(8,128)(2,1)S(1)} %collective-permute-done.9.gr_ref, ...), custom_call_target="tpu_custom_call" | custom-call | tf_op jit(solution)/shard_map/pallas_call | solution.py:322
  85.8 0.1 collective-permute-start.10
  86.0 0.5 collective-permute-start.12
  86.5 0.1 convert_element_type.66
  86.6 0.8 collective-permute-done.10
  87.4 0.7 fusion.1
  88.1 7.6 %all-to-all-start = ((bf16[8,8,1728]{2,1,0:T(8,128)(2,1)}), bf16[8,8,1728]{2,1,0:T(8,128)(2,1)S(1)}, u32[]{:S(2)}, u32[]{:S(2)}) async-start(bf16[8,8,1728]{2,1,0:T(8,128)(2,1)} %fusion.1), calls=%async_computation | async-start | bytes 458752 | tf_op jit(solution)/shard_map/all_to_all | solution.py:342
  95.8 0.1 fusion
  95.8 1.0 pad_maximum_fusion.2
  96.8 7.7 %all-to-all-done = bf16[8,8,1728]{2,1,0:T(8,128)(2,1)S(1)} async-done(((bf16[8,8,1728]{2,1,0:T(8,128)(2,1)}), bf16[8,8,1728]{2,1,0:T(8,128)(2,1)S(1)}, u32[]{:S(2)}, u32[]{:S(2)}) %all-to-all-start) | async-done | bytes 221216 | tf_op jit(solution)/shard_map/all_to_all | solution.py:342
  104.5 3.6 %all-to-all-start.1 = ((bf16[8,48,1152]{2,1,0:T(8,128)(2,1)}), bf16[8,48,1152]{2,1,0:T(8,128)(2,1)S(1)}, u32[]{:S(2)}, u32[]{:S(2)}) async-start(bf16[8,48,1152]{2,1,0:T(8,128)(2,1)} %pad_maximum_fusion.2), calls=%async_computation.1 | async-start | bytes 1769472 | tf_op jit(solution)/shard_map/all_to_all | solution.py:340
  108.1 0.1 collective-permute-start.11
  108.2 1.6 %shard_map.70 = bf16[256,2,8,128]{3,2,1,0:T(8,128)(2,1)} custom-call(bf16[2,4,256,256]{3,2,1,0:T(8,128)(2,1)S(1)} %copy-done.13), custom_call_target="tpu_custom_call" | custom-call | tf_op jit(solution)/shard_map/pallas_call | solution.py:316
  109.9 20.2 %all-to-all-done.1 = bf16[8,48,1152]{2,1,0:T(8,128)(2,1)S(1)} async-done(((bf16[8,48,1152]{2,1,0:T(8,128)(2,1)}), bf16[8,48,1152]{2,1,0:T(8,128)(2,1)S(1)}, u32[]{:S(2)}, u32[]{:S(2)}) %all-to-all-start.1) | async-done | bytes 884768 | tf_op jit(solution)/shard_map/all_to_all | solution.py:340
  130.0 0.1 convert_reduce_fusion
  130.2 0.1 collective-permute-start.13
  130.2 0.7 pad_maximum_fusion.5
  130.9 0.8 collective-permute-done.13
  131.8 0.8 pad_maximum_fusion.3
  (61 shorter events, 0.5 us)
Async XLA Ops:
  0.6 1.0 slice-start
  1.8 4.0 %collective-permute-start = (bf16[64,16,256]{2,0,1:T(8,128)(2,1)S(1)}, bf16[64,16,256]{2,0,1:T(8,128)(2,1)S(1)}, u32[]{:S(2)}, u32[]{:S(2)}) collective-permute-start(bf16[64,16,256]{2,0,1:T(8,128)(2,1)S(1)} %bitcast.61), channel_id=1, source_target_pairs={{0,8},{1,9},{2,10},{3,11},{4,12},{5,13},{6,14},{7,15},{16,24},{17,... | collective-permute-start | bytes 1572872 | tf_op jit(solution)/shard_map/ppermute | solution.py:227
  5.8 0.8 copy-start.23
  6.7 17.5 %collective-permute-start.1 = (bf16[5,64,256]{2,1,0:T(8,128)(2,1)S(1)}, bf16[5,64,256]{2,1,0:T(8,128)(2,1)S(1)}, u32[]{:S(2)}, u32[]{:S(2)}) collective-permute-start(bf16[5,64,256]{2,1,0:T(8,128)(2,1)S(1)} %pad_maximum_fusion.4), channel_id=1, source_target_pairs={{0,1},{1,2},{2,3},{3,4},{4,5},{5,6},{6,7},{8,9},{9,10},{10,11},{11... | collective-permute-start | bytes 491528 | tf_op jit(solution)/shard_map/ppermute | solution.py:227
  10.9 4.1 %copy-start.6 = (bf16[64,4,16,256]{3,2,1,0:T(8,128)(2,1)S(1)}, bf16[64,4,16,256]{3,2,1,0:T(8,128)(2,1)}, u32[]{:S(2)}) copy-start(bf16[64,4,16,256]{3,2,1,0:T(8,128)(2,1)} %vol_ref.1) | copy-start | bytes 6291460
  10.9 4.1 %copy-start.7 = (bf16[256,2,8,128]{3,2,1,0:T(8,128)(2,1)S(1)}, bf16[256,2,8,128]{3,2,1,0:T(8,128)(2,1)}, u32[]{:S(2)}) copy-start(bf16[256,2,8,128]{3,2,1,0:T(8,128)(2,1)} %tgt_ref.1) | copy-start | bytes 3145732
  19.1 2.5 %copy-start.2 = (bf16[4,2880,256]{2,1,0:T(8,128)(2,1)}, bf16[4,2880,256]{2,1,0:T(8,128)(2,1)S(1)}, u32[]{:S(2)}) copy-start(bf16[4,2880,256]{2,1,0:T(8,128)(2,1)S(1)} %get-tuple-element.18.own_ref) | copy-start | bytes 17694724
  21.6 1.0 copy-start.8
  22.6 1.3 copy-start.24
  24.2 0.7 copy-start.16
  24.9 2.7 %copy-start.3 = (bf16[4,2880,256]{2,1,0:T(8,128)(2,1)S(1)}, bf16[4,2880,256]{2,1,0:T(8,128)(2,1)}, u32[]{:S(2)}) copy-start(bf16[4,2880,256]{2,1,0:T(8,128)(2,1)} %copy-done.2) | copy-start | bytes 17694724
  27.5 0.9 copy-start.17
  28.5 5.4 %copy-start.20 = (bf16[256,3456]{0,1:T(8,128)(2,1)S(1)}, bf16[256,3456]{0,1:T(8,128)(2,1)}, u32[]{:S(2)}) copy-start(bf16[256,3456]{0,1:T(8,128)(2,1)} %copy.29) | copy-start | bytes 5308420
  31.4 2.5 %copy-start = (bf16[4,2880,256]{2,1,0:T(8,128)(2,1)}, bf16[4,2880,256]{2,1,0:T(8,128)(2,1)S(1)}, u32[]{:S(2)}) copy-start(bf16[4,2880,256]{2,1,0:T(8,128)(2,1)S(1)} %get-tuple-element.28.vp_ref) | copy-start | bytes 17694724
  33.9 19.7 %collective-permute-start.4 = (bf16[2,4,128,256]{3,2,1,0:T(8,128)(2,1)}, bf16[2,4,128,256]{3,2,1,0:T(8,128)(2,1)}, u32[]{:S(2)}, u32[]{:S(2)}) collective-permute-start(bf16[2,4,128,256]{3,2,1,0:T(8,128)(2,1)} %get-tuple-element.19.refs_0_), channel_id=1, source_target_pairs={{0,8},{8,0},{1,9},{9,1},{2,10},{10,2},{3,11},{11,3},{4,12},{12,4},... | collective-permute-start | bytes 1572872 | tf_op jit(solution)/shard_map/ppermute | solution.py:231
  34.0 0.9 copy-start.18
  34.0 1.1 copy-start.19
  35.1 10.2 %collective-permute-start.2 = (bf16[2,128,256]{2,1,0:T(8,128)(2,1)S(1)}, bf16[2,128,256]{2,1,0:T(8,128)(2,1)S(1)}, u32[]{:S(2)}, u32[]{:S(2)}) collective-permute-start(bf16[2,128,256]{2,1,0:T(8,128)(2,1)S(1)} %get-tuple-element.20), channel_id=1, source_target_pairs={{0,1},{1,2},{2,3},{3,4},{4,5},{5,6},{6,7},{8,9},{9,10},{10,11},{11... | collective-permute-start | bytes 393224 | tf_op jit(solution)/shard_map/ppermute | solution.py:227
  38.5 7.6 %collective-permute-start.3 = (bf16[2,128,256]{2,1,0:T(8,128)(2,1)S(1)}, bf16[2,128,256]{2,1,0:T(8,128)(2,1)}, u32[]{:S(2)}, u32[]{:S(2)}) collective-permute-start(bf16[2,128,256]{2,1,0:T(8,128)(2,1)S(1)} %get-tuple-element.21), channel_id=1, source_target_pairs={{1,0},{2,1},{3,2},{4,3},{5,4},{6,5},{7,6},{9,8},{10,9},{11,10},{12... | collective-permute-start | bytes 393224 | tf_op jit(solution)/shard_map/ppermute | solution.py:227
  45.3 8.3 %collective-permute-start.5 = (bf16[2,128,256]{2,1,0:T(8,128)(2,1)S(1)}, bf16[2,128,256]{2,1,0:T(8,128)(2,1)}, u32[]{:S(2)}, u32[]{:S(2)}) collective-permute-start(bf16[2,128,256]{2,1,0:T(8,128)(2,1)S(1)} %collective-permute-done.2.refs_1_), channel_id=1, source_target_pairs={{0,8},{8,0},{1,9},{9,1},{2,10},{10,2},{3,11},{11,3},{4,12},{12,4},... | collective-permute-start | bytes 393224 | tf_op jit(solution)/shard_map/ppermute | solution.py:231
  46.1 7.5 %collective-permute-start.6 = (bf16[2,128,256]{2,1,0:T(8,128)(2,1)}, bf16[2,128,256]{2,1,0:T(8,128)(2,1)}, u32[]{:S(2)}, u32[]{:S(2)}) collective-permute-start(bf16[2,128,256]{2,1,0:T(8,128)(2,1)} %collective-permute-done.3.refs_2_), channel_id=1, source_target_pairs={{0,8},{8,0},{1,9},{9,1},{2,10},{10,2},{3,11},{11,3},{4,12},{12,4},... | collective-permute-start | bytes 393224 | tf_op jit(solution)/shard_map/ppermute | solution.py:231
  53.6 1.2 copy-start.9
  61.5 2.2 %copy-start.4 = (bf16[2,6,768,256]{3,2,1,0:T(8,128)(2,1)}, bf16[2,6,768,256]{3,2,1,0:T(8,128)(2,1)S(1)}, u32[]{:S(2)}) copy-start(bf16[2,6,768,256]{3,2,1,0:T(8,128)(2,1)S(1)} %get-tuple-element.30.hs_ref) | copy-start | bytes 14155780
  63.7 1.0 copy-start.14
  64.7 3.4 %copy-start.10 = (f32[2,4,128,256]{3,2,1,0:T(8,128)}, f32[2,4,128,256]{3,2,1,0:T(8,128)S(1)}, u32[]{:S(2)}) copy-start(f32[2,4,128,256]{3,2,1,0:T(8,128)S(1)} %get-tuple-element.24.gown_ref) | copy-start | bytes 3145732
  64.7 3.4 %copy-start.12 = (bf16[2,4,256,256]{3,2,1,0:T(8,128)(2,1)}, bf16[2,4,256,256]{3,2,1,0:T(8,128)(2,1)S(1)}, u32[]{:S(2)}) copy-start(bf16[2,4,256,256]{3,2,1,0:T(8,128)(2,1)S(1)} %get-tuple-element.23.pred_ref) | copy-start | bytes 3145732
  64.7 9.2 %copy-start.15 = (bf16[2,4,256,256]{3,2,1,0:T(8,128)(2,1)S(1)}, bf16[2,4,256,256]{3,2,1,0:T(8,128)(2,1)}, u32[]{:S(2)}) copy-start(bf16[2,4,256,256]{3,2,1,0:T(8,128)(2,1)} %copy-done.14) | copy-start | bytes 3145732
  64.8 2.5 %collective-permute-start.7 = (bf16[2,6,128,256]{3,2,0,1:T(8,128)(2,1)S(1)}, bf16[2,6,128,256]{3,2,0,1:T(8,128)(2,1)S(1)}, u32[]{:S(2)}, u32[]{:S(2)}) collective-permute-start(bf16[2,6,128,256]{3,2,0,1:T(8,128)(2,1)S(1)} %copy.33), channel_id=1, source_target_pairs={{0,8},{8,0},{1,9},{9,1},{2,10},{10,2},{3,11},{11,3},{4,12},{12,4},... | collective-permute-start | bytes 2359304 | tf_op jit(solution)/shard_map/ppermute | solution.py:231
  67.3 5.2 %copy-start.21 = (bf16[2,6,128,256]{3,2,0,1:T(8,128)(2,1)}, bf16[2,6,128,256]{3,2,0,1:T(8,128)(2,1)S(1)}, u32[]{:S(2)}) copy-start(bf16[2,6,128,256]{3,2,0,1:T(8,128)(2,1)S(1)} %collective-permute-done.7) | copy-start | bytes 2359300
  68.1 11.7 %collective-permute-start.8 = (bf16[2,128,256]{2,1,0:T(8,128)(2,1)}, bf16[2,128,256]{2,1,0:T(8,128)(2,1)S(1)}, u32[]{:S(2)}, u32[]{:S(2)}) collective-permute-start(bf16[2,128,256]{2,1,0:T(8,128)(2,1)} %get-tuple-element.36), channel_id=1, source_target_pairs={{0,1},{1,2},{2,3},{3,4},{4,5},{5,6},{6,7},{8,9},{9,10},{10,11},{11... | collective-permute-start | bytes 393224 | tf_op jit(solution)/shard_map/ppermute | solution.py:227
  72.5 7.9 %collective-permute-start.9 = (bf16[2,128,256]{2,1,0:T(8,128)(2,1)}, bf16[2,128,256]{2,1,0:T(8,128)(2,1)S(1)}, u32[]{:S(2)}, u32[]{:S(2)}) collective-permute-start(bf16[2,128,256]{2,1,0:T(8,128)(2,1)} %get-tuple-element.35), channel_id=1, source_target_pairs={{1,0},{2,1},{3,2},{4,3},{5,4},{6,5},{7,6},{9,8},{10,9},{11,10},{12... | collective-permute-start | bytes 393224 | tf_op jit(solution)/shard_map/ppermute | solution.py:227
  74.0 2.3 %copy-start.5 = (bf16[2,6,768,256]{3,2,1,0:T(8,128)(2,1)S(1)}, bf16[2,6,768,256]{3,2,1,0:T(8,128)(2,1)}, u32[]{:S(2)}) copy-start(bf16[2,6,768,256]{3,2,1,0:T(8,128)(2,1)} %copy-done.4) | copy-start | bytes 14155780
  76.3 3.4 %copy-start.22 = (bf16[2,6,128,256]{3,2,0,1:T(8,128)(2,1)S(1)}, bf16[2,6,128,256]{3,2,0,1:T(8,128)(2,1)}, u32[]{:S(2)}) copy-start(bf16[2,6,128,256]{3,2,0,1:T(8,128)(2,1)} %copy-done.21) | copy-start | bytes 2359300
  79.7 1.2 copy-start.11
  81.0 2.7 %copy-start.1 = (bf16[4,2880,256]{2,1,0:T(8,128)(2,1)S(1)}, bf16[4,2880,256]{2,1,0:T(8,128)(2,1)}, u32[]{:S(2)}) copy-start(bf16[4,2880,256]{2,1,0:T(8,128)(2,1)} %copy-done) | copy-start | bytes 17694724
  85.8 1.6 %collective-permute-start.10 = (bf16[8,8,1728]{2,1,0:T(8,128)(2,1)S(1)}, bf16[8,8,1728]{2,1,0:T(8,128)(2,1)S(1)}, u32[]{:S(2)}, u32[]{:S(2)}) collective-permute-start(bf16[8,8,1728]{2,1,0:T(8,128)(2,1)S(1)} %fusion.5), channel_id=1, source_target_pairs={{0,8},{8,0},{1,9},{9,1},{2,10},{10,2},{3,11},{11,3},{4,12},{12,4},... | collective-permute-start | bytes 663560 | tf_op jit(solution)/shard_map/ppermute | solution.py:231
  86.0 9.7 %collective-permute-start.12 = (bf16[8,16,1152]{2,1,0:T(8,128)(2,1)S(1)}, bf16[8,16,1152]{2,1,0:T(8,128)(2,1)S(1)}, u32[]{:S(2)}, u32[]{:S(2)}) collective-permute-start(bf16[8,16,1152]{2,1,0:T(8,128)(2,1)S(1)} %fusion.2), channel_id=1, source_target_pairs={{0,8},{8,0},{1,9},{9,1},{2,10},{10,2},{3,11},{11,3},{4,12},{12,4},... | collective-permute-start | bytes 884744 | tf_op jit(solution)/shard_map/ppermute | solution.py:231
  88.1 16.4 %all-to-all-start = ((bf16[8,8,1728]{2,1,0:T(8,128)(2,1)}), bf16[8,8,1728]{2,1,0:T(8,128)(2,1)S(1)}, u32[]{:S(2)}, u32[]{:S(2)}) async-start(bf16[8,8,1728]{2,1,0:T(8,128)(2,1)} %fusion.1), calls=%async_computation | async-start | bytes 458752 | tf_op jit(solution)/shard_map/all_to_all | solution.py:342
  96.8 11.4 %copy-start.13 = (bf16[2,4,256,256]{3,2,1,0:T(8,128)(2,1)S(1)}, bf16[2,4,256,256]{3,2,1,0:T(8,128)(2,1)}, u32[]{:S(2)}) copy-start(bf16[2,4,256,256]{3,2,1,0:T(8,128)(2,1)} %copy-done.12) | copy-start | bytes 3145732
  104.5 25.5 %all-to-all-start.1 = ((bf16[8,48,1152]{2,1,0:T(8,128)(2,1)}), bf16[8,48,1152]{2,1,0:T(8,128)(2,1)S(1)}, u32[]{:S(2)}, u32[]{:S(2)}) async-start(bf16[8,48,1152]{2,1,0:T(8,128)(2,1)} %pad_maximum_fusion.2), calls=%async_computation.1 | async-start | bytes 1769472 | tf_op jit(solution)/shard_map/all_to_all | solution.py:340
  108.1 1.7 %collective-permute-start.11 = (f32[8,1728]{1,0:T(8,128)S(1)}, f32[8,1728]{1,0:T(8,128)S(1)}, u32[]{:S(2)}, u32[]{:S(2)}) collective-permute-start(f32[8,1728]{1,0:T(8,128)S(1)} %convert_reduce_fusion.1), channel_id=1, source_target_pairs={{0,8},{8,0},{1,9},{9,1},{2,10},{10,2},{3,11},{11,3},{4,12},{12,4},... | collective-permute-start | bytes 165896 | tf_op jit(solution)/shard_map/ppermute | solution.py:231
  130.2 1.5 %collective-permute-start.13 = (f32[48,1152]{1,0:T(8,128)S(1)}, f32[48,1152]{1,0:T(8,128)S(1)}, u32[]{:S(2)}, u32[]{:S(2)}) collective-permute-start(f32[48,1152]{1,0:T(8,128)S(1)} %convert_reduce_fusion), channel_id=1, source_target_pairs={{0,8},{8,0},{1,9},{9,1},{2,10},{10,2},{3,11},{11,3},{4,12},{12,4},... | collective-permute-start | bytes 663560 | tf_op jit(solution)/shard_map/ppermute | solution.py:231

commit v2 on v1

--- a/solution.py
+++ b/solution.py
@@ -14,12 +14,13 @@
 VMEM_LIMIT = 24 * 1024 * 1024
 
 
-def vmem_call(body, out_shape, n_in, scratch=()):
+def vmem_call(body, out_shape, n_in, scratch=(), scalars=0):
     spec = pl.BlockSpec(memory_space=pltpu.VMEM)
+    scalar = pl.BlockSpec(memory_space=pltpu.SMEM)
     return pl.pallas_call(
         body,
         out_shape=out_shape,
-        in_specs=[spec] * n_in,
+        in_specs=[scalar] * scalars + [spec] * n_in,
         out_specs=jax.tree.map(lambda _: spec, out_shape),
         scratch_shapes=list(scratch),
         compiler_params=pltpu.CompilerParams(vmem_limit_bytes=VMEM_LIMIT),
@@ -124,9 +125,35 @@
     return jnp.concatenate(parts, axis=1)
 
 
+def weights_body(slab_ref, wd_ref, ws_ref, w2_ref, wg_ref, wst_ref):
+    outs, width = wd_ref.shape
+    mid = width // 27
+    wst_ref[...] = ws_ref[...].T
+
+    def fill(src, a):
+        for b in range(3):
+            block = (a * 3 + b) * 3 * mid
+            to = (b * 2 + src) * 3 * mid
+            w2_ref[:, to : to + 3 * mid] = wd_ref[:, block : block + 3 * mid]
+            for c in range(3):
+                tap = wd_ref[:, block + c * mid : block + (c + 1) * mid]
+                column = ((2 - b) * 3 + c) * outs
+                wg_ref[src * mid : (src + 1) * mid, column : column + outs] = tap.T
+
+    fill(0, 1)
+
+    @pl.when(slab_ref[0] == 0)
+    def _():
+        fill(1, 2)
+
+    @pl.when(slab_ref[0] != 0)
+    def _():
+        fill(1, 0)
+
+
 def forward_body(
-    scale, step, h_ref, hl_ref, hr_ref, o_ref, ol_ref, or_ref, w2_ref, wg_ref, tp_ref,
-    hs_ref, pred_ref, res_ref, gown_ref, ghalo_ref, gother_ref, rs_ref,
+    scale, step, h_ref, hl_ref, hr_ref, o_ref, ol_ref, or_ref, w2_ref, tp_ref,
+    hs_ref, pred_ref, rs_ref,
 ):
     orows, pairs, mid, lanes = h_ref.shape
     outs = w2_ref.shape[0]
@@ -147,12 +174,15 @@
             out = jnp.dot(w2_ref[...], window, preferred_element_type=F32)
             pred_ref[r, m] = out.astype(BF16)
             res = ((out - tp_ref[r, m].astype(F32)) * scale).astype(BF16)
-            res_ref[r, m] = res
             wide = res.astype(F32)
             rs_ref[r, m, 0:outs, :] = shifted(wide, -step).astype(BF16)
             rs_ref[r, m, outs : 2 * outs, :] = res
             rs_ref[r, m, 2 * outs : 3 * outs, :] = shifted(wide, step).astype(BF16)
-    block = 3 * outs
+
+
+def hidden_grad_body(rs_ref, wg_ref, gown_ref, ghalo_ref, gother_ref):
+    orows, pairs, block, lanes = rs_ref.shape
+    mid = gown_ref.shape[2]
     for r in range(orows):
         for x in range(pairs + 2):
             low, high = max(x - 2, 0), min(x, pairs - 1)
@@ -172,22 +202,38 @@
 NT = (((1,), (1,)), ((), ()))
 
 
-def dilated_grad_body(res_ref, hs_ref, own_ref, other_ref):
-    orows, pairs, outs, lanes = res_ref.shape
+def split_rows(slab_ref, total, mine_ref, send_ref, columns):
+    strips, rows, _ = mine_ref.shape
+    parts = total.reshape(strips, 2, rows, total.shape[1])
+    first = slab_ref[0] == 0
+    mine_ref[:, :, columns] = jnp.where(first, parts[:, 0], parts[:, 1])
+    send_ref[:, :, columns] = jnp.where(first, parts[:, 1], parts[:, 0]).astype(BF16)
+
+
+def dilated_grad_body(slab_ref, rs_ref, hs_ref, mine_ref, send_ref, other_ref):
+    orows, pairs, block, lanes = rs_ref.shape
+    outs = block // 3
     mid = hs_ref.shape[2] // 6
     for b in range(3):
-        for src, ref in enumerate((own_ref, other_ref)):
+        columns = slice(b * 3 * mid, (b + 1) * 3 * mid)
+        for src in range(2):
             base = src * 3 * mid
             total = None
             for r in range(orows):
                 for m in range(pairs):
                     window = hs_ref[r, m + b, base : base + 3 * mid, :]
-                    part = lax.dot_general(res_ref[r, m], window, NT, preferred_element_type=F32)
+                    part = lax.dot_general(
+                        rs_ref[r, m, outs : 2 * outs, :], window, NT, preferred_element_type=F32
+                    )
                     total = part if total is None else total + part
-            ref[:, b * 3 * mid : (b + 1) * 3 * mid] = total
-
-
-def strided_grad_body(gown_ref, gx_ref, gl_ref, gr_ref, slope_ref, vp_ref, out_ref):
+            if src == 0:
+                split_rows(slab_ref, total, mine_ref, send_ref, columns)
+            else:
+                strips, rows, _ = other_ref.shape
+                other_ref[:, :, columns] = total.reshape(strips, rows, 3 * mid).astype(BF16)
+
+
+def strided_grad_body(slab_ref, gown_ref, gx_ref, gl_ref, gr_ref, slope_ref, vp_ref, mine_ref, send_ref):
     orows, pairs, mid, lanes = gown_ref.shape
     plane = vp_ref.shape[1] // (2 * orows + 1)
     total = None
@@ -202,7 +248,7 @@
             window = vp_ref[m, 2 * i * plane : (2 * i + 3) * plane, :]
             part = lax.dot_general(pg, window, NT, preferred_element_type=F32)
             total = part if total is None else total + part
-    out_ref[...] = total
+    split_rows(slab_ref, total, mine_ref, send_ref, slice(None))
 
 
 def prediction_body(pred_ref, out_ref, tall_ref):
@@ -239,6 +285,7 @@
     pairs, lanes = ocols // 2, 2 * half
     strips = lax.axis_size("strip")
     slab = lax.axis_index("slab")
+    slab_id = slab.reshape(1).astype(jnp.int32)
     step = 2
     assert lax.axis_size("slab") == 2 and orows == step and ocols % 2 == 0
     cells = orows * ocols * half * lax.axis_size("slab") * strips
@@ -248,17 +295,16 @@
     last = jnp.concatenate([lower[None, :, -1, :], volume[:, :, -1, :].transpose(1, 0, 2)], axis=0)
     left = shift_along(last, "strip", 1)
 
-    planes = dilated_weight.reshape(outs, 3, 9 * mid)
-    w_own = planes[:, 1].reshape(outs, 3, 3 * mid)
-    w_other = lax.dynamic_index_in_dim(planes, 2 - 2 * slab, 1, False).reshape(outs, 3, 3 * mid)
-    both = jnp.stack([w_own, w_other], axis=2)
-    w2 = both.reshape(outs, 18 * mid)
-    wg = (
-        both.reshape(outs, 3, 2, 3, mid)[:, ::-1]
-        .transpose(2, 4, 1, 3, 0)
-        .reshape(2 * mid, 9 * outs)
-    )
-
+    w2, wg, ws = vmem_call(
+        weights_body,
+        (
+            sds((outs, 18 * mid), BF16),
+            sds((2 * mid, 9 * outs), BF16),
+            sds((mid, 27 * channels), BF16),
+        ),
+        2,
+        scalars=1,
+    )(slab_id, dilated_weight, strided_weight.T)
     vp, tp = vmem_call(
         split_body,
         (
@@ -279,7 +325,7 @@
         ),
         4,
         [VMEM((3, channels * cols_in, half), F32)],
-    )(vp, lower, left, strided_weight)
+    )(vp, lower, left, ws)
 
     from_left = shift_along(hid_r, "strip", 1)
     from_right = shift_along(hid_l, "strip", -1)
@@ -290,19 +336,41 @@
     def forward(*refs):
         forward_body(scale, step, *refs)
 
-    hs, pred, residual, gown, ghalo, gother = vmem_call(
+    hs, pred, residual = vmem_call(
         forward,
         (
             sds((orows, pairs + 2, 6 * mid, lanes), BF16),
             sds((orows, pairs, outs, lanes), BF16),
-            sds((orows, pairs, outs, lanes), BF16),
+            sds((orows, pairs, 3 * outs, lanes), BF16),
+        ),
+        8,
+    )(hidden, from_left, from_right, other, other_left, other_right, w2, tp)
+
+    rows = outs // strips
+    half_rows = rows // 2
+    mine, send, apart = vmem_call(
+        dilated_grad_body,
+        (
+            sds((strips, half_rows, 9 * mid), F32),
+            sds((strips, half_rows, 9 * mid), BF16),
+            sds((strips, rows, 9 * mid), BF16),
+        ),
+        2,
+        scalars=1,
+    )(slab_id, residual, hs)
+    dg = jnp.concatenate([(mine + swap(send).astype(F32)).astype(BF16), apart], axis=1)
+    dg, residual = lax.optimization_barrier((dg, residual))
+    dg = lax.all_to_all(dg, "strip", 0, 0, tiled=True)
+
+    gown, ghalo, gother = vmem_call(
+        hidden_grad_body,
+        (
             sds((orows, pairs, mid, lanes), F32),
             sds((2, orows, mid, lanes), F32),
             sds((orows, pairs + 2, mid, lanes), BF16),
         ),
-        9,
-        [VMEM((orows, pairs, 3 * outs, lanes), BF16)],
-    )(hidden, from_left, from_right, other, other_left, other_right, w2, wg, tp)
+        2,
+    )(residual, wg)
 
     gx = swap(gother)
     to_left = (ghalo[0] + gx[:, 0].astype(F32)).astype(BF16)
@@ -310,45 +378,34 @@
     grad_l = shift_along(to_right, "strip", 1)
     grad_r = shift_along(to_left, "strip", -1)
 
-    dg_own, dg_other = vmem_call(
-        dilated_grad_body, (sds((outs, 9 * mid), F32), sds((outs, 9 * mid), F32)), 2
-    )(residual, hs)
     prediction = vmem_call(
         prediction_body,
         sds((outs, orows, ocols, half), BF16),
         1,
         [VMEM((2, outs * ocols, half), F32)],
     )(pred)
-    sg = vmem_call(strided_grad_body, sds((mid, 27 * channels), F32), 6)(
-        gown, gx, grad_l, grad_r, slope, vp
-    )
-
-    def halves(grad):
-        rows = grad.shape[0] // strips
-        return grad.reshape(strips, 2, rows // 2, grad.shape[1])
-
-    def combined(grad):
-        parts = halves(grad)
-        mine = lax.dynamic_index_in_dim(parts, slab, 1, False)
-        theirs = lax.dynamic_index_in_dim(parts, 1 - slab, 1, False)
-        return mine + swap(theirs.astype(BF16)).astype(F32)
-
-    rows = outs // strips
-    dg = jnp.concatenate(
-        [combined(dg_own).astype(BF16), dg_other.astype(BF16).reshape(strips, rows, 9 * mid)], axis=1
-    )
-    dg = lax.all_to_all(dg, "strip", 0, 0, tiled=True)
+    mid_rows = mid // strips // 2
+    smine, ssend = vmem_call(
+        strided_grad_body,
+        (
+            sds((strips, mid_rows, 27 * channels), F32),
+            sds((strips, mid_rows, 27 * channels), BF16),
+        ),
+        6,
+        scalars=1,
+    )(slab_id, gown, gx, grad_l, grad_r, slope, vp)
+    sg = (smine + swap(ssend).astype(F32)).astype(BF16)
+    sg = lax.all_to_all(sg, "strip", 0, 0, tiled=True)
+
+    sg = jnp.sum(sg.astype(F32), axis=0)
     dg = jnp.sum(dg.astype(F32), axis=0)
-    sgc = lax.all_to_all(combined(sg).astype(BF16), "strip", 0, 0, tiled=True)
-    sgc = jnp.sum(sgc.astype(F32), axis=0)
-    dg_x, sg_x = swap(dg), swap(sgc)
+    dg_x, sg_x = swap(dg), swap(sg)
     first = slab == 0
-    half_rows = rows // 2
     dg0, dg1 = jnp.where(first, dg, dg_x), jnp.where(first, dg_x, dg)
     middle = jnp.concatenate([dg0[:half_rows], dg1[:half_rows]], axis=0)
     dilated_grad = jnp.concatenate([dg1[half_rows:], middle, dg0[half_rows:]], axis=1)
     strided_grad = jnp.concatenate(
-        [jnp.where(first, sgc, sg_x), jnp.where(first, sg_x, sgc)], axis=0
+        [jnp.where(first, sg, sg_x), jnp.where(first, sg_x, sg)], axis=0
     )
     return prediction, strided_grad, dilated_grad
 

time: 133 us -> 103 us (0.77)
  local copies, waits for them, and re-layouts: 42.2 us -> 3.46 us
  blocking collectives: 0 us -> 14.6 us
  starting transfers between devices: 30.2 us -> 22.4 us
  waiting for transfers between devices: 32.5 us -> 39.4 us
  other arithmetic: 5.79 us -> 2.83 us
  Pallas kernels: 20.8 us -> 19.4 us
    unnamed x54 -> x14, local copies, waits for them, and re-layouts: 27.7 us -> 1.51 us
    all_to_all x0 -> x1, blocking collectives: none -> 14.6 us  [local(): sg = lax.all_to_all(sg, 'strip', 0, 0, tiled=True)]
    ppermute x6, waiting for transfers between devices: 1.06 us -> 12 us  [shift_along(): return lax.ppermute(value, axis, pairs)]
    reshape x3 -> x0, local copies, waits for them, and re-layouts: 8.36 us -> none  [the longest x2 5.21 us: local(): wg = both.reshape(outs, 3, 2, 3, mid)[:, ::-1].transpose(2, 4, 1, 3, 0).r...]
    all_to_all x1 -> x0, waiting for transfers between devices: 7.68 us -> none  [local(): sgc = lax.all_to_all(combined(sg).astype(BF16), 'strip', 0, 0, tiled=True)]
    all_to_all x1 -> x0, starting transfers between devices: 7.63 us -> none  [local(): sgc = lax.all_to_all(combined(sg).astype(BF16), 'strip', 0, 0, tiled=True)]
    pallas_call x1, Pallas kernels: 6.6 us -> 2.94 us  [local(): vmem_call(forward, (sds((orows, pairs + 2, 6 * mid, lanes), BF16), sds((o...]
    ppermute x8, waiting for transfers between devices: 3.54 us -> 7.17 us  [swap(): return lax.ppermute(value, 'slab', [(0, 1), (1, 0)])]
  transfers between devices with their start and end apart: 16 -> 15, of which waited for: 7 -> 11; matrix products, arithmetic and copies ran while one was open for 17% -> 1% of each run, Pallas kernels for 7% -> 6%
where the time goes in v2:
time: 103 us
  waiting for transfers between devices  39.4 us (38%)
  starting transfers between devices  22.4 us (22%)
  Pallas kernels  19.4 us (19%)
  blocking collectives  14.6 us (14%)
  local copies, waits for them, and re-layouts  3.46 us (3%)
  other arithmetic  2.83 us (3%)
    all_to_all x1, waiting for transfers between devices, local(): dg = lax.all_to_all(dg, 'strip', 0, 0, tiled=True)  20.2 us
    ppermute x6, starting transfers between devices, shift_along(): return lax.ppermute(value, axis, pairs)  18 us
    all_to_all x1, blocking collectives, local(): sg = lax.all_to_all(sg, 'strip', 0, 0, tiled=True)  14.6 us
    ppermute x6, waiting for transfers between devices, shift_along(): return lax.ppermute(value, axis, pairs)  12 us
    ppermute x8, waiting for transfers between devices, swap(): return lax.ppermute(value, 'slab', [(0, 1), (1, 0)])  7.17 us
    pallas_call x1, Pallas kernels, local(): vmem_call(split_body, (sds((pairs, (rows_in + 1) * 9 * channels, lanes),...  4.07 us
    all_to_all x1, starting transfers between devices, local(): dg = lax.all_to_all(dg, 'strip', 0, 0, tiled=True)  3.55 us
    pallas_call x1, Pallas kernels, local(): vmem_call(dilated_grad_body, (sds((strips, half_rows, 9 * mid), F32), sds...  3.41 us
  transfers between devices with their start and end apart: 15, of which 11 were waited for; matrix products, arithmetic and copies ran while one was open for 1% of the time, Pallas kernels for 6%

profile of v2, /device:TPU:0, one launch (start us, length us, event | category | flops | bytes accessed | tf_op | source)
XLA Modules:
  0.0 103.1 jit_solution(1657340718153111136)
XLA Ops:
  0.6 0.0 copy-start
  0.6 0.0 copy-start.2
  0.6 1.2 %slice.33 = bf16[64,1,16,256]{3,2,1,0:T(8,128)(2,1)S(1)} slice(bf16[64,4,16,256]{3,2,1,0:T(8,128)(2,1)} %vol_ref.1), slice={[0:64], [3:4], [0:16], [0:256]} | slice | bytes 1048576 | tf_op jit(solution)/shard_map/slice | solution.py:294
  1.9 0.2 copy.16
  2.1 2.4 %collective-permute-start = (bf16[64,16,256]{2,0,1:T(8,128)(2,1)S(1)}, bf16[64,16,256]{2,0,1:T(8,128)(2,1)S(1)}, u32[]{:S(2)}, u32[]{:S(2)}) collective-permute-start(bf16[64,16,256]{2,0,1:T(8,128)(2,1)S(1)} %bitcast.28), channel_id=1, source_target_pairs={{0,8},{1,9},{2,10},{3,11},{4,12},{5,13},{6,14},{7,15},{16,24},{17,... | collective-permute-start | bytes 1572872 | tf_op jit(solution)/shard_map/ppermute | solution.py:273
  4.5 0.0 copy-done
  4.5 0.3 slice.35
  4.8 1.1 %collective-permute-done = bf16[64,16,256]{2,0,1:T(8,128)(2,1)S(1)} collective-permute-done((bf16[64,16,256]{2,0,1:T(8,128)(2,1)S(1)}, bf16[64,16,256]{2,0,1:T(8,128)(2,1)S(1)}, u32[]{:S(2)}, u32[]{:S(2)}) %collective-permute-start) | collective-permute-done | bytes 524320 | tf_op jit(solution)/shard_map/ppermute | solution.py:273
  5.9 0.0 copy-start.4
  5.9 0.8 copy-done.4
  6.8 4.3 %collective-permute-start.1 = (bf16[5,64,256]{2,1,0:T(8,128)(2,1)S(1)}, bf16[5,64,256]{2,1,0:T(8,128)(2,1)S(1)}, u32[]{:S(2)}, u32[]{:S(2)}) collective-permute-start(bf16[5,64,256]{2,1,0:T(8,128)(2,1)S(1)} %pad_maximum_fusion.2), channel_id=1, source_target_pairs={{0,1},{1,2},{2,3},{3,4},{4,5},{5,6},{6,7},{8,9},{9,10},{10,11},{11... | collective-permute-start | bytes 491528 | tf_op jit(solution)/shard_map/ppermute | solution.py:273
  11.0 0.0 copy-done.2
  11.1 0.0 copy-start.1
  11.1 0.0 copy-start.3
  11.1 4.1 %shard_map.67 = (bf16[4,2880,256]{2,1,0:T(8,128)(2,1)S(1)}, bf16[2,4,256,256]{3,2,1,0:T(8,128)(2,1)S(1)}) custom-call(bf16[64,4,16,256]{3,2,1,0:T(8,128)(2,1)S(1)} %copy-done, bf16[256,2,8,128]{3,2,1,0:T(8,128)(2,1)S(1)} %copy-done.2), custom_call_target="tpu_custom_call" | custom-call | tf_op jit(solution)/shard_map/pallas_call | solution.py:308
  15.2 0.0 copy-start.5
  15.2 0.0 copy-done.1
  15.2 0.0 copy-done.3
  15.2 0.5 shard_map.68
  15.7 0.5 copy-done.5
  16.2 0.3 copy.9.hrow_ref
  16.5 0.0 collective-permute-done.1.hcol_ref
  16.5 2.1 %shard_map.69 = (bf16[4,2880,256]{2,1,0:T(8,128)(2,1)S(1)}, bf16[2,4,128,256]{3,2,1,0:T(8,128)(2,1)S(1)}, bf16[2,128,256]{2,1,0:T(8,128)(2,1)S(1)}, bf16[2,128,2...) custom-call(bf16[4,2880,256]{2,1,0:T(8,128)(2,1)S(1)} %get-tuple-element.26.own_ref, bf16[64,16,256]{2,1,0:T(8,128)(2,1)S(1)} %copy.9.hrow_ref, ...), custom_call_target="tpu_custom_call" | custom-call | tf_op jit(solution)/shard_map/pallas_call | solution.py:317
  18.6 0.1 collective-permute-start.4
  18.8 3.4 %collective-permute-start.2 = (bf16[2,128,256]{2,1,0:T(8,128)(2,1)S(1)}, bf16[2,128,256]{2,1,0:T(8,128)(2,1)S(1)}, u32[]{:S(2)}, u32[]{:S(2)}) collective-permute-start(bf16[2,128,256]{2,1,0:T(8,128)(2,1)S(1)} %get-tuple-element.29), channel_id=1, source_target_pairs={{0,1},{1,2},{2,3},{3,4},{4,5},{5,6},{6,7},{8,9},{9,10},{10,11},{11... | collective-permute-start | bytes 393224 | tf_op jit(solution)/shard_map/ppermute | solution.py:273
  22.2 1.5 %collective-permute-start.3 = (bf16[2,128,256]{2,1,0:T(8,128)(2,1)S(1)}, bf16[2,128,256]{2,1,0:T(8,128)(2,1)S(1)}, u32[]{:S(2)}, u32[]{:S(2)}) collective-permute-start(bf16[2,128,256]{2,1,0:T(8,128)(2,1)S(1)} %get-tuple-element.30), channel_id=1, source_target_pairs={{1,0},{2,1},{3,2},{4,3},{5,4},{6,5},{7,6},{9,8},{10,9},{11,10},{12... | collective-permute-start | bytes 393224 | tf_op jit(solution)/shard_map/ppermute | solution.py:273
  23.7 1.9 %collective-permute-done.2.refs_1_ = bf16[2,128,256]{2,1,0:T(8,128)(2,1)S(1)} collective-permute-done((bf16[2,128,256]{2,1,0:T(8,128)(2,1)S(1)}, bf16[2,128,256]{2,1,0:T(8,128)(2,1)S(1)}, u32[]{:S(2)}, u32[]{:S(2)}) %collective-permute-start.2) | collective-permute-done | bytes 131104 | tf_op jit(solution)/shard_map/ppermute | solution.py:273
  25.5 0.0 collective-permute-start.5
  25.5 4.2 %collective-permute-done.3.refs_2_ = bf16[2,128,256]{2,1,0:T(8,128)(2,1)S(1)} collective-permute-done((bf16[2,128,256]{2,1,0:T(8,128)(2,1)S(1)}, bf16[2,128,256]{2,1,0:T(8,128)(2,1)S(1)}, u32[]{:S(2)}, u32[]{:S(2)}) %collective-permute-start.3) | collective-permute-done | bytes 131104 | tf_op jit(solution)/shard_map/ppermute | solution.py:273
  29.8 0.0 collective-permute-start.6
  29.8 0.0 collective-permute-done.5.refs_4_
  29.8 1.3 %collective-permute-done.6.refs_5_ = bf16[2,128,256]{2,1,0:T(8,128)(2,1)S(1)} collective-permute-done((bf16[2,128,256]{2,1,0:T(8,128)(2,1)S(1)}, bf16[2,128,256]{2,1,0:T(8,128)(2,1)S(1)}, u32[]{:S(2)}, u32[]{:S(2)}) %collective-permute-start.6) | collective-permute-done | bytes 131104 | tf_op jit(solution)/shard_map/ppermute | solution.py:277
  31.1 0.0 collective-permute-done.4.refs_3_
  31.1 2.9 %shard_map.70 = (bf16[2,6,768,256]{3,2,1,0:T(8,128)(2,1)S(1)}, bf16[2,4,256,256]{3,2,1,0:T(8,128)(2,1)S(1)}, bf16[2,4,768,256]{3,2,1,0:T(8,128)(2,1)S(1)}) custom-call(bf16[2,4,128,256]{3,2,1,0:T(8,128)(2,1)S(1)} %get-tuple-element.28.refs_0_, bf16[2,128,256]{2,1,0:T(8,128)(2,1)S(1)} %collective-permute-done.2.refs_1_, ...), custom_call_target="tpu_custom_call" | custom-call | tf_op jit(solution)/shard_map/pallas_call | solution.py:339
  34.1 3.4 %shard_map.72 = (f32[8,16,1152]{2,1,0:T(8,128)S(1)}, bf16[8,16,1152]{2,1,0:T(8,128)(2,1)S(1)}, bf16[8,32,1152]{2,1,0:T(8,128)(2,1)S(1)}) custom-call(s32[1]{0:T(128)} %bitcast.4.slab_ref, bf16[2,4,768,256]{3,2,1,0:T(8,128)(2,1)S(1)} %get-tuple-element.39.rs_ref, bf16[2,6,768,256]{3,2,1,0:T(8,128)(2,1)S(1)} %get-tuple-element.35.hs_ref), custom_call_target="tpu_custom_call" | custom-call | tf_op jit(solution)/shard_map/pallas_call | solution.py:351
  37.5 0.2 collective-permute-start.7
  37.7 1.4 %collective-permute-done.7 = bf16[8,16,1152]{2,1,0:T(8,128)(2,1)S(1)} collective-permute-done((bf16[8,16,1152]{2,1,0:T(8,128)(2,1)S(1)}, bf16[8,16,1152]{2,1,0:T(8,128)(2,1)S(1)}, u32[]{:S(2)}, u32[]{:S(2)}) %collective-permute-start.7) | collective-permute-done | bytes 294944 | tf_op jit(solution)/shard_map/ppermute | solution.py:277
  39.1 0.1 add_convert_fusion
  39.2 1.0 pad_maximum_fusion
  40.2 2.6 %shard_map.73 = (f32[2,4,128,256]{3,2,1,0:T(8,128)S(1)}, f32[2,2,128,256]{3,2,1,0:T(8,128)S(1)}, bf16[2,6,128,256]{3,2,1,0:T(8,128)(2,1)S(1)}) custom-call(bf16[2,4,768,256]{3,2,1,0:T(8,128)(2,1)S(1)} %get-tuple-element.39.rs_ref, bf16[256,2304]{1,0:T(8,128)(2,1)S(1)} %get-tuple-element.40.wg_ref), custom_call_target="tpu_custom_call" | custom-call | tf_op jit(solution)/shard_map/pallas_call | solution.py:365
  42.8 0.1 copy.10
  42.8 0.2 collective-permute-start.8
  43.1 2.1 %collective-permute-done.8 = bf16[2,6,128,256]{3,2,0,1:T(8,128)(2,1)S(1)} collective-permute-done((bf16[2,6,128,256]{3,2,0,1:T(8,128)(2,1)S(1)}, bf16[2,6,128,256]{3,2,0,1:T(8,128)(2,1)S(1)}, u32[]{:S(2)}, u32[]{:S(2)}) %collective-permute-start.8) | collective-permute-done | bytes 786464 | tf_op jit(solution)/shard_map/ppermute | solution.py:277
  45.2 0.1 fusion
  45.3 1.3 %collective-permute-start.10 = (bf16[2,128,256]{2,1,0:T(8,128)(2,1)S(1)}, bf16[2,128,256]{2,1,0:T(8,128)(2,1)S(1)}, u32[]{:S(2)}, u32[]{:S(2)}) collective-permute-start(bf16[2,128,256]{2,1,0:T(8,128)(2,1)S(1)} %get-tuple-element.49), channel_id=1, source_target_pairs={{1,0},{2,1},{3,2},{4,3},{5,4},{6,5},{7,6},{9,8},{10,9},{11,10},{12... | collective-permute-start | bytes 393224 | tf_op jit(solution)/shard_map/ppermute | solution.py:273
  46.6 5.2 %collective-permute-start.9 = (bf16[2,128,256]{2,1,0:T(8,128)(2,1)S(1)}, bf16[2,128,256]{2,1,0:T(8,128)(2,1)S(1)}, u32[]{:S(2)}, u32[]{:S(2)}) collective-permute-start(bf16[2,128,256]{2,1,0:T(8,128)(2,1)S(1)} %get-tuple-element.50), channel_id=1, source_target_pairs={{0,1},{1,2},{2,3},{3,4},{4,5},{5,6},{6,7},{8,9},{9,10},{10,11},{11... | collective-permute-start | bytes 393224 | tf_op jit(solution)/shard_map/ppermute | solution.py:273
  51.8 0.1 copy.11.gx_ref
  51.8 1.8 %collective-permute-done.10.gr_ref = bf16[2,128,256]{2,1,0:T(8,128)(2,1)S(1)} collective-permute-done((bf16[2,128,256]{2,1,0:T(8,128)(2,1)S(1)}, bf16[2,128,256]{2,1,0:T(8,128)(2,1)S(1)}, u32[]{:S(2)}, u32[]{:S(2)}) %collective-permute-start.10) | collective-permute-done | bytes 131104 | tf_op jit(solution)/shard_map/ppermute | solution.py:273
  53.6 3.0 %collective-permute-done.9.gl_ref = bf16[2,128,256]{2,1,0:T(8,128)(2,1)S(1)} collective-permute-done((bf16[2,128,256]{2,1,0:T(8,128)(2,1)S(1)}, bf16[2,128,256]{2,1,0:T(8,128)(2,1)S(1)}, u32[]{:S(2)}, u32[]{:S(2)}) %collective-permute-start.9) | collective-permute-done | bytes 131104 | tf_op jit(solution)/shard_map/ppermute | solution.py:273
  56.6 2.2 %shard_map.74 = (f32[8,8,1728]{2,1,0:T(8,128)S(1)}, bf16[8,8,1728]{2,1,0:T(8,128)(2,1)S(1)}) custom-call(s32[1]{0:T(128)} %bitcast.4.slab_ref, f32[2,4,128,256]{3,2,1,0:T(8,128)S(1)} %get-tuple-element.41.gown_ref, bf16[2,6,128,256]{3,2,1,0:T(8,128)(2,1)S(1)} %copy.11.gx_ref, bf16[2,128,256]{2,1,0:T(8,128)(2,1)S(1)} %collective-permute-done.9.gl_ref, ...), custom_call_target="tpu_custom_call" | custom-call | tf_op jit(solution)/shard_map/pallas_call | solution.py:388
  58.8 0.1 collective-permute-start.11
  58.9 1.5 %collective-permute-done.11 = bf16[8,8,1728]{2,1,0:T(8,128)(2,1)S(1)} collective-permute-done((bf16[8,8,1728]{2,1,0:T(8,128)(2,1)S(1)}, bf16[8,8,1728]{2,1,0:T(8,128)(2,1)S(1)}, u32[]{:S(2)}, u32[]{:S(2)}) %collective-permute-start.11) | collective-permute-done | bytes 221216 | tf_op jit(solution)/shard_map/ppermute | solution.py:277
  60.4 14.6 %all_to_all.10 = bf16[8,8,1728]{2,1,0:T(8,128)(2,1)S(1)} all-to-all(bf16[8,8,1728]{2,1,0:T(8,128)(2,1)S(1)} %add_convert_fusion.1), channel_id=1, replica_groups=mesh['fold'=2,'slab'=2,'strip'=8] {'strip'}, dimensions={0} | all-to-all | bytes 442368 | tf_op jit(solution)/shard_map/all_to_all | solution.py:398
  75.0 3.6 %all-to-all-start.1 = ((bf16[8,48,1152]{2,1,0:T(8,128)(2,1)}), bf16[8,48,1152]{2,1,0:T(8,128)(2,1)S(1)}, u32[]{:S(2)}, u32[]{:S(2)}) async-start(bf16[8,48,1152]{2,1,0:T(8,128)(2,1)} %pad_maximum_fusion), calls=%async_computation.1 | async-start | bytes 1769472 | tf_op jit(solution)/shard_map/all_to_all | solution.py:363
  78.5 1.6 %shard_map.71 = bf16[256,2,8,128]{3,2,1,0:T(8,128)(2,1)} custom-call(bf16[2,4,256,256]{3,2,1,0:T(8,128)(2,1)S(1)} %get-tuple-element.33.pred_ref), custom_call_target="tpu_custom_call" | custom-call | tf_op jit(solution)/shard_map/pallas_call | solution.py:381
  80.2 0.1 collective-permute-start.12
  80.3 20.2 %all-to-all-done.1 = bf16[8,48,1152]{2,1,0:T(8,128)(2,1)S(1)} async-done(((bf16[8,48,1152]{2,1,0:T(8,128)(2,1)}), bf16[8,48,1152]{2,1,0:T(8,128)(2,1)S(1)}, u32[]{:S(2)}, u32[]{:S(2)}) %all-to-all-start.1) | async-done | bytes 884768 | tf_op jit(solution)/shard_map/all_to_all | solution.py:363
  100.5 0.1 convert_reduce_fusion
  100.6 0.1 collective-permute-start.13
  100.7 0.0 collective-permute-done.12
  100.7 0.7 pad_maximum_fusion.3
  101.4 0.8 collective-permute-done.13
  102.3 0.8 pad_maximum_fusion.1
  (11 shorter events, 0.2 us)
Async XLA Ops:
  0.6 3.8 %copy-start = (bf16[64,4,16,256]{3,2,1,0:T(8,128)(2,1)S(1)}, bf16[64,4,16,256]{3,2,1,0:T(8,128)(2,1)}, u32[]{:S(2)}) copy-start(bf16[64,4,16,256]{3,2,1,0:T(8,128)(2,1)} %vol_ref.1) | copy-start | bytes 6291460
  0.6 10.4 %copy-start.2 = (bf16[256,2,8,128]{3,2,1,0:T(8,128)(2,1)S(1)}, bf16[256,2,8,128]{3,2,1,0:T(8,128)(2,1)}, u32[]{:S(2)}) copy-start(bf16[256,2,8,128]{3,2,1,0:T(8,128)(2,1)} %tgt_ref.1) | copy-start | bytes 3145732
  2.1 3.9 %collective-permute-start = (bf16[64,16,256]{2,0,1:T(8,128)(2,1)S(1)}, bf16[64,16,256]{2,0,1:T(8,128)(2,1)S(1)}, u32[]{:S(2)}, u32[]{:S(2)}) collective-permute-start(bf16[64,16,256]{2,0,1:T(8,128)(2,1)S(1)} %bitcast.28), channel_id=1, source_target_pairs={{0,8},{1,9},{2,10},{3,11},{4,12},{5,13},{6,14},{7,15},{16,24},{17,... | collective-permute-start | bytes 1572872 | tf_op jit(solution)/shard_map/ppermute | solution.py:273
  5.9 0.8 copy-start.4
  6.8 9.7 %collective-permute-start.1 = (bf16[5,64,256]{2,1,0:T(8,128)(2,1)S(1)}, bf16[5,64,256]{2,1,0:T(8,128)(2,1)S(1)}, u32[]{:S(2)}, u32[]{:S(2)}) collective-permute-start(bf16[5,64,256]{2,1,0:T(8,128)(2,1)S(1)} %pad_maximum_fusion.2), channel_id=1, source_target_pairs={{0,1},{1,2},{2,3},{3,4},{4,5},{5,6},{6,7},{8,9},{9,10},{10,11},{11... | collective-permute-start | bytes 491528 | tf_op jit(solution)/shard_map/ppermute | solution.py:273
  11.1 4.1 %copy-start.1 = (bf16[256,3456]{1,0:T(8,128)(2,1)S(1)}, bf16[256,3456]{1,0:T(8,128)(2,1)}, u32[]{:S(2)}) copy-start(bf16[256,3456]{1,0:T(8,128)(2,1)} %wd_ref.1) | copy-start | bytes 5308420
  11.1 4.1 %copy-start.3 = (bf16[128,1728]{0,1:T(8,128)(2,1)S(1)}, bf16[128,1728]{0,1:T(8,128)(2,1)}, u32[]{:S(2)}) copy-start(bf16[128,1728]{0,1:T(8,128)(2,1)} %param.6) | copy-start | bytes 1327108
  15.2 1.0 %copy-start.5 = (bf16[64,16,256]{2,0,1:T(8,128)(2,1)S(1)}, bf16[64,16,256]{2,0,1:T(8,128)(2,1)}, u32[]{:S(2)}) copy-start(bf16[64,16,256]{2,0,1:T(8,128)(2,1)} %copy-done.4) | copy-start | bytes 1572868
  18.6 12.5 %collective-permute-start.4 = (bf16[2,4,128,256]{3,2,1,0:T(8,128)(2,1)S(1)}, bf16[2,4,128,256]{3,2,1,0:T(8,128)(2,1)S(1)}, u32[]{:S(2)}, u32[]{:S(2)}) collective-permute-start(bf16[2,4,128,256]{3,2,1,0:T(8,128)(2,1)S(1)} %get-tuple-element.28.refs_0_), channel_id=1, source_target_pairs={{0,8},{8,0},{1,9},{9,1},{2,10},{10,2},{3,11},{11,3},{4,12},{12,4},... | collective-permute-start | bytes 1572872 | tf_op jit(solution)/shard_map/ppermute | solution.py:277
  18.8 6.8 %collective-permute-start.2 = (bf16[2,128,256]{2,1,0:T(8,128)(2,1)S(1)}, bf16[2,128,256]{2,1,0:T(8,128)(2,1)S(1)}, u32[]{:S(2)}, u32[]{:S(2)}) collective-permute-start(bf16[2,128,256]{2,1,0:T(8,128)(2,1)S(1)} %get-tuple-element.29), channel_id=1, source_target_pairs={{0,1},{1,2},{2,3},{3,4},{4,5},{5,6},{6,7},{8,9},{9,10},{10,11},{11... | collective-permute-start | bytes 393224 | tf_op jit(solution)/shard_map/ppermute | solution.py:273
  22.2 7.6 %collective-permute-start.3 = (bf16[2,128,256]{2,1,0:T(8,128)(2,1)S(1)}, bf16[2,128,256]{2,1,0:T(8,128)(2,1)S(1)}, u32[]{:S(2)}, u32[]{:S(2)}) collective-permute-start(bf16[2,128,256]{2,1,0:T(8,128)(2,1)S(1)} %get-tuple-element.30), channel_id=1, source_target_pairs={{1,0},{2,1},{3,2},{4,3},{5,4},{6,5},{7,6},{9,8},{10,9},{11,10},{12... | collective-permute-start | bytes 393224 | tf_op jit(solution)/shard_map/ppermute | solution.py:273
  25.5 4.2 %collective-permute-start.5 = (bf16[2,128,256]{2,1,0:T(8,128)(2,1)S(1)}, bf16[2,128,256]{2,1,0:T(8,128)(2,1)S(1)}, u32[]{:S(2)}, u32[]{:S(2)}) collective-permute-start(bf16[2,128,256]{2,1,0:T(8,128)(2,1)S(1)} %collective-permute-done.2.refs_1_), channel_id=1, source_target_pairs={{0,8},{8,0},{1,9},{9,1},{2,10},{10,2},{3,11},{11,3},{4,12},{12,4},... | collective-permute-start | bytes 393224 | tf_op jit(solution)/shard_map/ppermute | solution.py:277
  29.8 1.3 %collective-permute-start.6 = (bf16[2,128,256]{2,1,0:T(8,128)(2,1)S(1)}, bf16[2,128,256]{2,1,0:T(8,128)(2,1)S(1)}, u32[]{:S(2)}, u32[]{:S(2)}) collective-permute-start(bf16[2,128,256]{2,1,0:T(8,128)(2,1)S(1)} %collective-permute-done.3.refs_2_), channel_id=1, source_target_pairs={{0,8},{8,0},{1,9},{9,1},{2,10},{10,2},{3,11},{11,3},{4,12},{12,4},... | collective-permute-start | bytes 393224 | tf_op jit(solution)/shard_map/ppermute | solution.py:277
  37.5 1.6 %collective-permute-start.7 = (bf16[8,16,1152]{2,1,0:T(8,128)(2,1)S(1)}, bf16[8,16,1152]{2,1,0:T(8,128)(2,1)S(1)}, u32[]{:S(2)}, u32[]{:S(2)}) collective-permute-start(bf16[8,16,1152]{2,1,0:T(8,128)(2,1)S(1)} %get-tuple-element.37), channel_id=1, source_target_pairs={{0,8},{8,0},{1,9},{9,1},{2,10},{10,2},{3,11},{11,3},{4,12},{12,4},... | collective-permute-start | bytes 884744 | tf_op jit(solution)/shard_map/ppermute | solution.py:277
  42.8 2.4 %collective-permute-start.8 = (bf16[2,6,128,256]{3,2,0,1:T(8,128)(2,1)S(1)}, bf16[2,6,128,256]{3,2,0,1:T(8,128)(2,1)S(1)}, u32[]{:S(2)}, u32[]{:S(2)}) collective-permute-start(bf16[2,6,128,256]{3,2,0,1:T(8,128)(2,1)S(1)} %copy.10), channel_id=1, source_target_pairs={{0,8},{8,0},{1,9},{9,1},{2,10},{10,2},{3,11},{11,3},{4,12},{12,4},... | collective-permute-start | bytes 2359304 | tf_op jit(solution)/shard_map/ppermute | solution.py:277
  45.3 8.3 %collective-permute-start.10 = (bf16[2,128,256]{2,1,0:T(8,128)(2,1)S(1)}, bf16[2,128,256]{2,1,0:T(8,128)(2,1)S(1)}, u32[]{:S(2)}, u32[]{:S(2)}) collective-permute-start(bf16[2,128,256]{2,1,0:T(8,128)(2,1)S(1)} %get-tuple-element.49), channel_id=1, source_target_pairs={{1,0},{2,1},{3,2},{4,3},{5,4},{6,5},{7,6},{9,8},{10,9},{11,10},{12... | collective-permute-start | bytes 393224 | tf_op jit(solution)/shard_map/ppermute | solution.py:273
  46.6 10.0 %collective-permute-start.9 = (bf16[2,128,256]{2,1,0:T(8,128)(2,1)S(1)}, bf16[2,128,256]{2,1,0:T(8,128)(2,1)S(1)}, u32[]{:S(2)}, u32[]{:S(2)}) collective-permute-start(bf16[2,128,256]{2,1,0:T(8,128)(2,1)S(1)} %get-tuple-element.50), channel_id=1, source_target_pairs={{0,1},{1,2},{2,3},{3,4},{4,5},{5,6},{6,7},{8,9},{9,10},{10,11},{11... | collective-permute-start | bytes 393224 | tf_op jit(solution)/shard_map/ppermute | solution.py:273
  58.8 1.6 %collective-permute-start.11 = (bf16[8,8,1728]{2,1,0:T(8,128)(2,1)S(1)}, bf16[8,8,1728]{2,1,0:T(8,128)(2,1)S(1)}, u32[]{:S(2)}, u32[]{:S(2)}) collective-permute-start(bf16[8,8,1728]{2,1,0:T(8,128)(2,1)S(1)} %get-tuple-element.47), channel_id=1, source_target_pairs={{0,8},{8,0},{1,9},{9,1},{2,10},{10,2},{3,11},{11,3},{4,12},{12,4},... | collective-permute-start | bytes 663560 | tf_op jit(solution)/shard_map/ppermute | solution.py:277
  75.0 25.5 %all-to-all-start.1 = ((bf16[8,48,1152]{2,1,0:T(8,128)(2,1)}), bf16[8,48,1152]{2,1,0:T(8,128)(2,1)S(1)}, u32[]{:S(2)}, u32[]{:S(2)}) async-start(bf16[8,48,1152]{2,1,0:T(8,128)(2,1)} %pad_maximum_fusion), calls=%async_computation.1 | async-start | bytes 1769472 | tf_op jit(solution)/shard_map/all_to_all | solution.py:363
  80.2 20.5 %collective-permute-start.12 = (f32[8,1728]{1,0:T(8,128)S(1)}, f32[8,1728]{1,0:T(8,128)S(1)}, u32[]{:S(2)}, u32[]{:S(2)}) collective-permute-start(f32[8,1728]{1,0:T(8,128)S(1)} %convert_reduce_fusion.1), channel_id=1, source_target_pairs={{0,8},{8,0},{1,9},{9,1},{2,10},{10,2},{3,11},{11,3},{4,12},{12,4},... | collective-permute-start | bytes 165896 | tf_op jit(solution)/shard_map/ppermute | solution.py:277
  100.6 1.5 %collective-permute-start.13 = (f32[48,1152]{1,0:T(8,128)S(1)}, f32[48,1152]{1,0:T(8,128)S(1)}, u32[]{:S(2)}, u32[]{:S(2)}) collective-permute-start(f32[48,1152]{1,0:T(8,128)S(1)} %convert_reduce_fusion), channel_id=1, source_target_pairs={{0,8},{8,0},{1,9},{9,1},{2,10},{10,2},{3,11},{11,3},{4,12},{12,4},... | collective-permute-start | bytes 663560 | tf_op jit(solution)/shard_map/ppermute | solution.py:277

commit v3 on v2

--- a/solution.py
+++ b/solution.py
@@ -11,7 +11,7 @@
 BF16 = jnp.bfloat16
 F32 = jnp.float32
 VMEM = pltpu.VMEM
-VMEM_LIMIT = 24 * 1024 * 1024
+VMEM_LIMIT = 20 * 1024 * 1024
 
 
 def vmem_call(body, out_shape, n_in, scratch=(), scalars=0):
@@ -190,7 +190,7 @@
             window = rs_ref[r, low : high + 1].reshape((high - low + 1) * block, lanes)
             weights = wg_ref[:, first * block : (first + high - low + 1) * block]
             grad = jnp.dot(weights, window, preferred_element_type=F32)
-            gother_ref[r, x] = grad[mid:].astype(BF16)
+            gother_ref[x, r] = grad[mid:].astype(BF16)
             if x == 0:
                 ghalo_ref[0, r] = grad[:mid]
             elif x == pairs + 1:
@@ -239,7 +239,7 @@
     total = None
     for i in range(orows):
         for m in range(pairs):
-            grad = gown_ref[i, m] + gx_ref[i, m + 1].astype(F32)
+            grad = gown_ref[i, m] + gx_ref[m + 1, i].astype(F32)
             if m == 0:
                 grad = grad + gl_ref[i].astype(F32)
             if m == pairs - 1:
@@ -248,7 +248,12 @@
             window = vp_ref[m, 2 * i * plane : (2 * i + 3) * plane, :]
             part = lax.dot_general(pg, window, NT, preferred_element_type=F32)
             total = part if total is None else total + part
-    split_rows(slab_ref, total, mine_ref, send_ref, slice(None))
+    width = mine_ref.shape[2]
+    pad = jnp.zeros((mid, 2 * width - total.shape[1]), F32)
+    low, high = total[:, :width], jnp.concatenate([total[:, width:], pad], axis=1)
+    first = slab_ref[0] == 0
+    mine_ref[...] = jnp.where(first, low, high).reshape(mine_ref.shape)
+    send_ref[...] = jnp.where(first, high, low).reshape(mine_ref.shape).astype(BF16)
 
 
 def prediction_body(pred_ref, out_ref, tall_ref):
@@ -285,6 +290,12 @@
     pairs, lanes = ocols // 2, 2 * half
     strips = lax.axis_size("strip")
     slab = lax.axis_index("slab")
+    strip = lax.axis_index("strip")
+    groups = strips // 2
+    place, parity = strip // 2, strip % 2
+    scalars = (slab == 0, slab, parity, 1 - parity, *((place + d) % groups for d in range(groups)))
+    target, scalars = lax.optimization_barrier((target, scalars))
+    first, slab, parity, other_parity, *places = scalars
     slab_id = slab.reshape(1).astype(jnp.int32)
     step = 2
     assert lax.axis_size("slab") == 2 and orows == step and ocols % 2 == 0
@@ -358,23 +369,41 @@
         2,
         scalars=1,
     )(slab_id, residual, hs)
+    def pick(array, index, dim):
+        return lax.dynamic_index_in_dim(array, index, dim, False, allow_negative_indices=False)
+
+    def pair_stage(grad):
+        chunks = grad.reshape(groups, 2, *grad.shape[1:])
+        got = lax.ppermute(
+            pick(chunks, other_parity, 1), "strip", [(i, i ^ 1) for i in range(strips)]
+        )
+        return pick(chunks, parity, 1).astype(F32) + got.astype(F32)
+
+    def far_stage(grad):
+        total = pick(grad, places[0], 0)
+        for d in range(1, groups):
+            sent = pick(grad, places[d], 0).astype(BF16)
+            got = lax.ppermute(sent, "strip", [(i, (i + 2 * d) % strips) for i in range(strips)])
+            total = total + got.astype(F32)
+        return total
+
     dg = jnp.concatenate([(mine + swap(send).astype(F32)).astype(BF16), apart], axis=1)
-    dg, residual = lax.optimization_barrier((dg, residual))
-    dg = lax.all_to_all(dg, "strip", 0, 0, tiled=True)
-
+    dg = pair_stage(dg)
+
+    residual, send = lax.optimization_barrier((residual, send))
     gown, ghalo, gother = vmem_call(
         hidden_grad_body,
         (
             sds((orows, pairs, mid, lanes), F32),
             sds((2, orows, mid, lanes), F32),
-            sds((orows, pairs + 2, mid, lanes), BF16),
+            sds((pairs + 2, orows, mid, lanes), BF16),
         ),
         2,
     )(residual, wg)
 
     gx = swap(gother)
-    to_left = (ghalo[0] + gx[:, 0].astype(F32)).astype(BF16)
-    to_right = (ghalo[1] + gx[:, -1].astype(F32)).astype(BF16)
+    to_left = (ghalo[0] + gx[0].astype(F32)).astype(BF16)
+    to_right = (ghalo[1] + gx[-1].astype(F32)).astype(BF16)
     grad_l = shift_along(to_right, "strip", 1)
     grad_r = shift_along(to_left, "strip", -1)
 
@@ -384,29 +413,24 @@
         1,
         [VMEM((2, outs * ocols, half), F32)],
     )(pred)
-    mid_rows = mid // strips // 2
+    mid_rows = mid // strips
+    width = 9 * mid
+    assert width < 27 * channels <= 2 * width
+    grad_l, grad_r, dg, prediction = lax.optimization_barrier((grad_l, grad_r, dg, prediction))
     smine, ssend = vmem_call(
         strided_grad_body,
-        (
-            sds((strips, mid_rows, 27 * channels), F32),
-            sds((strips, mid_rows, 27 * channels), BF16),
-        ),
+        (sds((strips, mid_rows, width), F32), sds((strips, mid_rows, width), BF16)),
         6,
         scalars=1,
     )(slab_id, gown, gx, grad_l, grad_r, slope, vp)
-    sg = (smine + swap(ssend).astype(F32)).astype(BF16)
-    sg = lax.all_to_all(sg, "strip", 0, 0, tiled=True)
-
-    sg = jnp.sum(sg.astype(F32), axis=0)
-    dg = jnp.sum(dg.astype(F32), axis=0)
-    dg_x, sg_x = swap(dg), swap(sg)
-    first = slab == 0
-    dg0, dg1 = jnp.where(first, dg, dg_x), jnp.where(first, dg_x, dg)
-    middle = jnp.concatenate([dg0[:half_rows], dg1[:half_rows]], axis=0)
-    dilated_grad = jnp.concatenate([dg1[half_rows:], middle, dg0[half_rows:]], axis=1)
-    strided_grad = jnp.concatenate(
-        [jnp.where(first, sg, sg_x), jnp.where(first, sg_x, sg)], axis=0
-    )
+    sg = pair_stage((smine + swap(ssend).astype(F32)).astype(BF16))
+    total = far_stage(jnp.concatenate([dg, sg], axis=1))
+    across = swap(total)
+    low, high = jnp.where(first, total, across), jnp.where(first, across, total)
+    middle = jnp.concatenate([low[:half_rows], high[:half_rows]], axis=0)
+    end = half_rows + rows
+    dilated_grad = jnp.concatenate([high[half_rows:end], middle, low[half_rows:end]], axis=1)
+    strided_grad = jnp.concatenate([low[end:], high[end:, : 27 * channels - width]], axis=1)
     return prediction, strided_grad, dilated_grad
 
 

time: 103 us -> 87.8 us (0.85); the launches traced: 103 us -> 86.6 us
  blocking collectives: 14.6 us -> 0 us
  waiting for transfers between devices: 39.4 us -> 31.5 us
  starting transfers between devices: 22.4 us -> 29.2 us
    all_to_all x1 -> x0, waiting for transfers between devices: 20.2 us -> none  [local(): dg = lax.all_to_all(dg, 'strip', 0, 0, tiled=True)]
    ppermute x0 -> x5, waiting for transfers between devices: none -> 18 us  [the longest x2 9.9 us: pair_stage(): lax.ppermute(pick(chunks, other_parity, 1), 'strip', [(i, i ^ 1) for i in...]
    all_to_all x1 -> x0, blocking collectives: 14.6 us -> none  [local(): sg = lax.all_to_all(sg, 'strip', 0, 0, tiled=True)]
    ppermute x0 -> x5, starting transfers between devices: none -> 10.8 us  [the longest x3 5.58 us: far_stage(): lax.ppermute(sent, 'strip', [(i, (i + 2 * d) % strips) for i in range(str...]
    all_to_all x1 -> x0, starting transfers between devices: 3.55 us -> none  [local(): dg = lax.all_to_all(dg, 'strip', 0, 0, tiled=True)]
    ppermute x6, waiting for transfers between devices: 12 us -> 9.08 us  [shift_along(): return lax.ppermute(value, axis, pairs)]
    ppermute x8 -> x7, waiting for transfers between devices: 7.17 us -> 4.49 us  [swap(): return lax.ppermute(value, 'slab', [(0, 1), (1, 0)])]
  transfers between devices with their start and end apart: 15 -> 18, of which waited for: 11 -> 11; matrix products, arithmetic and copies ran while one was open for 1% -> 1% of each run, Pallas kernels for 6% -> 10%
where the time goes in v3:
time: 87.8 us; the launch traced here: 86.6 us
  waiting for transfers between devices  31.5 us (36%)
  starting transfers between devices  29.2 us (33%)
  Pallas kernels  19.4 us (22%)
  local copies, waits for them, and re-layouts  3.44 us (4%)
  other arithmetic  2.01 us (2%)
  between operations  1.06 us (1%)
    ppermute x6, starting transfers between devices, shift_along(): return lax.ppermute(value, axis, pairs)  17.4 us
    ppermute x2, waiting for transfers between devices, pair_stage(): lax.ppermute(pick(chunks, other_parity, 1), 'strip', [(i, i ^ 1) for i in...  9.9 us
    ppermute x6, waiting for transfers between devices, shift_along(): return lax.ppermute(value, axis, pairs)  9.08 us
    ppermute x3, waiting for transfers between devices, far_stage(): lax.ppermute(sent, 'strip', [(i, (i + 2 * d) % strips) for i in range(str...  8.07 us
    ppermute x3, starting transfers between devices, far_stage(): lax.ppermute(sent, 'strip', [(i, (i + 2 * d) % strips) for i in range(str...  5.58 us
    ppermute x2, starting transfers between devices, pair_stage(): lax.ppermute(pick(chunks, other_parity, 1), 'strip', [(i, i ^ 1) for i in...  5.24 us
    ppermute x7, waiting for transfers between devices, swap(): return lax.ppermute(value, 'slab', [(0, 1), (1, 0)])  4.49 us
    pallas_call x1, Pallas kernels, local(): vmem_call(split_body, (sds((pairs, (rows_in + 1) * 9 * channels, lanes),...  4.08 us
  transfers between devices with their start and end apart: 18, of which 11 were waited for; matrix products, arithmetic and copies ran while one was open for 1% of the time, Pallas kernels for 10%

profile of v3, /device:TPU:0, one launch (start us, length us, event | category | flops | bytes accessed | tf_op | source)
XLA Modules:
  0.0 86.6 jit_solution(2438439260333252501)
XLA Ops:
  0.6 1.2 %slice.39 = bf16[64,1,16,256]{3,2,1,0:T(8,128)(2,1)S(1)} slice(bf16[64,4,16,256]{3,2,1,0:T(8,128)(2,1)} %vol_ref.1), slice={[0:64], [3:4], [0:16], [0:256]} | slice | bytes 1048576 | tf_op jit(solution)/shard_map/slice | solution.py:305
  1.9 0.2 copy.18
  2.1 2.4 %collective-permute-start = (bf16[64,16,256]{2,0,1:T(8,128)(2,1)S(1)}, bf16[64,16,256]{2,0,1:T(8,128)(2,1)S(1)}, u32[]{:S(2)}, u32[]{:S(2)}) collective-permute-start(bf16[64,16,256]{2,0,1:T(8,128)(2,1)S(1)} %bitcast.52), channel_id=1, source_target_pairs={{0,8},{1,9},{2,10},{3,11},{4,12},{5,13},{6,14},{7,15},{16,24},{17,... | collective-permute-start | bytes 1572872 | tf_op jit(solution)/shard_map/ppermute | solution.py:278
  4.5 0.0 copy-done
  4.5 0.3 slice.41
  4.8 1.1 %collective-permute-done = bf16[64,16,256]{2,0,1:T(8,128)(2,1)S(1)} collective-permute-done((bf16[64,16,256]{2,0,1:T(8,128)(2,1)S(1)}, bf16[64,16,256]{2,0,1:T(8,128)(2,1)S(1)}, u32[]{:S(2)}, u32[]{:S(2)}) %collective-permute-start) | collective-permute-done | bytes 524320 | tf_op jit(solution)/shard_map/ppermute | solution.py:278
  5.9 0.8 copy-done.4
  6.8 4.3 %collective-permute-start.1 = (bf16[5,64,256]{2,1,0:T(8,128)(2,1)S(1)}, bf16[5,64,256]{2,1,0:T(8,128)(2,1)S(1)}, u32[]{:S(2)}, u32[]{:S(2)}) collective-permute-start(bf16[5,64,256]{2,1,0:T(8,128)(2,1)S(1)} %pad_maximum_fusion.2), channel_id=1, source_target_pairs={{0,1},{1,2},{2,3},{3,4},{4,5},{5,6},{6,7},{8,9},{9,10},{10,11},{11... | collective-permute-start | bytes 491528 | tf_op jit(solution)/shard_map/ppermute | solution.py:278
  11.1 0.0 copy-done.2
  11.1 0.0 copy-start.1
  11.1 0.0 copy-start.3
  11.2 4.1 %shard_map.67 = (bf16[4,2880,256]{2,1,0:T(8,128)(2,1)S(1)}, bf16[2,4,256,256]{3,2,1,0:T(8,128)(2,1)S(1)}) custom-call(bf16[64,4,16,256]{3,2,1,0:T(8,128)(2,1)S(1)} %copy-done, bf16[256,2,8,128]{3,2,1,0:T(8,128)(2,1)S(1)} %copy-done.2), custom_call_target="tpu_custom_call" | custom-call | tf_op jit(solution)/shard_map/pallas_call | solution.py:319
  15.2 0.0 copy-start.5
  15.3 0.5 shard_map.68
  15.8 0.5 copy-done.5
  16.3 0.3 copy.9.hrow_ref
  16.6 0.0 collective-permute-done.1.hcol_ref
  16.6 2.1 %shard_map.69 = (bf16[4,2880,256]{2,1,0:T(8,128)(2,1)S(1)}, bf16[2,4,128,256]{3,2,1,0:T(8,128)(2,1)S(1)}, bf16[2,128,256]{2,1,0:T(8,128)(2,1)S(1)}, bf16[2,128,2...) custom-call(bf16[4,2880,256]{2,1,0:T(8,128)(2,1)S(1)} %get-tuple-element.39.own_ref, bf16[64,16,256]{2,1,0:T(8,128)(2,1)S(1)} %copy.9.hrow_ref, ...), custom_call_target="tpu_custom_call" | custom-call | tf_op jit(solution)/shard_map/pallas_call | solution.py:328
  18.7 0.1 collective-permute-start.4
  18.9 3.4 %collective-permute-start.2 = (bf16[2,128,256]{2,1,0:T(8,128)(2,1)S(1)}, bf16[2,128,256]{2,1,0:T(8,128)(2,1)S(1)}, u32[]{:S(2)}, u32[]{:S(2)}) collective-permute-start(bf16[2,128,256]{2,1,0:T(8,128)(2,1)S(1)} %get-tuple-element.43), channel_id=1, source_target_pairs={{0,1},{1,2},{2,3},{3,4},{4,5},{5,6},{6,7},{8,9},{9,10},{10,11},{11... | collective-permute-start | bytes 393224 | tf_op jit(solution)/shard_map/ppermute | solution.py:278
  22.3 1.5 %collective-permute-start.3 = (bf16[2,128,256]{2,1,0:T(8,128)(2,1)S(1)}, bf16[2,128,256]{2,1,0:T(8,128)(2,1)S(1)}, u32[]{:S(2)}, u32[]{:S(2)}) collective-permute-start(bf16[2,128,256]{2,1,0:T(8,128)(2,1)S(1)} %get-tuple-element.44), channel_id=1, source_target_pairs={{1,0},{2,1},{3,2},{4,3},{5,4},{6,5},{7,6},{9,8},{10,9},{11,10},{12... | collective-permute-start | bytes 393224 | tf_op jit(solution)/shard_map/ppermute | solution.py:278
  23.7 1.9 %collective-permute-done.2.refs_1_ = bf16[2,128,256]{2,1,0:T(8,128)(2,1)S(1)} collective-permute-done((bf16[2,128,256]{2,1,0:T(8,128)(2,1)S(1)}, bf16[2,128,256]{2,1,0:T(8,128)(2,1)S(1)}, u32[]{:S(2)}, u32[]{:S(2)}) %collective-permute-start.2) | collective-permute-done | bytes 131104 | tf_op jit(solution)/shard_map/ppermute | solution.py:278
  25.6 0.0 collective-permute-start.5
  25.6 4.2 %collective-permute-done.3.refs_2_ = bf16[2,128,256]{2,1,0:T(8,128)(2,1)S(1)} collective-permute-done((bf16[2,128,256]{2,1,0:T(8,128)(2,1)S(1)}, bf16[2,128,256]{2,1,0:T(8,128)(2,1)S(1)}, u32[]{:S(2)}, u32[]{:S(2)}) %collective-permute-start.3) | collective-permute-done | bytes 131104 | tf_op jit(solution)/shard_map/ppermute | solution.py:278
  29.8 0.0 collective-permute-start.6
  29.8 0.0 collective-permute-done.5.refs_4_
  29.8 1.3 %collective-permute-done.6.refs_5_ = bf16[2,128,256]{2,1,0:T(8,128)(2,1)S(1)} collective-permute-done((bf16[2,128,256]{2,1,0:T(8,128)(2,1)S(1)}, bf16[2,128,256]{2,1,0:T(8,128)(2,1)S(1)}, u32[]{:S(2)}, u32[]{:S(2)}) %collective-permute-start.6) | collective-permute-done | bytes 131104 | tf_op jit(solution)/shard_map/ppermute | solution.py:282
  31.1 0.0 collective-permute-done.4.refs_3_
  31.1 2.9 %shard_map.70 = (bf16[2,6,768,256]{3,2,1,0:T(8,128)(2,1)S(1)}, bf16[2,4,256,256]{3,2,1,0:T(8,128)(2,1)S(1)}, bf16[2,4,768,256]{3,2,1,0:T(8,128)(2,1)S(1)}) custom-call(bf16[2,4,128,256]{3,2,1,0:T(8,128)(2,1)S(1)} %get-tuple-element.42.refs_0_, bf16[2,128,256]{2,1,0:T(8,128)(2,1)S(1)} %collective-permute-done.2.refs_1_, ...), custom_call_target="tpu_custom_call" | custom-call | tf_op jit(solution)/shard_map/pallas_call | solution.py:350
  34.1 3.4 %shard_map.71 = (f32[8,16,1152]{2,1,0:T(8,128)S(1)}, bf16[8,16,1152]{2,1,0:T(8,128)(2,1)S(1)}, bf16[8,32,1152]{2,1,0:T(8,128)(2,1)S(1)}) custom-call(s32[1]{0:T(128)} %bitcast.4.slab_ref, bf16[2,4,768,256]{3,2,1,0:T(8,128)(2,1)S(1)} %get-tuple-element.50.rs_ref, bf16[2,6,768,256]{3,2,1,0:T(8,128)(2,1)S(1)} %get-tuple-element.48.hs_ref), custom_call_target="tpu_custom_call" | custom-call | tf_op jit(solution)/shard_map/pallas_call | solution.py:362
  37.5 0.2 collective-permute-start.10
  37.7 2.6 %shard_map.72 = (f32[2,4,128,256]{3,2,1,0:T(8,128)S(1)}, f32[2,2,128,256]{3,2,1,0:T(8,128)S(1)}, bf16[6,2,128,256]{3,2,1,0:T(8,128)(2,1)S(1)}) custom-call(bf16[2,4,768,256]{3,2,1,0:T(8,128)(2,1)S(1)} %get-tuple-element.50.rs_ref, bf16[256,2304]{1,0:T(8,128)(2,1)S(1)} %get-tuple-element.51.wg_ref), custom_call_target="tpu_custom_call" | custom-call | tf_op jit(solution)/shard_map/pallas_call | solution.py:394
  40.3 0.4 collective-permute-start.7
  40.7 0.0 collective-permute-done.10
  40.7 0.1 add_convert_fusion.1
  40.8 0.1 pad_maximum_fusion
  40.9 2.7 %collective-permute-start.11 = (bf16[4,48,1152]{2,1,0:T(8,128)(2,1)S(1)}, bf16[4,48,1152]{2,1,0:T(8,128)(2,1)S(1)}, u32[]{:S(2)}, u32[]{:S(2)}) collective-permute-start(bf16[4,48,1152]{2,1,0:T(8,128)(2,1)S(1)} %dynamic-slice_bitcast_fusion), channel_id=1, source_target_pairs={{0,1},{1,0},{2,3},{3,2},{4,5},{5,4},{6,7},{7,6},{8,9},{9,8},{10,11... | collective-permute-start | bytes 1327112 | tf_op jit(solution)/shard_map/ppermute | solution.py:377
  43.6 1.6 %shard_map.73 = bf16[256,2,8,128]{3,2,1,0:T(8,128)(2,1)} custom-call(bf16[2,4,256,256]{3,2,1,0:T(8,128)(2,1)S(1)} %get-tuple-element.58.pred_ref), custom_call_target="tpu_custom_call" | custom-call | tf_op jit(solution)/shard_map/pallas_call | solution.py:410
  45.3 0.0 collective-permute-done.7.gx_ref
  45.3 0.1 fusion.15
  45.3 1.3 %collective-permute-start.9 = (bf16[2,128,256]{2,1,0:T(8,128)(2,1)S(1)}, bf16[2,128,256]{2,1,0:T(8,128)(2,1)S(1)}, u32[]{:S(2)}, u32[]{:S(2)}) collective-permute-start(bf16[2,128,256]{2,1,0:T(8,128)(2,1)S(1)} %get-tuple-element.73), channel_id=1, source_target_pairs={{1,0},{2,1},{3,2},{4,3},{5,4},{6,5},{7,6},{9,8},{10,9},{11,10},{12... | collective-permute-start | bytes 393224 | tf_op jit(solution)/shard_map/ppermute | solution.py:278
  46.6 4.6 %collective-permute-start.8 = (bf16[2,128,256]{2,1,0:T(8,128)(2,1)S(1)}, bf16[2,128,256]{2,1,0:T(8,128)(2,1)S(1)}, u32[]{:S(2)}, u32[]{:S(2)}) collective-permute-start(bf16[2,128,256]{2,1,0:T(8,128)(2,1)S(1)} %get-tuple-element.74), channel_id=1, source_target_pairs={{0,1},{1,2},{2,3},{3,4},{4,5},{5,6},{6,7},{8,9},{9,10},{10,11},{11... | collective-permute-start | bytes 393224 | tf_op jit(solution)/shard_map/ppermute | solution.py:278
  51.2 5.8 %collective-permute-done.11 = bf16[4,48,1152]{2,1,0:T(8,128)(2,1)S(1)} collective-permute-done((bf16[4,48,1152]{2,1,0:T(8,128)(2,1)S(1)}, bf16[4,48,1152]{2,1,0:T(8,128)(2,1)S(1)}, u32[]{:S(2)}, u32[]{:S(2)}) %collective-permute-start.11) | collective-permute-done | bytes 442400 | tf_op jit(solution)/shard_map/ppermute | solution.py:377
  57.0 0.1 convert_add_fusion
  57.0 0.0 collective-permute-done.9.gr_ref
  57.1 1.9 %collective-permute-done.8.gl_ref = bf16[2,128,256]{2,1,0:T(8,128)(2,1)S(1)} collective-permute-done((bf16[2,128,256]{2,1,0:T(8,128)(2,1)S(1)}, bf16[2,128,256]{2,1,0:T(8,128)(2,1)S(1)}, u32[]{:S(2)}, u32[]{:S(2)}) %collective-permute-start.8) | collective-permute-done | bytes 131104 | tf_op jit(solution)/shard_map/ppermute | solution.py:278
  59.0 2.2 %shard_map.74 = (f32[8,16,1152]{2,1,0:T(8,128)S(1)}, bf16[8,16,1152]{2,1,0:T(8,128)(2,1)S(1)}) custom-call(s32[1]{0:T(128)} %bitcast.4.slab_ref, f32[2,4,128,256]{3,2,1,0:T(8,128)S(1)} %get-tuple-element.62.gown_ref, bf16[6,2,128,256]{3,2,1,0:T(8,128)(2,1)S(1)} %collective-permute-done.7.gx_ref, bf16[2,128,256]{2,1,0:T(8,128)(2,1)S(1)} %collective-permute-done.8.gl_ref, ...), custom_call_target="tpu_custom_call" | custom-call | tf_op jit(solution)/shard_map/pallas_call | solution.py:420
  61.1 0.1 collective-permute-start.12
  61.2 1.6 %collective-permute-done.12 = bf16[8,16,1152]{2,1,0:T(8,128)(2,1)S(1)} collective-permute-done((bf16[8,16,1152]{2,1,0:T(8,128)(2,1)S(1)}, bf16[8,16,1152]{2,1,0:T(8,128)(2,1)S(1)}, u32[]{:S(2)}, u32[]{:S(2)}) %collective-permute-start.12) | collective-permute-done | bytes 294944 | tf_op jit(solution)/shard_map/ppermute | solution.py:282
  62.8 0.1 add_convert_fusion
  62.9 2.5 %collective-permute-start.13 = (bf16[4,16,1152]{2,1,0:T(8,128)(2,1)S(1)}, bf16[4,16,1152]{2,1,0:T(8,128)(2,1)S(1)}, u32[]{:S(2)}, u32[]{:S(2)}) collective-permute-start(bf16[4,16,1152]{2,1,0:T(8,128)(2,1)S(1)} %dynamic-slice_bitcast_fusion.1), channel_id=1, source_target_pairs={{0,1},{1,0},{2,3},{3,2},{4,5},{5,4},{6,7},{7,6},{8,9},{9,8},{10,11... | collective-permute-start | bytes 442376 | tf_op jit(solution)/shard_map/ppermute | solution.py:377
  65.4 4.1 %collective-permute-done.13 = bf16[4,16,1152]{2,1,0:T(8,128)(2,1)S(1)} collective-permute-done((bf16[4,16,1152]{2,1,0:T(8,128)(2,1)S(1)}, bf16[4,16,1152]{2,1,0:T(8,128)(2,1)S(1)}, u32[]{:S(2)}, u32[]{:S(2)}) %collective-permute-start.13) | collective-permute-done | bytes 147488 | tf_op jit(solution)/shard_map/ppermute | solution.py:377
  69.6 0.1 fusion.12
  69.7 1.6 %collective-permute-start.14 = (bf16[64,1152]{1,0:T(8,128)(2,1)S(1)}, bf16[64,1152]{1,0:T(8,128)(2,1)S(1)}, u32[]{:S(2)}, u32[]{:S(2)}) collective-permute-start(bf16[64,1152]{1,0:T(8,128)(2,1)S(1)} %get-tuple-element.75), channel_id=1, source_target_pairs={{0,2},{1,3},{2,4},{3,5},{4,6},{5,7},{6,0},{7,1},{8,10},{9,11},{10,... | collective-permute-start | bytes 442376 | tf_op jit(solution)/shard_map/ppermute | solution.py:386
  71.3 2.5 %collective-permute-start.15 = (bf16[64,1152]{1,0:T(8,128)(2,1)S(1)}, bf16[64,1152]{1,0:T(8,128)(2,1)S(1)}, u32[]{:S(2)}, u32[]{:S(2)}) collective-permute-start(bf16[64,1152]{1,0:T(8,128)(2,1)S(1)} %get-tuple-element.76), channel_id=1, source_target_pairs={{0,4},{1,5},{2,6},{3,7},{4,0},{5,1},{6,2},{7,3},{8,12},{9,13},{10,... | collective-permute-start | bytes 442376 | tf_op jit(solution)/shard_map/ppermute | solution.py:386
  73.8 1.5 %collective-permute-start.16 = (bf16[64,1152]{1,0:T(8,128)(2,1)S(1)}, bf16[64,1152]{1,0:T(8,128)(2,1)S(1)}, u32[]{:S(2)}, u32[]{:S(2)}) collective-permute-start(bf16[64,1152]{1,0:T(8,128)(2,1)S(1)} %get-tuple-element.77), channel_id=1, source_target_pairs={{0,6},{1,7},{2,0},{3,1},{4,2},{5,3},{6,4},{7,5},{8,14},{9,15},{10,... | collective-permute-start | bytes 442376 | tf_op jit(solution)/shard_map/ppermute | solution.py:386
  75.3 3.1 %collective-permute-done.14 = bf16[64,1152]{1,0:T(8,128)(2,1)S(1)} collective-permute-done((bf16[64,1152]{1,0:T(8,128)(2,1)S(1)}, bf16[64,1152]{1,0:T(8,128)(2,1)S(1)}, u32[]{:S(2)}, u32[]{:S(2)}) %collective-permute-start.14) | collective-permute-done | bytes 147488 | tf_op jit(solution)/shard_map/ppermute | solution.py:386
  78.4 4.9 %collective-permute-done.15 = bf16[64,1152]{1,0:T(8,128)(2,1)S(1)} collective-permute-done((bf16[64,1152]{1,0:T(8,128)(2,1)S(1)}, bf16[64,1152]{1,0:T(8,128)(2,1)S(1)}, u32[]{:S(2)}, u32[]{:S(2)}) %collective-permute-start.15) | collective-permute-done | bytes 147488 | tf_op jit(solution)/shard_map/ppermute | solution.py:386
  83.3 0.0 collective-permute-done.16
  83.3 0.1 fusion.6
  83.4 0.1 collective-permute-start.17
  83.5 1.6 %collective-permute-done.17 = f32[64,1152]{1,0:T(8,128)S(1)} collective-permute-done((f32[64,1152]{1,0:T(8,128)S(1)}, f32[64,1152]{1,0:T(8,128)S(1)}, u32[]{:S(2)}, u32[]{:S(2)}) %collective-permute-start.17) | collective-permute-done | bytes 294944 | tf_op jit(solution)/shard_map/ppermute | solution.py:282
  85.2 0.7 pad_maximum_fusion.3
  85.8 0.8 pad_maximum_fusion.1
  (17 shorter events, 0.3 us)
Async XLA Ops:
  0.6 3.8 %copy-start = (bf16[64,4,16,256]{3,2,1,0:T(8,128)(2,1)S(1)}, bf16[64,4,16,256]{3,2,1,0:T(8,128)(2,1)}, u32[]{:S(2)}) copy-start(bf16[64,4,16,256]{3,2,1,0:T(8,128)(2,1)} %vol_ref.1) | copy-start | bytes 6291460
  0.6 10.5 %copy-start.2 = (bf16[256,2,8,128]{3,2,1,0:T(8,128)(2,1)S(1)}, bf16[256,2,8,128]{3,2,1,0:T(8,128)(2,1)}, u32[]{:S(2)}) copy-start(bf16[256,2,8,128]{3,2,1,0:T(8,128)(2,1)} %tgt_ref) | copy-start | bytes 3145732
  2.1 3.9 %collective-permute-start = (bf16[64,16,256]{2,0,1:T(8,128)(2,1)S(1)}, bf16[64,16,256]{2,0,1:T(8,128)(2,1)S(1)}, u32[]{:S(2)}, u32[]{:S(2)}) collective-permute-start(bf16[64,16,256]{2,0,1:T(8,128)(2,1)S(1)} %bitcast.52), channel_id=1, source_target_pairs={{0,8},{1,9},{2,10},{3,11},{4,12},{5,13},{6,14},{7,15},{16,24},{17,... | collective-permute-start | bytes 1572872 | tf_op jit(solution)/shard_map/ppermute | solution.py:278
  5.9 0.8 copy-start.4
  6.8 9.8 %collective-permute-start.1 = (bf16[5,64,256]{2,1,0:T(8,128)(2,1)S(1)}, bf16[5,64,256]{2,1,0:T(8,128)(2,1)S(1)}, u32[]{:S(2)}, u32[]{:S(2)}) collective-permute-start(bf16[5,64,256]{2,1,0:T(8,128)(2,1)S(1)} %pad_maximum_fusion.2), channel_id=1, source_target_pairs={{0,1},{1,2},{2,3},{3,4},{4,5},{5,6},{6,7},{8,9},{9,10},{10,11},{11... | collective-permute-start | bytes 491528 | tf_op jit(solution)/shard_map/ppermute | solution.py:278
  11.1 4.1 %copy-start.1 = (bf16[256,3456]{1,0:T(8,128)(2,1)S(1)}, bf16[256,3456]{1,0:T(8,128)(2,1)}, u32[]{:S(2)}) copy-start(bf16[256,3456]{1,0:T(8,128)(2,1)} %wd_ref.1) | copy-start | bytes 5308420
  11.1 4.1 %copy-start.3 = (bf16[128,1728]{0,1:T(8,128)(2,1)S(1)}, bf16[128,1728]{0,1:T(8,128)(2,1)}, u32[]{:S(2)}) copy-start(bf16[128,1728]{0,1:T(8,128)(2,1)} %param.6) | copy-start | bytes 1327108
  15.2 1.0 %copy-start.5 = (bf16[64,16,256]{2,0,1:T(8,128)(2,1)S(1)}, bf16[64,16,256]{2,0,1:T(8,128)(2,1)}, u32[]{:S(2)}) copy-start(bf16[64,16,256]{2,0,1:T(8,128)(2,1)} %copy-done.4) | copy-start | bytes 1572868
  18.7 12.4 %collective-permute-start.4 = (bf16[2,4,128,256]{3,2,1,0:T(8,128)(2,1)S(1)}, bf16[2,4,128,256]{3,2,1,0:T(8,128)(2,1)S(1)}, u32[]{:S(2)}, u32[]{:S(2)}) collective-permute-start(bf16[2,4,128,256]{3,2,1,0:T(8,128)(2,1)S(1)} %get-tuple-element.42.refs_0_), channel_id=1, source_target_pairs={{0,8},{8,0},{1,9},{9,1},{2,10},{10,2},{3,11},{11,3},{4,12},{12,4},... | collective-permute-start | bytes 1572872 | tf_op jit(solution)/shard_map/ppermute | solution.py:282
  18.9 6.8 %collective-permute-start.2 = (bf16[2,128,256]{2,1,0:T(8,128)(2,1)S(1)}, bf16[2,128,256]{2,1,0:T(8,128)(2,1)S(1)}, u32[]{:S(2)}, u32[]{:S(2)}) collective-permute-start(bf16[2,128,256]{2,1,0:T(8,128)(2,1)S(1)} %get-tuple-element.43), channel_id=1, source_target_pairs={{0,1},{1,2},{2,3},{3,4},{4,5},{5,6},{6,7},{8,9},{9,10},{10,11},{11... | collective-permute-start | bytes 393224 | tf_op jit(solution)/shard_map/ppermute | solution.py:278
  22.3 7.5 %collective-permute-start.3 = (bf16[2,128,256]{2,1,0:T(8,128)(2,1)S(1)}, bf16[2,128,256]{2,1,0:T(8,128)(2,1)S(1)}, u32[]{:S(2)}, u32[]{:S(2)}) collective-permute-start(bf16[2,128,256]{2,1,0:T(8,128)(2,1)S(1)} %get-tuple-element.44), channel_id=1, source_target_pairs={{1,0},{2,1},{3,2},{4,3},{5,4},{6,5},{7,6},{9,8},{10,9},{11,10},{12... | collective-permute-start | bytes 393224 | tf_op jit(solution)/shard_map/ppermute | solution.py:278
  25.6 4.2 %collective-permute-start.5 = (bf16[2,128,256]{2,1,0:T(8,128)(2,1)S(1)}, bf16[2,128,256]{2,1,0:T(8,128)(2,1)S(1)}, u32[]{:S(2)}, u32[]{:S(2)}) collective-permute-start(bf16[2,128,256]{2,1,0:T(8,128)(2,1)S(1)} %collective-permute-done.2.refs_1_), channel_id=1, source_target_pairs={{0,8},{8,0},{1,9},{9,1},{2,10},{10,2},{3,11},{11,3},{4,12},{12,4},... | collective-permute-start | bytes 393224 | tf_op jit(solution)/shard_map/ppermute | solution.py:282
  29.8 1.3 %collective-permute-start.6 = (bf16[2,128,256]{2,1,0:T(8,128)(2,1)S(1)}, bf16[2,128,256]{2,1,0:T(8,128)(2,1)S(1)}, u32[]{:S(2)}, u32[]{:S(2)}) collective-permute-start(bf16[2,128,256]{2,1,0:T(8,128)(2,1)S(1)} %collective-permute-done.3.refs_2_), channel_id=1, source_target_pairs={{0,8},{8,0},{1,9},{9,1},{2,10},{10,2},{3,11},{11,3},{4,12},{12,4},... | collective-permute-start | bytes 393224 | tf_op jit(solution)/shard_map/ppermute | solution.py:282
  37.5 3.3 %collective-permute-start.10 = (bf16[8,16,1152]{2,1,0:T(8,128)(2,1)S(1)}, bf16[8,16,1152]{2,1,0:T(8,128)(2,1)S(1)}, u32[]{:S(2)}, u32[]{:S(2)}) collective-permute-start(bf16[8,16,1152]{2,1,0:T(8,128)(2,1)S(1)} %get-tuple-element.49), channel_id=1, source_target_pairs={{0,8},{8,0},{1,9},{9,1},{2,10},{10,2},{3,11},{11,3},{4,12},{12,4},... | collective-permute-start | bytes 884744 | tf_op jit(solution)/shard_map/ppermute | solution.py:282
  40.3 5.0 %collective-permute-start.7 = (bf16[6,2,128,256]{3,2,1,0:T(8,128)(2,1)S(1)}, bf16[6,2,128,256]{3,2,1,0:T(8,128)(2,1)S(1)}, u32[]{:S(2)}, u32[]{:S(2)}) collective-permute-start(bf16[6,2,128,256]{3,2,1,0:T(8,128)(2,1)S(1)} %get-tuple-element.53), channel_id=1, source_target_pairs={{0,8},{8,0},{1,9},{9,1},{2,10},{10,2},{3,11},{11,3},{4,12},{12,4},... | collective-permute-start | bytes 2359304 | tf_op jit(solution)/shard_map/ppermute | solution.py:282
  40.9 16.0 %collective-permute-start.11 = (bf16[4,48,1152]{2,1,0:T(8,128)(2,1)S(1)}, bf16[4,48,1152]{2,1,0:T(8,128)(2,1)S(1)}, u32[]{:S(2)}, u32[]{:S(2)}) collective-permute-start(bf16[4,48,1152]{2,1,0:T(8,128)(2,1)S(1)} %dynamic-slice_bitcast_fusion), channel_id=1, source_target_pairs={{0,1},{1,0},{2,3},{3,2},{4,5},{5,4},{6,7},{7,6},{8,9},{9,8},{10,11... | collective-permute-start | bytes 1327112 | tf_op jit(solution)/shard_map/ppermute | solution.py:377
  45.3 11.7 %collective-permute-start.9 = (bf16[2,128,256]{2,1,0:T(8,128)(2,1)S(1)}, bf16[2,128,256]{2,1,0:T(8,128)(2,1)S(1)}, u32[]{:S(2)}, u32[]{:S(2)}) collective-permute-start(bf16[2,128,256]{2,1,0:T(8,128)(2,1)S(1)} %get-tuple-element.73), channel_id=1, source_target_pairs={{1,0},{2,1},{3,2},{4,3},{5,4},{6,5},{7,6},{9,8},{10,9},{11,10},{12... | collective-permute-start | bytes 393224 | tf_op jit(solution)/shard_map/ppermute | solution.py:278
  46.6 12.3 %collective-permute-start.8 = (bf16[2,128,256]{2,1,0:T(8,128)(2,1)S(1)}, bf16[2,128,256]{2,1,0:T(8,128)(2,1)S(1)}, u32[]{:S(2)}, u32[]{:S(2)}) collective-permute-start(bf16[2,128,256]{2,1,0:T(8,128)(2,1)S(1)} %get-tuple-element.74), channel_id=1, source_target_pairs={{0,1},{1,2},{2,3},{3,4},{4,5},{5,6},{6,7},{8,9},{9,10},{10,11},{11... | collective-permute-start | bytes 393224 | tf_op jit(solution)/shard_map/ppermute | solution.py:278
  61.1 1.6 %collective-permute-start.12 = (bf16[8,16,1152]{2,1,0:T(8,128)(2,1)S(1)}, bf16[8,16,1152]{2,1,0:T(8,128)(2,1)S(1)}, u32[]{:S(2)}, u32[]{:S(2)}) collective-permute-start(bf16[8,16,1152]{2,1,0:T(8,128)(2,1)S(1)} %get-tuple-element.68), channel_id=1, source_target_pairs={{0,8},{8,0},{1,9},{9,1},{2,10},{10,2},{3,11},{11,3},{4,12},{12,4},... | collective-permute-start | bytes 884744 | tf_op jit(solution)/shard_map/ppermute | solution.py:282
  62.9 6.7 %collective-permute-start.13 = (bf16[4,16,1152]{2,1,0:T(8,128)(2,1)S(1)}, bf16[4,16,1152]{2,1,0:T(8,128)(2,1)S(1)}, u32[]{:S(2)}, u32[]{:S(2)}) collective-permute-start(bf16[4,16,1152]{2,1,0:T(8,128)(2,1)S(1)} %dynamic-slice_bitcast_fusion.1), channel_id=1, source_target_pairs={{0,1},{1,0},{2,3},{3,2},{4,5},{5,4},{6,7},{7,6},{8,9},{9,8},{10,11... | collective-permute-start | bytes 442376 | tf_op jit(solution)/shard_map/ppermute | solution.py:377
  69.7 8.7 %collective-permute-start.14 = (bf16[64,1152]{1,0:T(8,128)(2,1)S(1)}, bf16[64,1152]{1,0:T(8,128)(2,1)S(1)}, u32[]{:S(2)}, u32[]{:S(2)}) collective-permute-start(bf16[64,1152]{1,0:T(8,128)(2,1)S(1)} %get-tuple-element.75), channel_id=1, source_target_pairs={{0,2},{1,3},{2,4},{3,5},{4,6},{5,7},{6,0},{7,1},{8,10},{9,11},{10,... | collective-permute-start | bytes 442376 | tf_op jit(solution)/shard_map/ppermute | solution.py:386
  71.3 12.0 %collective-permute-start.15 = (bf16[64,1152]{1,0:T(8,128)(2,1)S(1)}, bf16[64,1152]{1,0:T(8,128)(2,1)S(1)}, u32[]{:S(2)}, u32[]{:S(2)}) collective-permute-start(bf16[64,1152]{1,0:T(8,128)(2,1)S(1)} %get-tuple-element.76), channel_id=1, source_target_pairs={{0,4},{1,5},{2,6},{3,7},{4,0},{5,1},{6,2},{7,3},{8,12},{9,13},{10,... | collective-permute-start | bytes 442376 | tf_op jit(solution)/shard_map/ppermute | solution.py:386
  73.8 9.5 %collective-permute-start.16 = (bf16[64,1152]{1,0:T(8,128)(2,1)S(1)}, bf16[64,1152]{1,0:T(8,128)(2,1)S(1)}, u32[]{:S(2)}, u32[]{:S(2)}) collective-permute-start(bf16[64,1152]{1,0:T(8,128)(2,1)S(1)} %get-tuple-element.77), channel_id=1, source_target_pairs={{0,6},{1,7},{2,0},{3,1},{4,2},{5,3},{6,4},{7,5},{8,14},{9,15},{10,... | collective-permute-start | bytes 442376 | tf_op jit(solution)/shard_map/ppermute | solution.py:386
  83.4 1.6 %collective-permute-start.17 = (f32[64,1152]{1,0:T(8,128)S(1)}, f32[64,1152]{1,0:T(8,128)S(1)}, u32[]{:S(2)}, u32[]{:S(2)}) collective-permute-start(f32[64,1152]{1,0:T(8,128)S(1)} %fusion.6), channel_id=1, source_target_pairs={{0,8},{8,0},{1,9},{9,1},{2,10},{10,2},{3,11},{11,3},{4,12},{12,4},... | collective-permute-start | bytes 884744 | tf_op jit(solution)/shard_map/ppermute | solution.py:282

commit v4 on v3

--- a/solution.py
+++ b/solution.py
@@ -151,45 +151,127 @@
         fill(1, 0)
 
 
-def forward_body(
-    scale, step, h_ref, hl_ref, hr_ref, o_ref, ol_ref, or_ref, w2_ref, tp_ref,
-    hs_ref, pred_ref, rs_ref,
-):
+NT = (((1,), (1,)), ((), ()))
+
+
+def put_window(ref, at, tile, base, step):
+    mid = tile.shape[0]
+    wide = tile.astype(F32)
+    ref[(*at, slice(base, base + mid))] = shifted(wide, step).astype(BF16)
+    ref[(*at, slice(base + mid, base + 2 * mid))] = tile
+    ref[(*at, slice(base + 2 * mid, base + 3 * mid))] = shifted(wide, -step).astype(BF16)
+
+
+def put_residual(out, target, scale, step, pred_ref, rs_ref, at):
+    outs = out.shape[0]
+    pred_ref[at] = out.astype(BF16)
+    res = ((out - target.astype(F32)) * scale).astype(BF16)
+    wide = res.astype(F32)
+    rs_ref[(*at, slice(0, outs))] = shifted(wide, -step).astype(BF16)
+    rs_ref[(*at, slice(outs, 2 * outs))] = res
+    rs_ref[(*at, slice(2 * outs, 3 * outs))] = shifted(wide, step).astype(BF16)
+
+
+def added(parts):
+    total = None
+    for part in parts:
+        total = part if total is None else total + part
+    return total
+
+
+def inner_body(scale, step, h_ref, o_ref, w2_ref, wg_ref, tp_ref, hs_ref, pred_ref, dg_ref, g_ref, rs_ref):
     orows, pairs, mid, lanes = h_ref.shape
     outs = w2_ref.shape[0]
-    for r in range(orows):
-        for src, (whole, left, right) in enumerate(
-            ((h_ref, hl_ref, hr_ref), (o_ref, ol_ref, or_ref))
-        ):
-            for x in range(pairs + 2):
-                tile = left[r] if x == 0 else right[r] if x == pairs + 1 else whole[r, x - 1]
-                wide = tile.astype(F32)
-                base = src * 3 * mid
-                hs_ref[r, x, base : base + mid, :] = shifted(wide, step).astype(BF16)
-                hs_ref[r, x, base + mid : base + 2 * mid, :] = tile
-                hs_ref[r, x, base + 2 * mid : base + 3 * mid, :] = shifted(wide, -step).astype(BF16)
-    for r in range(orows):
-        for m in range(pairs):
-            window = hs_ref[r, m : m + 3].reshape(3 * 6 * mid, lanes)
+    block = 3 * outs
+    for r in range(orows):
+        for x in range(pairs):
+            put_window(hs_ref, (r, x), h_ref[r, x], 0, step)
+            put_window(hs_ref, (r, x), o_ref[r, x], 3 * mid, step)
+    for r in range(orows):
+        for m in range(1, pairs - 1):
+            window = hs_ref[r, m - 1 : m + 2].reshape(18 * mid, lanes)
             out = jnp.dot(w2_ref[...], window, preferred_element_type=F32)
-            pred_ref[r, m] = out.astype(BF16)
-            res = ((out - tp_ref[r, m].astype(F32)) * scale).astype(BF16)
-            wide = res.astype(F32)
-            rs_ref[r, m, 0:outs, :] = shifted(wide, -step).astype(BF16)
-            rs_ref[r, m, outs : 2 * outs, :] = res
-            rs_ref[r, m, 2 * outs : 3 * outs, :] = shifted(wide, step).astype(BF16)
-
-
-def hidden_grad_body(rs_ref, wg_ref, gown_ref, ghalo_ref, gother_ref):
-    orows, pairs, block, lanes = rs_ref.shape
-    mid = gown_ref.shape[2]
+            put_residual(out, tp_ref[r, m], scale, step, pred_ref, rs_ref, (r, m - 1))
+    for b in range(3):
+        for src in range(2):
+            rows = slice(src * 3 * mid, (src + 1) * 3 * mid)
+            to = (b * 2 + src) * 3 * mid
+            dg_ref[:, to : to + 3 * mid] = added(
+                lax.dot_general(
+                    rs_ref[r, m - 1, outs : 2 * outs], hs_ref[r, m - 1 + b, rows], NT,
+                    preferred_element_type=F32,
+                )
+                for r in range(orows)
+                for m in range(1, pairs - 1)
+            )
+    for r in range(orows):
+        for x in range(1, pairs + 1):
+            low, high = max(x - 2, 1), min(x, pairs - 2)
+            first = low - (x - 2)
+            window = rs_ref[r, low - 1 : high].reshape((high - low + 1) * block, lanes)
+            weights = wg_ref[:, first * block : (first + high - low + 1) * block]
+            g_ref[r, x - 1] = jnp.dot(weights, window, preferred_element_type=F32)
+
+
+def outer_body(
+    scale, step, slab_ref, hs_ref, hl_ref, hr_ref, ol_ref, or_ref, w2_ref, tp_ref, dg_ref,
+    pred_ref, rs_ref, mine_ref, send_ref, other_ref, edge_ref,
+):
+    orows, pairs, depth, lanes = hs_ref.shape
+    mid = depth // 6
+    outs = w2_ref.shape[0]
+    ends = (0, pairs - 1)
+    for r in range(orows):
+        for k, (own, other) in enumerate(((hl_ref, ol_ref), (hr_ref, or_ref))):
+            put_window(edge_ref, (r, k), own[r], 0, step)
+            put_window(edge_ref, (r, k), other[r], 3 * mid, step)
+
+    def taps(r, m, b):
+        x = m - 1 + b
+        return edge_ref.at[r, 0] if x < 0 else edge_ref.at[r, 1] if x == pairs else hs_ref.at[r, x]
+
+    for r in range(orows):
+        for k, m in enumerate(ends):
+            edge = edge_ref[r, k]
+            near = hs_ref[r, 0:2] if k == 0 else hs_ref[r, pairs - 2 : pairs]
+            near = near.reshape(2 * depth, lanes)
+            w_edge = w2_ref[:, :depth] if k == 0 else w2_ref[:, 2 * depth :]
+            w_near = w2_ref[:, depth:] if k == 0 else w2_ref[:, : 2 * depth]
+            out = jnp.dot(w_edge, edge, preferred_element_type=F32)
+            out = out + jnp.dot(w_near, near, preferred_element_type=F32)
+            put_residual(out, tp_ref[r, m], scale, step, pred_ref, rs_ref, (r, k))
+    for b in range(3):
+        columns = slice(b * 3 * mid, (b + 1) * 3 * mid)
+        for src in range(2):
+            rows = slice(src * 3 * mid, (src + 1) * 3 * mid)
+            at = (b * 2 + src) * 3 * mid
+            total = dg_ref[:, at : at + 3 * mid] + added(
+                lax.dot_general(
+                    rs_ref[r, k, outs : 2 * outs], taps(r, m, b)[rows], NT,
+                    preferred_element_type=F32,
+                )
+                for r in range(orows)
+                for k, m in enumerate(ends)
+            )
+            if src == 0:
+                split_rows(slab_ref, total, mine_ref, send_ref, columns)
+            else:
+                strips, count, _ = other_ref.shape
+                other_ref[:, :, columns] = total.reshape(strips, count, 3 * mid).astype(BF16)
+
+
+def hidden_grad_body(rs_ref, wg_ref, g_ref, gown_ref, ghalo_ref, gother_ref):
+    orows, _, block, lanes = rs_ref.shape
+    pairs, mid = gown_ref.shape[1:3]
     for r in range(orows):
         for x in range(pairs + 2):
-            low, high = max(x - 2, 0), min(x, pairs - 1)
-            first = low - (x - 2)
-            window = rs_ref[r, low : high + 1].reshape((high - low + 1) * block, lanes)
-            weights = wg_ref[:, first * block : (first + high - low + 1) * block]
-            grad = jnp.dot(weights, window, preferred_element_type=F32)
+            parts = [g_ref[r, x - 1]] if 0 < x <= pairs else []
+            for k, m in enumerate((0, pairs - 1)):
+                tap = m - (x - 2)
+                if 0 <= tap < 3:
+                    weights = wg_ref[:, tap * block : (tap + 1) * block]
+                    parts.append(jnp.dot(weights, rs_ref[r, k], preferred_element_type=F32))
+            grad = added(parts)
             gother_ref[x, r] = grad[mid:].astype(BF16)
             if x == 0:
                 ghalo_ref[0, r] = grad[:mid]
@@ -199,9 +281,6 @@
                 gown_ref[r, x - 1] = grad[:mid]
 
 
-NT = (((1,), (1,)), ((), ()))
-
-
 def split_rows(slab_ref, total, mine_ref, send_ref, columns):
     strips, rows, _ = mine_ref.shape
     parts = total.reshape(strips, 2, rows, total.shape[1])
@@ -210,44 +289,34 @@
     send_ref[:, :, columns] = jnp.where(first, parts[:, 1], parts[:, 0]).astype(BF16)
 
 
-def dilated_grad_body(slab_ref, rs_ref, hs_ref, mine_ref, send_ref, other_ref):
-    orows, pairs, block, lanes = rs_ref.shape
-    outs = block // 3
-    mid = hs_ref.shape[2] // 6
-    for b in range(3):
-        columns = slice(b * 3 * mid, (b + 1) * 3 * mid)
-        for src in range(2):
-            base = src * 3 * mid
-            total = None
-            for r in range(orows):
-                for m in range(pairs):
-                    window = hs_ref[r, m + b, base : base + 3 * mid, :]
-                    part = lax.dot_general(
-                        rs_ref[r, m, outs : 2 * outs, :], window, NT, preferred_element_type=F32
-                    )
-                    total = part if total is None else total + part
-            if src == 0:
-                split_rows(slab_ref, total, mine_ref, send_ref, columns)
-            else:
-                strips, rows, _ = other_ref.shape
-                other_ref[:, :, columns] = total.reshape(strips, rows, 3 * mid).astype(BF16)
-
-
-def strided_grad_body(slab_ref, gown_ref, gx_ref, gl_ref, gr_ref, slope_ref, vp_ref, mine_ref, send_ref):
-    orows, pairs, mid, lanes = gown_ref.shape
+def strided_part(gown_ref, gx_ref, extra, slope_ref, vp_ref, columns):
+    orows = gown_ref.shape[0]
     plane = vp_ref.shape[1] // (2 * orows + 1)
-    total = None
-    for i in range(orows):
-        for m in range(pairs):
-            grad = gown_ref[i, m] + gx_ref[m + 1, i].astype(F32)
-            if m == 0:
-                grad = grad + gl_ref[i].astype(F32)
-            if m == pairs - 1:
-                grad = grad + gr_ref[i].astype(F32)
-            pg = (grad * slope_ref[i, m]).astype(BF16)
-            window = vp_ref[m, 2 * i * plane : (2 * i + 3) * plane, :]
-            part = lax.dot_general(pg, window, NT, preferred_element_type=F32)
-            total = part if total is None else total + part
+
+    def part(i, m):
+        grad = gown_ref[i, m] + gx_ref[m + 1, i].astype(F32)
+        if m in extra:
+            grad = grad + extra[m][i].astype(F32)
+        pg = (grad * slope_ref[i, m]).astype(BF16)
+        window = vp_ref[m, 2 * i * plane : (2 * i + 3) * plane, :]
+        return lax.dot_general(pg, window, NT, preferred_element_type=F32)
+
+    return added(part(i, m) for i in range(orows) for m in columns)
+
+
+def strided_inner_body(gown_ref, gx_ref, slope_ref, vp_ref, sum_ref):
+    pairs = gown_ref.shape[1]
+    sum_ref[...] = strided_part(gown_ref, gx_ref, {}, slope_ref, vp_ref, range(1, pairs - 1))
+
+
+def strided_grad_body(
+    slab_ref, gown_ref, gx_ref, gl_ref, gr_ref, slope_ref, vp_ref, sum_ref, mine_ref, send_ref
+):
+    pairs, mid = gown_ref.shape[1:3]
+    extra = {0: gl_ref, pairs - 1: gr_ref}
+    total = sum_ref[...] + strided_part(
+        gown_ref, gx_ref, extra, slope_ref, vp_ref, (0, pairs - 1)
+    )
     width = mine_ref.shape[2]
     pad = jnp.zeros((mid, 2 * width - total.shape[1]), F32)
     low, high = total[:, :width], jnp.concatenate([total[:, width:], pad], axis=1)
@@ -256,14 +325,16 @@
     send_ref[...] = jnp.where(first, high, low).reshape(mine_ref.shape).astype(BF16)
 
 
-def prediction_body(pred_ref, out_ref, tall_ref):
-    orows, pairs, outs, lanes = pred_ref.shape
+def prediction_body(inner_ref, outer_ref, out_ref, tall_ref):
+    orows, inner, outs, lanes = inner_ref.shape
     half = lanes // 2
-    cols = 2 * pairs
+    cols = 2 * (inner + 2)
     for r in range(orows):
         slot = r % 2
         for col in range(cols):
-            values = pred_ref[r, col // 2, :, (col % 2) * half : (col % 2 + 1) * half]
+            m = col // 2
+            tile = outer_ref.at[r, m // (inner + 1)] if m in (0, inner + 1) else inner_ref.at[r, m - 1]
+            values = tile[:, (col % 2) * half : (col % 2 + 1) * half]
             tall_ref[slot, pl.ds(col, outs, stride=cols), :] = values.astype(F32)
         out_ref[:, r] = tall_ref[slot].reshape(outs, cols, half).astype(BF16)
 
@@ -341,34 +412,45 @@
     from_left = shift_along(hid_r, "strip", 1)
     from_right = shift_along(hid_l, "strip", -1)
     other = swap(hidden)
+
+    def inner(*refs):
+        inner_body(scale, step, *refs)
+
+    def outer(*refs):
+        outer_body(scale, step, *refs)
+
+    hs, pred_in, dg_in, g_in = vmem_call(
+        inner,
+        (
+            sds((orows, pairs, 6 * mid, lanes), BF16),
+            sds((orows, pairs - 2, outs, lanes), BF16),
+            sds((outs, 18 * mid), F32),
+            sds((orows, pairs, 2 * mid, lanes), F32),
+        ),
+        5,
+        [VMEM((orows, pairs - 2, 3 * outs, lanes), BF16)],
+    )(hidden, other, w2, wg, tp)
+
+    from_left, from_right, hs = lax.optimization_barrier((from_left, from_right, hs))
     other_left = swap(from_left)
     other_right = swap(from_right)
 
-    def forward(*refs):
-        forward_body(scale, step, *refs)
-
-    hs, pred, residual = vmem_call(
-        forward,
-        (
-            sds((orows, pairs + 2, 6 * mid, lanes), BF16),
-            sds((orows, pairs, outs, lanes), BF16),
-            sds((orows, pairs, 3 * outs, lanes), BF16),
-        ),
-        8,
-    )(hidden, from_left, from_right, other, other_left, other_right, w2, tp)
-
     rows = outs // strips
     half_rows = rows // 2
-    mine, send, apart = vmem_call(
-        dilated_grad_body,
+    pred_out, residual, mine, send, apart = vmem_call(
+        outer,
         (
+            sds((orows, 2, outs, lanes), BF16),
+            sds((orows, 2, 3 * outs, lanes), BF16),
             sds((strips, half_rows, 9 * mid), F32),
             sds((strips, half_rows, 9 * mid), BF16),
             sds((strips, rows, 9 * mid), BF16),
         ),
-        2,
+        8,
+        [VMEM((orows, 2, 6 * mid, lanes), BF16)],
         scalars=1,
-    )(slab_id, residual, hs)
+    )(slab_id, hs, from_left, from_right, other_left, other_right, w2, tp, dg_in)
+
     def pick(array, index, dim):
         return lax.dynamic_index_in_dim(array, index, dim, False, allow_negative_indices=False)
 
@@ -377,7 +459,7 @@
         got = lax.ppermute(
             pick(chunks, other_parity, 1), "strip", [(i, i ^ 1) for i in range(strips)]
         )
-        return pick(chunks, parity, 1).astype(F32) + got.astype(F32)
+        return pick(chunks, parity, 1).astype(F32), got
 
     def far_stage(grad):
         total = pick(grad, places[0], 0)
@@ -388,7 +470,7 @@
         return total
 
     dg = jnp.concatenate([(mine + swap(send).astype(F32)).astype(BF16), apart], axis=1)
-    dg = pair_stage(dg)
+    dg, dg_got = pair_stage(dg)
 
     residual, send = lax.optimization_barrier((residual, send))
     gown, ghalo, gother = vmem_call(
@@ -398,8 +480,8 @@
             sds((2, orows, mid, lanes), F32),
             sds((pairs + 2, orows, mid, lanes), BF16),
         ),
-        2,
-    )(residual, wg)
+        3,
+    )(residual, wg, g_in)
 
     gx = swap(gother)
     to_left = (ghalo[0] + gx[0].astype(F32)).astype(BF16)
@@ -410,20 +492,25 @@
     prediction = vmem_call(
         prediction_body,
         sds((outs, orows, ocols, half), BF16),
-        1,
+        2,
         [VMEM((2, outs * ocols, half), F32)],
-    )(pred)
+    )(pred_in, pred_out)
+    sg_in = vmem_call(strided_inner_body, sds((mid, 27 * channels), F32), 4)(gown, gx, slope, vp)
     mid_rows = mid // strips
     width = 9 * mid
     assert width < 27 * channels <= 2 * width
-    grad_l, grad_r, dg, prediction = lax.optimization_barrier((grad_l, grad_r, dg, prediction))
+    grad_l, grad_r, dg_got, prediction, sg_in = lax.optimization_barrier(
+        (grad_l, grad_r, dg_got, prediction, sg_in)
+    )
+    dg = dg + dg_got.astype(F32)
     smine, ssend = vmem_call(
         strided_grad_body,
         (sds((strips, mid_rows, width), F32), sds((strips, mid_rows, width), BF16)),
-        6,
+        7,
         scalars=1,
-    )(slab_id, gown, gx, grad_l, grad_r, slope, vp)
-    sg = pair_stage((smine + swap(ssend).astype(F32)).astype(BF16))
+    )(slab_id, gown, gx, grad_l, grad_r, slope, vp, sg_in)
+    sg, sg_got = pair_stage((smine + swap(ssend).astype(F32)).astype(BF16))
+    sg = sg + sg_got.astype(F32)
     total = far_stage(jnp.concatenate([dg, sg], axis=1))
     across = swap(total)
     low, high = jnp.where(first, total, across), jnp.where(first, across, total)

time: 87.8 us -> 82.8 us (0.943)
  waiting for transfers between devices: 31.5 us -> 25.8 us
    ppermute x6, waiting for transfers between devices: 9.08 us -> 4.94 us  [shift_along(): return lax.ppermute(value, axis, pairs)]
    pallas_call x3 -> x4, Pallas kernels: 7.98 us -> 10.3 us  [the longest x1 4.41 us: local(): vmem_call(inner, (sds((orows, pairs, 6 * mid, lanes), BF16), sds((orows,...]
    ppermute x2, waiting for transfers between devices: 9.9 us -> 8.62 us  [pair_stage(): lax.ppermute(pick(chunks, other_parity, 1), 'strip', [(i, i ^ 1) for i in...]
    pallas_call x1, Pallas kernels: 2.6 us -> 1.41 us  [local(): vmem_call(hidden_grad_body, (sds((orows, pairs, mid, lanes), F32), sds((2...]
    pallas_call x1, Pallas kernels: 2.17 us -> 1.18 us  [local(): vmem_call(strided_grad_body, (sds((strips, mid_rows, width), F32), sds((s...]
  transfers between devices with their start and end apart: 18 -> 18, of which waited for: 11 -> 12; matrix products, arithmetic and copies ran while one was open for 1% -> 1% of each run, Pallas kernels for 10% -> 16%
where the time goes in v4:
time: 82.8 us; the launch traced here: 81.6 us
  starting transfers between devices  29.6 us (36%)
  waiting for transfers between devices  25.8 us (31%)
  Pallas kernels  19.6 us (24%)
  local copies, waits for them, and re-layouts  3.44 us (4%)
  other arithmetic  2.04 us (2%)
  between operations  1.07 us (1%)
    ppermute x6, starting transfers between devices, shift_along(): return lax.ppermute(value, axis, pairs)  17.4 us
    ppermute x2, waiting for transfers between devices, pair_stage(): lax.ppermute(pick(chunks, other_parity, 1), 'strip', [(i, i ^ 1) for i in...  8.62 us
    ppermute x3, waiting for transfers between devices, far_stage(): lax.ppermute(sent, 'strip', [(i, (i + 2 * d) % strips) for i in range(str...  8.08 us
    ppermute x3, starting transfers between devices, far_stage(): lax.ppermute(sent, 'strip', [(i, (i + 2 * d) % strips) for i in range(str...  5.57 us
    ppermute x2, starting transfers between devices, pair_stage(): lax.ppermute(pick(chunks, other_parity, 1), 'strip', [(i, i ^ 1) for i in...  5.24 us
    ppermute x6, waiting for transfers between devices, shift_along(): return lax.ppermute(value, axis, pairs)  4.94 us
    pallas_call x1, Pallas kernels, local(): vmem_call(inner, (sds((orows, pairs, 6 * mid, lanes), BF16), sds((orows,...  4.41 us
    ppermute x7, waiting for transfers between devices, swap(): return lax.ppermute(value, 'slab', [(0, 1), (1, 0)])  4.17 us
  transfers between devices with their start and end apart: 18, of which 12 were waited for; matrix products, arithmetic and copies ran while one was open for 1% of the time, Pallas kernels for 16%

profile of v4, /device:TPU:0, one launch (start us, length us, event | category | flops | bytes accessed | tf_op | source)
XLA Modules:
  0.0 81.6 jit_solution(12834945449693034118)
XLA Ops:
  0.6 1.2 %slice.39 = bf16[64,1,16,256]{3,2,1,0:T(8,128)(2,1)S(1)} slice(bf16[64,4,16,256]{3,2,1,0:T(8,128)(2,1)} %vol_ref.1), slice={[0:64], [3:4], [0:16], [0:256]} | slice | bytes 1048576 | tf_op jit(solution)/shard_map/slice | solution.py:376
  1.9 0.2 copy.18
  2.1 2.4 %collective-permute-start = (bf16[64,16,256]{2,0,1:T(8,128)(2,1)S(1)}, bf16[64,16,256]{2,0,1:T(8,128)(2,1)S(1)}, u32[]{:S(2)}, u32[]{:S(2)}) collective-permute-start(bf16[64,16,256]{2,0,1:T(8,128)(2,1)S(1)} %bitcast.52), channel_id=1, source_target_pairs={{0,8},{1,9},{2,10},{3,11},{4,12},{5,13},{6,14},{7,15},{16,24},{17,... | collective-permute-start | bytes 1572872 | tf_op jit(solution)/shard_map/ppermute | solution.py:349
  4.5 0.0 copy-done
  4.5 0.3 slice.41
  4.8 1.1 %collective-permute-done = bf16[64,16,256]{2,0,1:T(8,128)(2,1)S(1)} collective-permute-done((bf16[64,16,256]{2,0,1:T(8,128)(2,1)S(1)}, bf16[64,16,256]{2,0,1:T(8,128)(2,1)S(1)}, u32[]{:S(2)}, u32[]{:S(2)}) %collective-permute-start) | collective-permute-done | bytes 524320 | tf_op jit(solution)/shard_map/ppermute | solution.py:349
  5.9 0.8 copy-done.4
  6.8 4.3 %collective-permute-start.1 = (bf16[5,64,256]{2,1,0:T(8,128)(2,1)S(1)}, bf16[5,64,256]{2,1,0:T(8,128)(2,1)S(1)}, u32[]{:S(2)}, u32[]{:S(2)}) collective-permute-start(bf16[5,64,256]{2,1,0:T(8,128)(2,1)S(1)} %pad_maximum_fusion.2), channel_id=1, source_target_pairs={{0,1},{1,2},{2,3},{3,4},{4,5},{5,6},{6,7},{8,9},{9,10},{10,11},{11... | collective-permute-start | bytes 491528 | tf_op jit(solution)/shard_map/ppermute | solution.py:349
  11.1 0.0 copy-start.1
  11.1 0.0 copy-start.3
  11.2 4.1 %shard_map.67 = (bf16[4,2880,256]{2,1,0:T(8,128)(2,1)S(1)}, bf16[2,4,256,256]{3,2,1,0:T(8,128)(2,1)S(1)}) custom-call(bf16[64,4,16,256]{3,2,1,0:T(8,128)(2,1)S(1)} %copy-done, bf16[256,2,8,128]{3,2,1,0:T(8,128)(2,1)S(1)} %copy-done.2), custom_call_target="tpu_custom_call" | custom-call | tf_op jit(solution)/shard_map/pallas_call | solution.py:390
  15.2 0.0 copy-start.5
  15.3 0.5 shard_map.68
  15.8 0.5 copy-done.5
  16.3 0.3 copy.9.hrow_ref
  16.6 0.0 collective-permute-done.1.hcol_ref
  16.6 2.2 %shard_map.69 = (bf16[4,2880,256]{2,1,0:T(8,128)(2,1)S(1)}, bf16[2,4,128,256]{3,2,1,0:T(8,128)(2,1)S(1)}, bf16[2,128,256]{2,1,0:T(8,128)(2,1)S(1)}, bf16[2,128,2...) custom-call(bf16[4,2880,256]{2,1,0:T(8,128)(2,1)S(1)} %get-tuple-element.47.own_ref, bf16[64,16,256]{2,1,0:T(8,128)(2,1)S(1)} %copy.9.hrow_ref, ...), custom_call_target="tpu_custom_call" | custom-call | tf_op jit(solution)/shard_map/pallas_call | solution.py:399
  18.8 0.1 collective-permute-start.4
  18.9 3.4 %collective-permute-start.2 = (bf16[2,128,256]{2,1,0:T(8,128)(2,1)S(1)}, bf16[2,128,256]{2,1,0:T(8,128)(2,1)S(1)}, u32[]{:S(2)}, u32[]{:S(2)}) collective-permute-start(bf16[2,128,256]{2,1,0:T(8,128)(2,1)S(1)} %get-tuple-element.49), channel_id=1, source_target_pairs={{0,1},{1,2},{2,3},{3,4},{4,5},{5,6},{6,7},{8,9},{9,10},{10,11},{11... | collective-permute-start | bytes 393224 | tf_op jit(solution)/shard_map/ppermute | solution.py:349
  22.3 1.5 %collective-permute-start.3 = (bf16[2,128,256]{2,1,0:T(8,128)(2,1)S(1)}, bf16[2,128,256]{2,1,0:T(8,128)(2,1)S(1)}, u32[]{:S(2)}, u32[]{:S(2)}) collective-permute-start(bf16[2,128,256]{2,1,0:T(8,128)(2,1)S(1)} %get-tuple-element.50), channel_id=1, source_target_pairs={{1,0},{2,1},{3,2},{4,3},{5,4},{6,5},{7,6},{9,8},{10,9},{11,10},{12... | collective-permute-start | bytes 393224 | tf_op jit(solution)/shard_map/ppermute | solution.py:349
  23.8 0.0 collective-permute-done.4.refs_1_
  23.8 4.4 %shard_map.70 = (bf16[2,4,768,256]{3,2,1,0:T(8,128)(2,1)S(1)}, bf16[2,2,256,256]{3,2,1,0:T(8,128)(2,1)S(1)}, f32[256,2304]{1,0:T(8,128)S(1)}, f32[2,4,256,256]{3,2,1,0:T(8,128)S(1)}) custom-call(bf16[2,4,128,256]{3,2,1,0:T(8,128)(2,1)S(1)} %get-tuple-element.51.refs_0_, bf16[2,4,128,256]{3,2,1,0:T(8,128)(2,1)S(1)} %collective-permute-done.4.refs_1_, ...), custom_call_target="tpu_custom_call" | custom-call | tf_op jit(solution)/shard_map/pallas_call | solution.py:422
  28.2 0.0 collective-permute-done.2.refs_2_
  28.2 1.6 %collective-permute-done.3.refs_3_ = bf16[2,128,256]{2,1,0:T(8,128)(2,1)S(1)} collective-permute-done((bf16[2,128,256]{2,1,0:T(8,128)(2,1)S(1)}, bf16[2,128,256]{2,1,0:T(8,128)(2,1)S(1)}, u32[]{:S(2)}, u32[]{:S(2)}) %collective-permute-start.3) | collective-permute-done | bytes 131104 | tf_op jit(solution)/shard_map/ppermute | solution.py:349
  29.8 0.0 collective-permute-start.5
  29.8 0.5 collective-permute-start.6
  30.3 0.8 %collective-permute-done.5.refs_4_ = bf16[2,128,256]{2,1,0:T(8,128)(2,1)S(1)} collective-permute-done((bf16[2,128,256]{2,1,0:T(8,128)(2,1)S(1)}, bf16[2,128,256]{2,1,0:T(8,128)(2,1)S(1)}, u32[]{:S(2)}, u32[]{:S(2)}) %collective-permute-start.5) | collective-permute-done | bytes 131104 | tf_op jit(solution)/shard_map/ppermute | solution.py:353
  31.2 0.2 collective-permute-done.6.refs_5_
  31.4 3.1 %shard_map.71 = (bf16[2,2,256,256]{3,2,1,0:T(8,128)(2,1)S(1)}, bf16[2,2,768,256]{3,2,1,0:T(8,128)(2,1)S(1)}, f32[8,16,1152]{2,1,0:T(8,128)S(1)}, bf16[8,16,1152]...) custom-call(s32[1]{0:T(128)} %bitcast.slab_ref.refs_0_, bf16[2,4,768,256]{3,2,1,0:T(8,128)(2,1)S(1)} %get-tuple-element.56.refs_1_, ...), custom_call_target="tpu_custom_call" | custom-call | tf_op jit(solution)/shard_map/pallas_call | solution.py:440
  34.4 0.4 collective-permute-start.10
  34.8 1.4 %shard_map.72 = (f32[2,4,128,256]{3,2,1,0:T(8,128)S(1)}, f32[2,2,128,256]{3,2,1,0:T(8,128)S(1)}, bf16[6,2,128,256]{3,2,1,0:T(8,128)(2,1)S(1)}) custom-call(bf16[2,2,768,256]{3,2,1,0:T(8,128)(2,1)S(1)} %get-tuple-element.62.rs_ref, bf16[256,2304]{1,0:T(8,128)(2,1)S(1)} %get-tuple-element.53.refs_3_.wg_ref, f32[2,4,256,256]{3,2,1,0:T(8,128)S(1)} %get-tuple-element.63.g_ref), custom_call_target="tpu_custom_call" | custom-call | tf_op jit(solution)/shard_map/pallas_call | solution.py:476
  36.2 0.3 collective-permute-start.7
  36.5 0.0 collective-permute-done.10
  36.5 0.1 add_convert_fusion.1
  36.6 0.1 pad_maximum_fusion
  36.7 2.7 %collective-permute-start.11 = (bf16[4,48,1152]{2,1,0:T(8,128)(2,1)S(1)}, bf16[4,48,1152]{2,1,0:T(8,128)(2,1)S(1)}, u32[]{:S(2)}, u32[]{:S(2)}) collective-permute-start(bf16[4,48,1152]{2,1,0:T(8,128)(2,1)S(1)} %dynamic-slice_bitcast_fusion), channel_id=1, source_target_pairs={{0,1},{1,0},{2,3},{3,2},{4,5},{5,4},{6,7},{7,6},{8,9},{9,8},{10,11... | collective-permute-start | bytes 1327112 | tf_op jit(solution)/shard_map/ppermute | solution.py:459
  39.4 0.0 collective-permute-done.7.gx_ref
  39.4 0.1 fusion.15
  39.5 1.3 %collective-permute-start.9 = (bf16[2,128,256]{2,1,0:T(8,128)(2,1)S(1)}, bf16[2,128,256]{2,1,0:T(8,128)(2,1)S(1)}, u32[]{:S(2)}, u32[]{:S(2)}) collective-permute-start(bf16[2,128,256]{2,1,0:T(8,128)(2,1)S(1)} %get-tuple-element.87), channel_id=1, source_target_pairs={{1,0},{2,1},{3,2},{4,3},{5,4},{6,5},{7,6},{9,8},{10,9},{11,10},{12... | collective-permute-start | bytes 393224 | tf_op jit(solution)/shard_map/ppermute | solution.py:349
  40.8 4.6 %collective-permute-start.8 = (bf16[2,128,256]{2,1,0:T(8,128)(2,1)S(1)}, bf16[2,128,256]{2,1,0:T(8,128)(2,1)S(1)}, u32[]{:S(2)}, u32[]{:S(2)}) collective-permute-start(bf16[2,128,256]{2,1,0:T(8,128)(2,1)S(1)} %get-tuple-element.88), channel_id=1, source_target_pairs={{0,1},{1,2},{2,3},{3,4},{4,5},{5,6},{6,7},{8,9},{9,10},{10,11},{11... | collective-permute-start | bytes 393224 | tf_op jit(solution)/shard_map/ppermute | solution.py:349
  45.3 1.6 %shard_map.73 = bf16[256,2,8,128]{3,2,1,0:T(8,128)(2,1)} custom-call(bf16[2,2,256,256]{3,2,1,0:T(8,128)(2,1)S(1)} %get-tuple-element.69.inner_ref, bf16[2,2,256,256]{3,2,1,0:T(8,128)(2,1)S(1)} %get-tuple-element.70.outer_ref), custom_call_target="tpu_custom_call" | custom-call | tf_op jit(solution)/shard_map/pallas_call | solution.py:492
  47.0 1.2 %shard_map.74.sum_ref = f32[128,1728]{1,0:T(8,128)S(1)} custom-call(f32[2,4,128,256]{3,2,1,0:T(8,128)S(1)} %get-tuple-element.71.gown_ref, bf16[6,2,128,256]{3,2,1,0:T(8,128)(2,1)S(1)} %collective-permute-done.7.gx_ref, f32[2,4,128,256]{3,2,1,0:T(8,128)S(1)} %get-tuple-element.72.slope_ref, bf16[4,2880,256]{2,1,0:T(8,128)(2,1)S(1)} %get-tuple-element.73.vp_ref), custom_call_target="tpu_custom_call" | custom-call | tf_op jit(solution)/shard_map/pallas_call | solution.py:498
  48.1 4.6 %collective-permute-done.11 = bf16[4,48,1152]{2,1,0:T(8,128)(2,1)S(1)} collective-permute-done((bf16[4,48,1152]{2,1,0:T(8,128)(2,1)S(1)}, bf16[4,48,1152]{2,1,0:T(8,128)(2,1)S(1)}, u32[]{:S(2)}, u32[]{:S(2)}) %collective-permute-start.11) | collective-permute-done | bytes 442400 | tf_op jit(solution)/shard_map/ppermute | solution.py:459
  52.7 0.1 collective-permute-done.9.gr_ref
  52.9 2.1 %collective-permute-done.8.gl_ref = bf16[2,128,256]{2,1,0:T(8,128)(2,1)S(1)} collective-permute-done((bf16[2,128,256]{2,1,0:T(8,128)(2,1)S(1)}, bf16[2,128,256]{2,1,0:T(8,128)(2,1)S(1)}, u32[]{:S(2)}, u32[]{:S(2)}) %collective-permute-start.8) | collective-permute-done | bytes 131104 | tf_op jit(solution)/shard_map/ppermute | solution.py:349
  54.9 1.2 %shard_map.75 = (f32[8,16,1152]{2,1,0:T(8,128)S(1)}, bf16[8,16,1152]{2,1,0:T(8,128)(2,1)S(1)}) custom-call(s32[1]{0:T(128)} %bitcast.slab_ref.refs_0_, f32[2,4,128,256]{3,2,1,0:T(8,128)S(1)} %get-tuple-element.71.gown_ref, bf16[6,2,128,256]{3,2,1,0:T(8,128)(2,1)S(1)} %collective-permute-done.7.gx_ref, ...), custom_call_target="tpu_custom_call" | custom-call | tf_op jit(solution)/shard_map/pallas_call | solution.py:506
  56.1 0.1 collective-permute-start.12
  56.2 1.6 %collective-permute-done.12 = bf16[8,16,1152]{2,1,0:T(8,128)(2,1)S(1)} collective-permute-done((bf16[8,16,1152]{2,1,0:T(8,128)(2,1)S(1)}, bf16[8,16,1152]{2,1,0:T(8,128)(2,1)S(1)}, u32[]{:S(2)}, u32[]{:S(2)}) %collective-permute-start.12) | collective-permute-done | bytes 294944 | tf_op jit(solution)/shard_map/ppermute | solution.py:353
  57.8 0.1 add_convert_fusion
  57.9 2.5 %collective-permute-start.13 = (bf16[4,16,1152]{2,1,0:T(8,128)(2,1)S(1)}, bf16[4,16,1152]{2,1,0:T(8,128)(2,1)S(1)}, u32[]{:S(2)}, u32[]{:S(2)}) collective-permute-start(bf16[4,16,1152]{2,1,0:T(8,128)(2,1)S(1)} %dynamic-slice_bitcast_fusion.1), channel_id=1, source_target_pairs={{0,1},{1,0},{2,3},{3,2},{4,5},{5,4},{6,7},{7,6},{8,9},{9,8},{10,11... | collective-permute-start | bytes 442376 | tf_op jit(solution)/shard_map/ppermute | solution.py:459
  60.4 0.1 convert_add_fusion
  60.5 4.1 %collective-permute-done.13 = bf16[4,16,1152]{2,1,0:T(8,128)(2,1)S(1)} collective-permute-done((bf16[4,16,1152]{2,1,0:T(8,128)(2,1)S(1)}, bf16[4,16,1152]{2,1,0:T(8,128)(2,1)S(1)}, u32[]{:S(2)}, u32[]{:S(2)}) %collective-permute-start.13) | collective-permute-done | bytes 147488 | tf_op jit(solution)/shard_map/ppermute | solution.py:459
  64.6 0.1 fusion.12
  64.7 1.6 %collective-permute-start.14 = (bf16[64,1152]{1,0:T(8,128)(2,1)S(1)}, bf16[64,1152]{1,0:T(8,128)(2,1)S(1)}, u32[]{:S(2)}, u32[]{:S(2)}) collective-permute-start(bf16[64,1152]{1,0:T(8,128)(2,1)S(1)} %get-tuple-element.89), channel_id=1, source_target_pairs={{0,2},{1,3},{2,4},{3,5},{4,6},{5,7},{6,0},{7,1},{8,10},{9,11},{10,... | collective-permute-start | bytes 442376 | tf_op jit(solution)/shard_map/ppermute | solution.py:468
  66.3 2.5 %collective-permute-start.15 = (bf16[64,1152]{1,0:T(8,128)(2,1)S(1)}, bf16[64,1152]{1,0:T(8,128)(2,1)S(1)}, u32[]{:S(2)}, u32[]{:S(2)}) collective-permute-start(bf16[64,1152]{1,0:T(8,128)(2,1)S(1)} %get-tuple-element.90), channel_id=1, source_target_pairs={{0,4},{1,5},{2,6},{3,7},{4,0},{5,1},{6,2},{7,3},{8,12},{9,13},{10,... | collective-permute-start | bytes 442376 | tf_op jit(solution)/shard_map/ppermute | solution.py:468
  68.8 1.5 %collective-permute-start.16 = (bf16[64,1152]{1,0:T(8,128)(2,1)S(1)}, bf16[64,1152]{1,0:T(8,128)(2,1)S(1)}, u32[]{:S(2)}, u32[]{:S(2)}) collective-permute-start(bf16[64,1152]{1,0:T(8,128)(2,1)S(1)} %get-tuple-element.91), channel_id=1, source_target_pairs={{0,6},{1,7},{2,0},{3,1},{4,2},{5,3},{6,4},{7,5},{8,14},{9,15},{10,... | collective-permute-start | bytes 442376 | tf_op jit(solution)/shard_map/ppermute | solution.py:468
  70.2 3.1 %collective-permute-done.14 = bf16[64,1152]{1,0:T(8,128)(2,1)S(1)} collective-permute-done((bf16[64,1152]{1,0:T(8,128)(2,1)S(1)}, bf16[64,1152]{1,0:T(8,128)(2,1)S(1)}, u32[]{:S(2)}, u32[]{:S(2)}) %collective-permute-start.14) | collective-permute-done | bytes 147488 | tf_op jit(solution)/shard_map/ppermute | solution.py:468
  73.4 4.9 %collective-permute-done.15 = bf16[64,1152]{1,0:T(8,128)(2,1)S(1)} collective-permute-done((bf16[64,1152]{1,0:T(8,128)(2,1)S(1)}, bf16[64,1152]{1,0:T(8,128)(2,1)S(1)}, u32[]{:S(2)}, u32[]{:S(2)}) %collective-permute-start.15) | collective-permute-done | bytes 147488 | tf_op jit(solution)/shard_map/ppermute | solution.py:468
  78.3 0.0 collective-permute-done.16
  78.3 0.1 fusion.6
  78.4 0.1 collective-permute-start.17
  78.5 1.6 %collective-permute-done.17 = f32[64,1152]{1,0:T(8,128)S(1)} collective-permute-done((f32[64,1152]{1,0:T(8,128)S(1)}, f32[64,1152]{1,0:T(8,128)S(1)}, u32[]{:S(2)}, u32[]{:S(2)}) %collective-permute-start.17) | collective-permute-done | bytes 294944 | tf_op jit(solution)/shard_map/ppermute | solution.py:353
  80.2 0.7 pad_maximum_fusion.3
  80.8 0.8 pad_maximum_fusion.1
  (18 shorter events, 0.3 us)
Async XLA Ops:
  0.6 3.8 %copy-start = (bf16[64,4,16,256]{3,2,1,0:T(8,128)(2,1)S(1)}, bf16[64,4,16,256]{3,2,1,0:T(8,128)(2,1)}, u32[]{:S(2)}) copy-start(bf16[64,4,16,256]{3,2,1,0:T(8,128)(2,1)} %vol_ref.1) | copy-start | bytes 6291460
  0.6 10.5 %copy-start.2 = (bf16[256,2,8,128]{3,2,1,0:T(8,128)(2,1)S(1)}, bf16[256,2,8,128]{3,2,1,0:T(8,128)(2,1)}, u32[]{:S(2)}) copy-start(bf16[256,2,8,128]{3,2,1,0:T(8,128)(2,1)} %tgt_ref) | copy-start | bytes 3145732
  2.1 3.9 %collective-permute-start = (bf16[64,16,256]{2,0,1:T(8,128)(2,1)S(1)}, bf16[64,16,256]{2,0,1:T(8,128)(2,1)S(1)}, u32[]{:S(2)}, u32[]{:S(2)}) collective-permute-start(bf16[64,16,256]{2,0,1:T(8,128)(2,1)S(1)} %bitcast.52), channel_id=1, source_target_pairs={{0,8},{1,9},{2,10},{3,11},{4,12},{5,13},{6,14},{7,15},{16,24},{17,... | collective-permute-start | bytes 1572872 | tf_op jit(solution)/shard_map/ppermute | solution.py:349
  5.9 0.8 copy-start.4
  6.8 9.8 %collective-permute-start.1 = (bf16[5,64,256]{2,1,0:T(8,128)(2,1)S(1)}, bf16[5,64,256]{2,1,0:T(8,128)(2,1)S(1)}, u32[]{:S(2)}, u32[]{:S(2)}) collective-permute-start(bf16[5,64,256]{2,1,0:T(8,128)(2,1)S(1)} %pad_maximum_fusion.2), channel_id=1, source_target_pairs={{0,1},{1,2},{2,3},{3,4},{4,5},{5,6},{6,7},{8,9},{9,10},{10,11},{11... | collective-permute-start | bytes 491528 | tf_op jit(solution)/shard_map/ppermute | solution.py:349
  11.1 4.1 %copy-start.1 = (bf16[256,3456]{1,0:T(8,128)(2,1)S(1)}, bf16[256,3456]{1,0:T(8,128)(2,1)}, u32[]{:S(2)}) copy-start(bf16[256,3456]{1,0:T(8,128)(2,1)} %wd_ref.1) | copy-start | bytes 5308420
  11.1 4.1 %copy-start.3 = (bf16[128,1728]{0,1:T(8,128)(2,1)S(1)}, bf16[128,1728]{0,1:T(8,128)(2,1)}, u32[]{:S(2)}) copy-start(bf16[128,1728]{0,1:T(8,128)(2,1)} %param.6) | copy-start | bytes 1327108
  15.2 1.0 %copy-start.5 = (bf16[64,16,256]{2,0,1:T(8,128)(2,1)S(1)}, bf16[64,16,256]{2,0,1:T(8,128)(2,1)}, u32[]{:S(2)}) copy-start(bf16[64,16,256]{2,0,1:T(8,128)(2,1)} %copy-done.4) | copy-start | bytes 1572868
  18.8 5.0 %collective-permute-start.4 = (bf16[2,4,128,256]{3,2,1,0:T(8,128)(2,1)S(1)}, bf16[2,4,128,256]{3,2,1,0:T(8,128)(2,1)S(1)}, u32[]{:S(2)}, u32[]{:S(2)}) collective-permute-start(bf16[2,4,128,256]{3,2,1,0:T(8,128)(2,1)S(1)} %get-tuple-element.51.refs_0_), channel_id=1, source_target_pairs={{0,8},{8,0},{1,9},{9,1},{2,10},{10,2},{3,11},{11,3},{4,12},{12,4},... | collective-permute-start | bytes 1572872 | tf_op jit(solution)/shard_map/ppermute | solution.py:353
  18.9 9.3 %collective-permute-start.2 = (bf16[2,128,256]{2,1,0:T(8,128)(2,1)S(1)}, bf16[2,128,256]{2,1,0:T(8,128)(2,1)S(1)}, u32[]{:S(2)}, u32[]{:S(2)}) collective-permute-start(bf16[2,128,256]{2,1,0:T(8,128)(2,1)S(1)} %get-tuple-element.49), channel_id=1, source_target_pairs={{0,1},{1,2},{2,3},{3,4},{4,5},{5,6},{6,7},{8,9},{9,10},{10,11},{11... | collective-permute-start | bytes 393224 | tf_op jit(solution)/shard_map/ppermute | solution.py:349
  22.3 7.5 %collective-permute-start.3 = (bf16[2,128,256]{2,1,0:T(8,128)(2,1)S(1)}, bf16[2,128,256]{2,1,0:T(8,128)(2,1)S(1)}, u32[]{:S(2)}, u32[]{:S(2)}) collective-permute-start(bf16[2,128,256]{2,1,0:T(8,128)(2,1)S(1)} %get-tuple-element.50), channel_id=1, source_target_pairs={{1,0},{2,1},{3,2},{4,3},{5,4},{6,5},{7,6},{9,8},{10,9},{11,10},{12... | collective-permute-start | bytes 393224 | tf_op jit(solution)/shard_map/ppermute | solution.py:349
  29.8 1.3 %collective-permute-start.5 = (bf16[2,128,256]{2,1,0:T(8,128)(2,1)S(1)}, bf16[2,128,256]{2,1,0:T(8,128)(2,1)S(1)}, u32[]{:S(2)}, u32[]{:S(2)}) collective-permute-start(bf16[2,128,256]{2,1,0:T(8,128)(2,1)S(1)} %collective-permute-done.2.refs_2_), channel_id=1, source_target_pairs={{0,8},{8,0},{1,9},{9,1},{2,10},{10,2},{3,11},{11,3},{4,12},{12,4},... | collective-permute-start | bytes 393224 | tf_op jit(solution)/shard_map/ppermute | solution.py:353
  29.8 1.5 %collective-permute-start.6 = (bf16[2,128,256]{2,1,0:T(8,128)(2,1)S(1)}, bf16[2,128,256]{2,1,0:T(8,128)(2,1)S(1)}, u32[]{:S(2)}, u32[]{:S(2)}) collective-permute-start(bf16[2,128,256]{2,1,0:T(8,128)(2,1)S(1)} %collective-permute-done.3.refs_3_), channel_id=1, source_target_pairs={{0,8},{8,0},{1,9},{9,1},{2,10},{10,2},{3,11},{11,3},{4,12},{12,4},... | collective-permute-start | bytes 393224 | tf_op jit(solution)/shard_map/ppermute | solution.py:353
  34.4 2.1 %collective-permute-start.10 = (bf16[8,16,1152]{2,1,0:T(8,128)(2,1)S(1)}, bf16[8,16,1152]{2,1,0:T(8,128)(2,1)S(1)}, u32[]{:S(2)}, u32[]{:S(2)}) collective-permute-start(bf16[8,16,1152]{2,1,0:T(8,128)(2,1)S(1)} %get-tuple-element.61), channel_id=1, source_target_pairs={{0,8},{8,0},{1,9},{9,1},{2,10},{10,2},{3,11},{11,3},{4,12},{12,4},... | collective-permute-start | bytes 884744 | tf_op jit(solution)/shard_map/ppermute | solution.py:353
  36.2 3.2 %collective-permute-start.7 = (bf16[6,2,128,256]{3,2,1,0:T(8,128)(2,1)S(1)}, bf16[6,2,128,256]{3,2,1,0:T(8,128)(2,1)S(1)}, u32[]{:S(2)}, u32[]{:S(2)}) collective-permute-start(bf16[6,2,128,256]{3,2,1,0:T(8,128)(2,1)S(1)} %get-tuple-element.65), channel_id=1, source_target_pairs={{0,8},{8,0},{1,9},{9,1},{2,10},{10,2},{3,11},{11,3},{4,12},{12,4},... | collective-permute-start | bytes 2359304 | tf_op jit(solution)/shard_map/ppermute | solution.py:353
  36.7 16.0 %collective-permute-start.11 = (bf16[4,48,1152]{2,1,0:T(8,128)(2,1)S(1)}, bf16[4,48,1152]{2,1,0:T(8,128)(2,1)S(1)}, u32[]{:S(2)}, u32[]{:S(2)}) collective-permute-start(bf16[4,48,1152]{2,1,0:T(8,128)(2,1)S(1)} %dynamic-slice_bitcast_fusion), channel_id=1, source_target_pairs={{0,1},{1,0},{2,3},{3,2},{4,5},{5,4},{6,7},{7,6},{8,9},{9,8},{10,11... | collective-permute-start | bytes 1327112 | tf_op jit(solution)/shard_map/ppermute | solution.py:459
  39.5 13.4 %collective-permute-start.9 = (bf16[2,128,256]{2,1,0:T(8,128)(2,1)S(1)}, bf16[2,128,256]{2,1,0:T(8,128)(2,1)S(1)}, u32[]{:S(2)}, u32[]{:S(2)}) collective-permute-start(bf16[2,128,256]{2,1,0:T(8,128)(2,1)S(1)} %get-tuple-element.87), channel_id=1, source_target_pairs={{1,0},{2,1},{3,2},{4,3},{5,4},{6,5},{7,6},{9,8},{10,9},{11,10},{12... | collective-permute-start | bytes 393224 | tf_op jit(solution)/shard_map/ppermute | solution.py:349
  40.8 14.1 %collective-permute-start.8 = (bf16[2,128,256]{2,1,0:T(8,128)(2,1)S(1)}, bf16[2,128,256]{2,1,0:T(8,128)(2,1)S(1)}, u32[]{:S(2)}, u32[]{:S(2)}) collective-permute-start(bf16[2,128,256]{2,1,0:T(8,128)(2,1)S(1)} %get-tuple-element.88), channel_id=1, source_target_pairs={{0,1},{1,2},{2,3},{3,4},{4,5},{5,6},{6,7},{8,9},{9,10},{10,11},{11... | collective-permute-start | bytes 393224 | tf_op jit(solution)/shard_map/ppermute | solution.py:349
  56.1 1.6 %collective-permute-start.12 = (bf16[8,16,1152]{2,1,0:T(8,128)(2,1)S(1)}, bf16[8,16,1152]{2,1,0:T(8,128)(2,1)S(1)}, u32[]{:S(2)}, u32[]{:S(2)}) collective-permute-start(bf16[8,16,1152]{2,1,0:T(8,128)(2,1)S(1)} %get-tuple-element.82), channel_id=1, source_target_pairs={{0,8},{8,0},{1,9},{9,1},{2,10},{10,2},{3,11},{11,3},{4,12},{12,4},... | collective-permute-start | bytes 884744 | tf_op jit(solution)/shard_map/ppermute | solution.py:353
  57.9 6.7 %collective-permute-start.13 = (bf16[4,16,1152]{2,1,0:T(8,128)(2,1)S(1)}, bf16[4,16,1152]{2,1,0:T(8,128)(2,1)S(1)}, u32[]{:S(2)}, u32[]{:S(2)}) collective-permute-start(bf16[4,16,1152]{2,1,0:T(8,128)(2,1)S(1)} %dynamic-slice_bitcast_fusion.1), channel_id=1, source_target_pairs={{0,1},{1,0},{2,3},{3,2},{4,5},{5,4},{6,7},{7,6},{8,9},{9,8},{10,11... | collective-permute-start | bytes 442376 | tf_op jit(solution)/shard_map/ppermute | solution.py:459
  64.7 8.7 %collective-permute-start.14 = (bf16[64,1152]{1,0:T(8,128)(2,1)S(1)}, bf16[64,1152]{1,0:T(8,128)(2,1)S(1)}, u32[]{:S(2)}, u32[]{:S(2)}) collective-permute-start(bf16[64,1152]{1,0:T(8,128)(2,1)S(1)} %get-tuple-element.89), channel_id=1, source_target_pairs={{0,2},{1,3},{2,4},{3,5},{4,6},{5,7},{6,0},{7,1},{8,10},{9,11},{10,... | collective-permute-start | bytes 442376 | tf_op jit(solution)/shard_map/ppermute | solution.py:468
  66.3 12.0 %collective-permute-start.15 = (bf16[64,1152]{1,0:T(8,128)(2,1)S(1)}, bf16[64,1152]{1,0:T(8,128)(2,1)S(1)}, u32[]{:S(2)}, u32[]{:S(2)}) collective-permute-start(bf16[64,1152]{1,0:T(8,128)(2,1)S(1)} %get-tuple-element.90), channel_id=1, source_target_pairs={{0,4},{1,5},{2,6},{3,7},{4,0},{5,1},{6,2},{7,3},{8,12},{9,13},{10,... | collective-permute-start | bytes 442376 | tf_op jit(solution)/shard_map/ppermute | solution.py:468
  68.8 9.6 %collective-permute-start.16 = (bf16[64,1152]{1,0:T(8,128)(2,1)S(1)}, bf16[64,1152]{1,0:T(8,128)(2,1)S(1)}, u32[]{:S(2)}, u32[]{:S(2)}) collective-permute-start(bf16[64,1152]{1,0:T(8,128)(2,1)S(1)} %get-tuple-element.91), channel_id=1, source_target_pairs={{0,6},{1,7},{2,0},{3,1},{4,2},{5,3},{6,4},{7,5},{8,14},{9,15},{10,... | collective-permute-start | bytes 442376 | tf_op jit(solution)/shard_map/ppermute | solution.py:468
  78.4 1.6 %collective-permute-start.17 = (f32[64,1152]{1,0:T(8,128)S(1)}, f32[64,1152]{1,0:T(8,128)S(1)}, u32[]{:S(2)}, u32[]{:S(2)}) collective-permute-start(f32[64,1152]{1,0:T(8,128)S(1)} %fusion.6), channel_id=1, source_target_pairs={{0,8},{8,0},{1,9},{9,1},{2,10},{10,2},{3,11},{11,3},{4,12},{12,4},... | collective-permute-start | bytes 884744 | tf_op jit(solution)/shard_map/ppermute | solution.py:353

commit v5 on v4

--- a/solution.py
+++ b/solution.py
@@ -454,25 +454,27 @@
     def pick(array, index, dim):
         return lax.dynamic_index_in_dim(array, index, dim, False, allow_negative_indices=False)
 
-    def pair_stage(grad):
-        chunks = grad.reshape(groups, 2, *grad.shape[1:])
-        got = lax.ppermute(
-            pick(chunks, other_parity, 1), "strip", [(i, i ^ 1) for i in range(strips)]
-        )
-        return pick(chunks, parity, 1).astype(F32), got
-
-    def far_stage(grad):
-        total = pick(grad, places[0], 0)
-        for d in range(1, groups):
-            sent = pick(grad, places[d], 0).astype(BF16)
-            got = lax.ppermute(sent, "strip", [(i, (i + 2 * d) % strips) for i in range(strips)])
-            total = total + got.astype(F32)
-        return total
-
-    dg = jnp.concatenate([(mine + swap(send).astype(F32)).astype(BF16), apart], axis=1)
-    dg, dg_got = pair_stage(dg)
-
-    residual, send = lax.optimization_barrier((residual, send))
+    def pair_swap(value):
+        return lax.ppermute(value, "strip", [(i, i ^ 1) for i in range(strips)])
+
+    def far_swap(chunks):
+        return [
+            lax.ppermute(
+                pick(chunks, places[d], 0).astype(BF16),
+                "strip",
+                [(i, (i + 2 * d) % strips) for i in range(strips)],
+            )
+            for d in range(1, groups)
+        ]
+
+    def far_sum(chunks, got):
+        return added([pick(chunks, places[0], 0).astype(F32), *(g.astype(F32) for g in got)])
+
+    apart = apart.reshape(groups, 2, rows, 9 * mid)
+    apart_got = pair_swap(pick(apart, other_parity, 1))
+    dg_own = (mine + swap(send).astype(F32)).astype(BF16)
+
+    send, residual = lax.optimization_barrier((send, residual))
     gown, ghalo, gother = vmem_call(
         hidden_grad_body,
         (
@@ -499,19 +501,31 @@
     mid_rows = mid // strips
     width = 9 * mid
     assert width < 27 * channels <= 2 * width
-    grad_l, grad_r, dg_got, prediction, sg_in = lax.optimization_barrier(
-        (grad_l, grad_r, dg_got, prediction, sg_in)
-    )
-    dg = dg + dg_got.astype(F32)
+    dg_own, prediction = lax.optimization_barrier((dg_own, prediction))
+    dg_own = dg_own.reshape(groups, 2, half_rows, 9 * mid)
+    own_got = far_swap(dg_own)
+    grad_l, grad_r, apart_got, sg_in = lax.optimization_barrier((grad_l, grad_r, apart_got, sg_in))
     smine, ssend = vmem_call(
         strided_grad_body,
         (sds((strips, mid_rows, width), F32), sds((strips, mid_rows, width), BF16)),
         7,
         scalars=1,
     )(slab_id, gown, gx, grad_l, grad_r, slope, vp, sg_in)
-    sg, sg_got = pair_stage((smine + swap(ssend).astype(F32)).astype(BF16))
-    sg = sg + sg_got.astype(F32)
-    total = far_stage(jnp.concatenate([dg, sg], axis=1))
+    sg = (smine + swap(ssend).astype(F32)).astype(BF16).reshape(groups, 2, mid_rows, width)
+    own = far_sum(dg_own, own_got)
+    sent = jnp.concatenate(
+        [
+            pick(sg, other_parity, 1).reshape(groups * mid_rows, width),
+            pick(own, other_parity, 0).astype(BF16),
+        ],
+        axis=0,
+    )
+    got = pair_swap(sent).astype(F32)
+    own = pick(own, parity, 0) + got[groups * mid_rows :]
+    sg = pick(sg, parity, 1).astype(F32) + got[: groups * mid_rows].reshape(groups, mid_rows, width)
+    dg = pick(apart, parity, 1).astype(F32) + apart_got.astype(F32)
+    total = jnp.concatenate([dg, sg], axis=1)
+    total = jnp.concatenate([own, far_sum(total, far_swap(total))], axis=0)
     across = swap(total)
     low, high = jnp.where(first, total, across), jnp.where(first, across, total)
     middle = jnp.concatenate([low[:half_rows], high[:half_rows]], axis=0)

time: 82.8 us -> 77.8 us (0.940); the launches traced: 81.6 us -> 77.6 us
  waiting for transfers between devices: 25.8 us -> 19.3 us
  starting transfers between devices: 29.6 us -> 32.5 us
    ppermute x5 -> x8, waiting for transfers between devices: 16.7 us -> 13.5 us  [the longest x6 8.73 us: far_swap(): lax.ppermute(pick(chunks, places[d], 0).astype(BF16), 'strip', [(i, (i +...]
    ppermute x5 -> x8, starting transfers between devices: 10.8 us -> 13.7 us  [the longest x6 9.56 us: far_swap(): lax.ppermute(pick(chunks, places[d], 0).astype(BF16), 'strip', [(i, (i +...]
    ppermute x6, waiting for transfers between devices: 4.94 us -> 3.18 us  [shift_along(): return lax.ppermute(value, axis, pairs)]
    ppermute x7, waiting for transfers between devices: 4.17 us -> 2.6 us  [swap(): return lax.ppermute(value, 'slab', [(0, 1), (1, 0)])]
  transfers between devices with their start and end apart: 18 -> 21, of which waited for: 12 -> 10; matrix products, arithmetic and copies ran while one was open for 1% -> 1% of each run, Pallas kernels for 16% -> 19%
where the time goes in v5:
time: 77.8 us; the launch traced here: 77.6 us
  starting transfers between devices  32.5 us (42%)
  Pallas kernels  19.6 us (25%)
  waiting for transfers between devices  19.3 us (25%)
  local copies, waits for them, and re-layouts  2.99 us (4%)
  other arithmetic  2.01 us (3%)
  between operations  1.17 us (2%)
    ppermute x6, starting transfers between devices, shift_along(): return lax.ppermute(value, axis, pairs)  17.4 us
    ppermute x6, starting transfers between devices, far_swap(): lax.ppermute(pick(chunks, places[d], 0).astype(BF16), 'strip', [(i, (i +...  9.56 us
    ppermute x6, waiting for transfers between devices, far_swap(): lax.ppermute(pick(chunks, places[d], 0).astype(BF16), 'strip', [(i, (i +...  8.73 us
    ppermute x2, waiting for transfers between devices, pair_swap(): return lax.ppermute(value, 'strip', [(i, i ^ 1) for i in range(strips)])  4.78 us
    pallas_call x1, Pallas kernels, local(): vmem_call(inner, (sds((orows, pairs, 6 * mid, lanes), BF16), sds((orows,...  4.41 us
    ppermute x2, starting transfers between devices, pair_swap(): return lax.ppermute(value, 'strip', [(i, i ^ 1) for i in range(strips)])  4.1 us
    pallas_call x1, Pallas kernels, local(): vmem_call(split_body, (sds((pairs, (rows_in + 1) * 9 * channels, lanes),...  4.07 us
    ppermute x6, waiting for transfers between devices, shift_along(): return lax.ppermute(value, axis, pairs)  3.18 us
  transfers between devices with their start and end apart: 21, of which 10 were waited for; matrix products, arithmetic and copies ran while one was open for 1% of the time, Pallas kernels for 19%

profile of v5, /device:TPU:0, one launch (start us, length us, event | category | flops | bytes accessed | tf_op | source)
XLA Modules:
  0.0 77.6 jit_solution(1853061453205471831)
XLA Ops:
  0.6 1.2 %slice.45 = bf16[64,1,16,256]{3,2,1,0:T(8,128)(2,1)S(1)} slice(bf16[64,4,16,256]{3,2,1,0:T(8,128)(2,1)} %vol_ref.1), slice={[0:64], [3:4], [0:16], [0:256]} | slice | bytes 1048576 | tf_op jit(solution)/shard_map/slice | solution.py:376
  1.9 0.2 copy.18
  2.1 2.4 %collective-permute-start = (bf16[64,16,256]{2,0,1:T(8,128)(2,1)S(1)}, bf16[64,16,256]{2,0,1:T(8,128)(2,1)S(1)}, u32[]{:S(2)}, u32[]{:S(2)}) collective-permute-start(bf16[64,16,256]{2,0,1:T(8,128)(2,1)S(1)} %bitcast.70), channel_id=1, source_target_pairs={{0,8},{1,9},{2,10},{3,11},{4,12},{5,13},{6,14},{7,15},{16,24},{17,... | collective-permute-start | bytes 1572872 | tf_op jit(solution)/shard_map/ppermute | solution.py:349
  4.5 0.3 slice.47
  4.8 1.1 %collective-permute-done = bf16[64,16,256]{2,0,1:T(8,128)(2,1)S(1)} collective-permute-done((bf16[64,16,256]{2,0,1:T(8,128)(2,1)S(1)}, bf16[64,16,256]{2,0,1:T(8,128)(2,1)S(1)}, u32[]{:S(2)}, u32[]{:S(2)}) %collective-permute-start) | collective-permute-done | bytes 524320 | tf_op jit(solution)/shard_map/ppermute | solution.py:349
  5.9 0.8 %copy-done.4 = bf16[64,16,256]{2,0,1:T(8,128)(2,1)} copy-done((bf16[64,16,256]{2,0,1:T(8,128)(2,1)}, bf16[64,16,256]{2,0,1:T(8,128)(2,1)S(1)}, u32[]{:S(2)}) %copy-start.4) | copy-done | bytes 524312
  6.8 4.3 %collective-permute-start.1 = (bf16[5,64,256]{2,1,0:T(8,128)(2,1)S(1)}, bf16[5,64,256]{2,1,0:T(8,128)(2,1)S(1)}, u32[]{:S(2)}, u32[]{:S(2)}) collective-permute-start(bf16[5,64,256]{2,1,0:T(8,128)(2,1)S(1)} %pad_maximum_fusion.3), channel_id=1, source_target_pairs={{0,1},{1,2},{2,3},{3,4},{4,5},{5,6},{6,7},{8,9},{9,10},{10,11},{11... | collective-permute-start | bytes 491528 | tf_op jit(solution)/shard_map/ppermute | solution.py:349
  11.1 0.0 copy-start.1
  11.1 0.0 copy-start.3
  11.2 0.0 copy-start.5
  11.2 4.1 %shard_map.67 = (bf16[4,2880,256]{2,1,0:T(8,128)(2,1)S(1)}, bf16[2,4,256,256]{3,2,1,0:T(8,128)(2,1)S(1)}) custom-call(bf16[64,4,16,256]{3,2,1,0:T(8,128)(2,1)S(1)} %copy-done, bf16[256,2,8,128]{3,2,1,0:T(8,128)(2,1)S(1)} %copy-done.2), custom_call_target="tpu_custom_call" | custom-call | tf_op jit(solution)/shard_map/pallas_call | solution.py:390
  15.3 0.5 shard_map.68
  15.8 0.3 copy.9.hrow_ref
  16.1 0.0 collective-permute-done.1.hcol_ref
  16.1 2.2 %shard_map.69 = (bf16[4,2880,256]{2,1,0:T(8,128)(2,1)S(1)}, bf16[2,4,128,256]{3,2,1,0:T(8,128)(2,1)S(1)}, bf16[2,128,256]{2,1,0:T(8,128)(2,1)S(1)}, bf16[2,128,2...) custom-call(bf16[4,2880,256]{2,1,0:T(8,128)(2,1)S(1)} %get-tuple-element.48.own_ref, bf16[64,16,256]{2,1,0:T(8,128)(2,1)S(1)} %copy.9.hrow_ref, ...), custom_call_target="tpu_custom_call" | custom-call | tf_op jit(solution)/shard_map/pallas_call | solution.py:399
  18.3 0.2 collective-permute-start.4
  18.4 3.4 %collective-permute-start.2 = (bf16[2,128,256]{2,1,0:T(8,128)(2,1)S(1)}, bf16[2,128,256]{2,1,0:T(8,128)(2,1)S(1)}, u32[]{:S(2)}, u32[]{:S(2)}) collective-permute-start(bf16[2,128,256]{2,1,0:T(8,128)(2,1)S(1)} %get-tuple-element.50), channel_id=1, source_target_pairs={{0,1},{1,2},{2,3},{3,4},{4,5},{5,6},{6,7},{8,9},{9,10},{10,11},{11... | collective-permute-start | bytes 393224 | tf_op jit(solution)/shard_map/ppermute | solution.py:349
  21.9 1.5 %collective-permute-start.3 = (bf16[2,128,256]{2,1,0:T(8,128)(2,1)S(1)}, bf16[2,128,256]{2,1,0:T(8,128)(2,1)S(1)}, u32[]{:S(2)}, u32[]{:S(2)}) collective-permute-start(bf16[2,128,256]{2,1,0:T(8,128)(2,1)S(1)} %get-tuple-element.51), channel_id=1, source_target_pairs={{1,0},{2,1},{3,2},{4,3},{5,4},{6,5},{7,6},{9,8},{10,9},{11,10},{12... | collective-permute-start | bytes 393224 | tf_op jit(solution)/shard_map/ppermute | solution.py:349
  23.3 0.0 collective-permute-done.4.refs_1_
  23.4 4.4 %shard_map.70 = (bf16[2,4,768,256]{3,2,1,0:T(8,128)(2,1)S(1)}, bf16[2,2,256,256]{3,2,1,0:T(8,128)(2,1)S(1)}, f32[256,2304]{1,0:T(8,128)S(1)}, f32[2,4,256,256]{3,2,1,0:T(8,128)S(1)}) custom-call(bf16[2,4,128,256]{3,2,1,0:T(8,128)(2,1)S(1)} %get-tuple-element.52.refs_0_, bf16[2,4,128,256]{3,2,1,0:T(8,128)(2,1)S(1)} %collective-permute-done.4.refs_1_, ...), custom_call_target="tpu_custom_call" | custom-call | tf_op jit(solution)/shard_map/pallas_call | solution.py:422
  27.8 0.0 collective-permute-done.2.refs_2_
  27.8 2.0 %collective-permute-done.3.refs_3_ = bf16[2,128,256]{2,1,0:T(8,128)(2,1)S(1)} collective-permute-done((bf16[2,128,256]{2,1,0:T(8,128)(2,1)S(1)}, bf16[2,128,256]{2,1,0:T(8,128)(2,1)S(1)}, u32[]{:S(2)}, u32[]{:S(2)}) %collective-permute-start.3) | collective-permute-done | bytes 131104 | tf_op jit(solution)/shard_map/ppermute | solution.py:349
  29.8 0.0 collective-permute-start.5
  29.8 0.5 collective-permute-start.6
  30.3 0.8 %collective-permute-done.5.refs_4_ = bf16[2,128,256]{2,1,0:T(8,128)(2,1)S(1)} collective-permute-done((bf16[2,128,256]{2,1,0:T(8,128)(2,1)S(1)}, bf16[2,128,256]{2,1,0:T(8,128)(2,1)S(1)}, u32[]{:S(2)}, u32[]{:S(2)}) %collective-permute-start.5) | collective-permute-done | bytes 131104 | tf_op jit(solution)/shard_map/ppermute | solution.py:353
  31.2 0.2 collective-permute-done.6.refs_5_
  31.4 3.1 %shard_map.71 = (bf16[2,2,256,256]{3,2,1,0:T(8,128)(2,1)S(1)}, bf16[2,2,768,256]{3,2,1,0:T(8,128)(2,1)S(1)}, f32[8,16,1152]{2,1,0:T(8,128)S(1)}, bf16[8,16,1152]...) custom-call(s32[1]{0:T(128)} %bitcast.slab_ref.refs_0_, bf16[2,4,768,256]{3,2,1,0:T(8,128)(2,1)S(1)} %get-tuple-element.57.refs_1_, ...), custom_call_target="tpu_custom_call" | custom-call | tf_op jit(solution)/shard_map/pallas_call | solution.py:440
  34.4 0.4 collective-permute-start.7
  34.8 1.4 %shard_map.73 = (f32[2,4,128,256]{3,2,1,0:T(8,128)S(1)}, f32[2,2,128,256]{3,2,1,0:T(8,128)S(1)}, bf16[6,2,128,256]{3,2,1,0:T(8,128)(2,1)S(1)}) custom-call(bf16[2,2,768,256]{3,2,1,0:T(8,128)(2,1)S(1)} %get-tuple-element.74.rs_ref, bf16[256,2304]{1,0:T(8,128)(2,1)S(1)} %get-tuple-element.54.refs_3_.wg_ref, f32[2,4,256,256]{3,2,1,0:T(8,128)S(1)} %get-tuple-element.75.g_ref), custom_call_target="tpu_custom_call" | custom-call | tf_op jit(solution)/shard_map/pallas_call | solution.py:478
  36.2 0.3 collective-permute-start.11
  36.5 2.7 %collective-permute-start.14 = (bf16[4,32,1152]{2,1,0:T(8,128)(2,1)S(1)}, bf16[4,32,1152]{2,1,0:T(8,128)(2,1)S(1)}, u32[]{:S(2)}, u32[]{:S(2)}) collective-permute-start(bf16[4,32,1152]{2,1,0:T(8,128)(2,1)S(1)} %dynamic-slice_bitcast_fusion), channel_id=1, source_target_pairs={{0,1},{1,0},{2,3},{3,2},{4,5},{5,4},{6,7},{7,6},{8,9},{9,8},{10,11... | collective-permute-start | bytes 884744 | tf_op jit(solution)/shard_map/ppermute | solution.py:458
  39.2 1.6 %shard_map.72 = bf16[256,2,8,128]{3,2,1,0:T(8,128)(2,1)} custom-call(bf16[2,2,256,256]{3,2,1,0:T(8,128)(2,1)S(1)} %get-tuple-element.63.inner_ref, bf16[2,2,256,256]{3,2,1,0:T(8,128)(2,1)S(1)} %get-tuple-element.64.outer_ref), custom_call_target="tpu_custom_call" | custom-call | tf_op jit(solution)/shard_map/pallas_call | solution.py:494
  40.9 0.0 collective-permute-done.7
  40.9 0.1 add_convert_fusion.1
  40.9 0.0 collective-permute-done.11.gx_ref
  40.9 0.1 fusion.14
  41.0 1.3 %collective-permute-start.13 = (bf16[2,128,256]{2,1,0:T(8,128)(2,1)S(1)}, bf16[2,128,256]{2,1,0:T(8,128)(2,1)S(1)}, u32[]{:S(2)}, u32[]{:S(2)}) collective-permute-start(bf16[2,128,256]{2,1,0:T(8,128)(2,1)S(1)} %get-tuple-element.89), channel_id=1, source_target_pairs={{1,0},{2,1},{3,2},{4,3},{5,4},{6,5},{7,6},{9,8},{10,9},{11,10},{12... | collective-permute-start | bytes 393224 | tf_op jit(solution)/shard_map/ppermute | solution.py:349
  42.3 4.6 %collective-permute-start.12 = (bf16[2,128,256]{2,1,0:T(8,128)(2,1)S(1)}, bf16[2,128,256]{2,1,0:T(8,128)(2,1)S(1)}, u32[]{:S(2)}, u32[]{:S(2)}) collective-permute-start(bf16[2,128,256]{2,1,0:T(8,128)(2,1)S(1)} %get-tuple-element.90), channel_id=1, source_target_pairs={{0,1},{1,2},{2,3},{3,4},{4,5},{5,6},{6,7},{8,9},{9,10},{10,11},{11... | collective-permute-start | bytes 393224 | tf_op jit(solution)/shard_map/ppermute | solution.py:349
  46.9 1.6 %collective-permute-start.8 = (bf16[2,16,1152]{2,1,0:T(8,128)(2,1)S(1)}, bf16[2,16,1152]{2,1,0:T(8,128)(2,1)S(1)}, u32[]{:S(2)}, u32[]{:S(2)}) collective-permute-start(bf16[2,16,1152]{2,1,0:T(8,128)(2,1)S(1)} %get-tuple-element.98), channel_id=1, source_target_pairs={{0,2},{1,3},{2,4},{3,5},{4,6},{5,7},{6,0},{7,1},{8,10},{9,11},{10,... | collective-permute-start | bytes 221192 | tf_op jit(solution)/shard_map/ppermute | solution.py:462
  48.5 2.3 %collective-permute-start.10 = (bf16[2,16,1152]{2,1,0:T(8,128)(2,1)S(1)}, bf16[2,16,1152]{2,1,0:T(8,128)(2,1)S(1)}, u32[]{:S(2)}, u32[]{:S(2)}) collective-permute-start(bf16[2,16,1152]{2,1,0:T(8,128)(2,1)S(1)} %get-tuple-element.99), channel_id=1, source_target_pairs={{0,6},{1,7},{2,0},{3,1},{4,2},{5,3},{6,4},{7,5},{8,14},{9,15},{10,... | collective-permute-start | bytes 221192 | tf_op jit(solution)/shard_map/ppermute | solution.py:462
  50.8 0.0 collective-permute-done.14
  50.8 1.2 %collective-permute-start.9 = (bf16[2,16,1152]{2,1,0:T(8,128)(2,1)S(1)}, bf16[2,16,1152]{2,1,0:T(8,128)(2,1)S(1)}, u32[]{:S(2)}, u32[]{:S(2)}) collective-permute-start(bf16[2,16,1152]{2,1,0:T(8,128)(2,1)S(1)} %get-tuple-element.100), channel_id=1, source_target_pairs={{0,4},{1,5},{2,6},{3,7},{4,0},{5,1},{6,2},{7,3},{8,12},{9,13},{10,... | collective-permute-start | bytes 221192 | tf_op jit(solution)/shard_map/ppermute | solution.py:462
  52.0 1.2 %shard_map.74.sum_ref = f32[128,1728]{1,0:T(8,128)S(1)} custom-call(f32[2,4,128,256]{3,2,1,0:T(8,128)S(1)} %get-tuple-element.76.gown_ref, bf16[6,2,128,256]{3,2,1,0:T(8,128)(2,1)S(1)} %collective-permute-done.11.gx_ref, f32[2,4,128,256]{3,2,1,0:T(8,128)S(1)} %get-tuple-element.81.slope_ref, bf16[4,2880,256]{2,1,0:T(8,128)(2,1)S(1)} %get-tuple-element.82.vp_ref), custom_call_target="tpu_custom_call" | custom-call | tf_op jit(solution)/shard_map/pallas_call | solution.py:500
  53.1 0.0 collective-permute-done.13.gr_ref
  53.1 1.2 %shard_map.75 = (f32[8,16,1152]{2,1,0:T(8,128)S(1)}, bf16[8,16,1152]{2,1,0:T(8,128)(2,1)S(1)}) custom-call(s32[1]{0:T(128)} %bitcast.slab_ref.refs_0_, f32[2,4,128,256]{3,2,1,0:T(8,128)S(1)} %get-tuple-element.76.gown_ref, bf16[6,2,128,256]{3,2,1,0:T(8,128)(2,1)S(1)} %collective-permute-done.11.gx_ref, ...), custom_call_target="tpu_custom_call" | custom-call | tf_op jit(solution)/shard_map/pallas_call | solution.py:508
  54.3 0.1 collective-permute-start.15
  54.4 0.0 collective-permute-done.10
  54.4 2.7 %collective-permute-done.9 = bf16[2,16,1152]{2,1,0:T(8,128)(2,1)S(1)} collective-permute-done((bf16[2,16,1152]{2,1,0:T(8,128)(2,1)S(1)}, bf16[2,16,1152]{2,1,0:T(8,128)(2,1)S(1)}, u32[]{:S(2)}, u32[]{:S(2)}) %collective-permute-start.9) | collective-permute-done | bytes 73760 | tf_op jit(solution)/shard_map/ppermute | solution.py:462
  57.2 0.1 add_convert_fusion
  57.3 1.4 %collective-permute-start.16 = (bf16[80,1152]{1,0:T(8,128)(2,1)S(1)}, bf16[80,1152]{1,0:T(8,128)(2,1)S(1)}, u32[]{:S(2)}, u32[]{:S(2)}) collective-permute-start(bf16[80,1152]{1,0:T(8,128)(2,1)S(1)} %pad_maximum_fusion.2), channel_id=1, source_target_pairs={{0,1},{1,0},{2,3},{3,2},{4,5},{5,4},{6,7},{7,6},{8,9},{9,8},{10,11... | collective-permute-start | bytes 552968 | tf_op jit(solution)/shard_map/ppermute | solution.py:458
  58.7 0.1 convert_add_fusion
  58.8 4.8 %collective-permute-done.16 = bf16[80,1152]{1,0:T(8,128)(2,1)S(1)} collective-permute-done((bf16[80,1152]{1,0:T(8,128)(2,1)S(1)}, bf16[80,1152]{1,0:T(8,128)(2,1)S(1)}, u32[]{:S(2)}, u32[]{:S(2)}) %collective-permute-start.16) | collective-permute-done | bytes 184352 | tf_op jit(solution)/shard_map/ppermute | solution.py:458
  63.7 0.1 fusion.16
  63.7 0.1 collective-permute-start.17
  63.8 3.4 %collective-permute-start.18 = (bf16[48,1152]{1,0:T(8,128)(2,1)S(1)}, bf16[48,1152]{1,0:T(8,128)(2,1)S(1)}, u32[]{:S(2)}, u32[]{:S(2)}) collective-permute-start(bf16[48,1152]{1,0:T(8,128)(2,1)S(1)} %get-tuple-element.92), channel_id=1, source_target_pairs={{0,4},{1,5},{2,6},{3,7},{4,0},{5,1},{6,2},{7,3},{8,12},{9,13},{10,... | collective-permute-start | bytes 331784 | tf_op jit(solution)/shard_map/ppermute | solution.py:462
  67.2 1.0 %collective-permute-start.19 = (bf16[48,1152]{1,0:T(8,128)(2,1)S(1)}, bf16[48,1152]{1,0:T(8,128)(2,1)S(1)}, u32[]{:S(2)}, u32[]{:S(2)}) collective-permute-start(bf16[48,1152]{1,0:T(8,128)(2,1)S(1)} %get-tuple-element.93), channel_id=1, source_target_pairs={{0,6},{1,7},{2,0},{3,1},{4,2},{5,3},{6,4},{7,5},{8,14},{9,15},{10,... | collective-permute-start | bytes 331784 | tf_op jit(solution)/shard_map/ppermute | solution.py:462
  68.3 3.3 %collective-permute-done.17 = bf16[48,1152]{1,0:T(8,128)(2,1)S(1)} collective-permute-done((bf16[48,1152]{1,0:T(8,128)(2,1)S(1)}, bf16[48,1152]{1,0:T(8,128)(2,1)S(1)}, u32[]{:S(2)}, u32[]{:S(2)}) %collective-permute-start.17) | collective-permute-done | bytes 110624 | tf_op jit(solution)/shard_map/ppermute | solution.py:462
  71.6 2.6 %collective-permute-done.18 = bf16[48,1152]{1,0:T(8,128)(2,1)S(1)} collective-permute-done((bf16[48,1152]{1,0:T(8,128)(2,1)S(1)}, bf16[48,1152]{1,0:T(8,128)(2,1)S(1)}, u32[]{:S(2)}, u32[]{:S(2)}) %collective-permute-start.18) | collective-permute-done | bytes 110624 | tf_op jit(solution)/shard_map/ppermute | solution.py:462
  74.2 0.1 collective-permute-done.19
  74.3 0.1 fusion.6
  74.4 0.1 collective-permute-start.20
  74.4 1.6 %collective-permute-done.20 = f32[64,1152]{1,0:T(8,128)S(1)} collective-permute-done((f32[64,1152]{1,0:T(8,128)S(1)}, f32[64,1152]{1,0:T(8,128)S(1)}, u32[]{:S(2)}, u32[]{:S(2)}) %collective-permute-start.20) | collective-permute-done | bytes 294944 | tf_op jit(solution)/shard_map/ppermute | solution.py:353
  76.1 0.7 pad_maximum_fusion.4
  76.8 0.8 %pad_maximum_fusion = f32[32,3456]{1,0:T(8,128)} fusion(f32[32,1152]{1,0:T(8,128)S(1)} %slice.70, f32[16,1152]{1,0:T(8,128)S(1)} %slice.69, f32[16,1152]{1,0:T(8,128)S(1)} %get-tuple-element.96, f32[32,1152]{1,0:T(8,128)S(1)} %slice.67), kind=kLoop, calls=%fused_computation.12 | loop fusion | flops 331776 | bytes 884736 | tf_op jit(solution)/shard_map/concatenate | solution.py:533
  (31 shorter events, 0.4 us)
Async XLA Ops:
  0.6 3.8 %copy-start = (bf16[64,4,16,256]{3,2,1,0:T(8,128)(2,1)S(1)}, bf16[64,4,16,256]{3,2,1,0:T(8,128)(2,1)}, u32[]{:S(2)}) copy-start(bf16[64,4,16,256]{3,2,1,0:T(8,128)(2,1)} %vol_ref.1) | copy-start | bytes 6291460
  0.6 10.5 %copy-start.2 = (bf16[256,2,8,128]{3,2,1,0:T(8,128)(2,1)S(1)}, bf16[256,2,8,128]{3,2,1,0:T(8,128)(2,1)}, u32[]{:S(2)}) copy-start(bf16[256,2,8,128]{3,2,1,0:T(8,128)(2,1)} %tgt_ref) | copy-start | bytes 3145732
  2.1 3.9 %collective-permute-start = (bf16[64,16,256]{2,0,1:T(8,128)(2,1)S(1)}, bf16[64,16,256]{2,0,1:T(8,128)(2,1)S(1)}, u32[]{:S(2)}, u32[]{:S(2)}) collective-permute-start(bf16[64,16,256]{2,0,1:T(8,128)(2,1)S(1)} %bitcast.70), channel_id=1, source_target_pairs={{0,8},{1,9},{2,10},{3,11},{4,12},{5,13},{6,14},{7,15},{16,24},{17,... | collective-permute-start | bytes 1572872 | tf_op jit(solution)/shard_map/ppermute | solution.py:349
  5.9 0.8 %copy-start.4 = (bf16[64,16,256]{2,0,1:T(8,128)(2,1)}, bf16[64,16,256]{2,0,1:T(8,128)(2,1)S(1)}, u32[]{:S(2)}) copy-start(bf16[64,16,256]{2,0,1:T(8,128)(2,1)S(1)} %collective-permute-done) | copy-start | bytes 1572868
  6.8 9.3 %collective-permute-start.1 = (bf16[5,64,256]{2,1,0:T(8,128)(2,1)S(1)}, bf16[5,64,256]{2,1,0:T(8,128)(2,1)S(1)}, u32[]{:S(2)}, u32[]{:S(2)}) collective-permute-start(bf16[5,64,256]{2,1,0:T(8,128)(2,1)S(1)} %pad_maximum_fusion.3), channel_id=1, source_target_pairs={{0,1},{1,2},{2,3},{3,4},{4,5},{5,6},{6,7},{8,9},{9,10},{10,11},{11... | collective-permute-start | bytes 491528 | tf_op jit(solution)/shard_map/ppermute | solution.py:349
  11.1 4.1 %copy-start.1 = (bf16[256,3456]{1,0:T(8,128)(2,1)S(1)}, bf16[256,3456]{1,0:T(8,128)(2,1)}, u32[]{:S(2)}) copy-start(bf16[256,3456]{1,0:T(8,128)(2,1)} %wd_ref.1) | copy-start | bytes 5308420
  11.1 4.1 %copy-start.3 = (bf16[128,1728]{0,1:T(8,128)(2,1)S(1)}, bf16[128,1728]{0,1:T(8,128)(2,1)}, u32[]{:S(2)}) copy-start(bf16[128,1728]{0,1:T(8,128)(2,1)} %param.6) | copy-start | bytes 1327108
  11.2 4.6 %copy-start.5 = (bf16[64,16,256]{2,0,1:T(8,128)(2,1)S(1)}, bf16[64,16,256]{2,0,1:T(8,128)(2,1)}, u32[]{:S(2)}) copy-start(bf16[64,16,256]{2,0,1:T(8,128)(2,1)} %copy-done.4) | copy-start | bytes 1572868
  18.3 5.1 %collective-permute-start.4 = (bf16[2,4,128,256]{3,2,1,0:T(8,128)(2,1)S(1)}, bf16[2,4,128,256]{3,2,1,0:T(8,128)(2,1)S(1)}, u32[]{:S(2)}, u32[]{:S(2)}) collective-permute-start(bf16[2,4,128,256]{3,2,1,0:T(8,128)(2,1)S(1)} %get-tuple-element.52.refs_0_), channel_id=1, source_target_pairs={{0,8},{8,0},{1,9},{9,1},{2,10},{10,2},{3,11},{11,3},{4,12},{12,4},... | collective-permute-start | bytes 1572872 | tf_op jit(solution)/shard_map/ppermute | solution.py:353
  18.4 9.3 %collective-permute-start.2 = (bf16[2,128,256]{2,1,0:T(8,128)(2,1)S(1)}, bf16[2,128,256]{2,1,0:T(8,128)(2,1)S(1)}, u32[]{:S(2)}, u32[]{:S(2)}) collective-permute-start(bf16[2,128,256]{2,1,0:T(8,128)(2,1)S(1)} %get-tuple-element.50), channel_id=1, source_target_pairs={{0,1},{1,2},{2,3},{3,4},{4,5},{5,6},{6,7},{8,9},{9,10},{10,11},{11... | collective-permute-start | bytes 393224 | tf_op jit(solution)/shard_map/ppermute | solution.py:349
  21.9 8.0 %collective-permute-start.3 = (bf16[2,128,256]{2,1,0:T(8,128)(2,1)S(1)}, bf16[2,128,256]{2,1,0:T(8,128)(2,1)S(1)}, u32[]{:S(2)}, u32[]{:S(2)}) collective-permute-start(bf16[2,128,256]{2,1,0:T(8,128)(2,1)S(1)} %get-tuple-element.51), channel_id=1, source_target_pairs={{1,0},{2,1},{3,2},{4,3},{5,4},{6,5},{7,6},{9,8},{10,9},{11,10},{12... | collective-permute-start | bytes 393224 | tf_op jit(solution)/shard_map/ppermute | solution.py:349
  29.8 1.3 %collective-permute-start.5 = (bf16[2,128,256]{2,1,0:T(8,128)(2,1)S(1)}, bf16[2,128,256]{2,1,0:T(8,128)(2,1)S(1)}, u32[]{:S(2)}, u32[]{:S(2)}) collective-permute-start(bf16[2,128,256]{2,1,0:T(8,128)(2,1)S(1)} %collective-permute-done.2.refs_2_), channel_id=1, source_target_pairs={{0,8},{8,0},{1,9},{9,1},{2,10},{10,2},{3,11},{11,3},{4,12},{12,4},... | collective-permute-start | bytes 393224 | tf_op jit(solution)/shard_map/ppermute | solution.py:353
  29.8 1.5 %collective-permute-start.6 = (bf16[2,128,256]{2,1,0:T(8,128)(2,1)S(1)}, bf16[2,128,256]{2,1,0:T(8,128)(2,1)S(1)}, u32[]{:S(2)}, u32[]{:S(2)}) collective-permute-start(bf16[2,128,256]{2,1,0:T(8,128)(2,1)S(1)} %collective-permute-done.3.refs_3_), channel_id=1, source_target_pairs={{0,8},{8,0},{1,9},{9,1},{2,10},{10,2},{3,11},{11,3},{4,12},{12,4},... | collective-permute-start | bytes 393224 | tf_op jit(solution)/shard_map/ppermute | solution.py:353
  34.4 6.4 %collective-permute-start.7 = (bf16[8,16,1152]{2,1,0:T(8,128)(2,1)S(1)}, bf16[8,16,1152]{2,1,0:T(8,128)(2,1)S(1)}, u32[]{:S(2)}, u32[]{:S(2)}) collective-permute-start(bf16[8,16,1152]{2,1,0:T(8,128)(2,1)S(1)} %get-tuple-element.62), channel_id=1, source_target_pairs={{0,8},{8,0},{1,9},{9,1},{2,10},{10,2},{3,11},{11,3},{4,12},{12,4},... | collective-permute-start | bytes 884744 | tf_op jit(solution)/shard_map/ppermute | solution.py:353
  36.2 4.7 %collective-permute-start.11 = (bf16[6,2,128,256]{3,2,1,0:T(8,128)(2,1)S(1)}, bf16[6,2,128,256]{3,2,1,0:T(8,128)(2,1)S(1)}, u32[]{:S(2)}, u32[]{:S(2)}) collective-permute-start(bf16[6,2,128,256]{3,2,1,0:T(8,128)(2,1)S(1)} %get-tuple-element.77), channel_id=1, source_target_pairs={{0,8},{8,0},{1,9},{9,1},{2,10},{10,2},{3,11},{11,3},{4,12},{12,4},... | collective-permute-start | bytes 2359304 | tf_op jit(solution)/shard_map/ppermute | solution.py:353
  36.5 14.3 %collective-permute-start.14 = (bf16[4,32,1152]{2,1,0:T(8,128)(2,1)S(1)}, bf16[4,32,1152]{2,1,0:T(8,128)(2,1)S(1)}, u32[]{:S(2)}, u32[]{:S(2)}) collective-permute-start(bf16[4,32,1152]{2,1,0:T(8,128)(2,1)S(1)} %dynamic-slice_bitcast_fusion), channel_id=1, source_target_pairs={{0,1},{1,0},{2,3},{3,2},{4,5},{5,4},{6,7},{7,6},{8,9},{9,8},{10,11... | collective-permute-start | bytes 884744 | tf_op jit(solution)/shard_map/ppermute | solution.py:458
  41.0 12.1 %collective-permute-start.13 = (bf16[2,128,256]{2,1,0:T(8,128)(2,1)S(1)}, bf16[2,128,256]{2,1,0:T(8,128)(2,1)S(1)}, u32[]{:S(2)}, u32[]{:S(2)}) collective-permute-start(bf16[2,128,256]{2,1,0:T(8,128)(2,1)S(1)} %get-tuple-element.89), channel_id=1, source_target_pairs={{1,0},{2,1},{3,2},{4,3},{5,4},{6,5},{7,6},{9,8},{10,9},{11,10},{12... | collective-permute-start | bytes 393224 | tf_op jit(solution)/shard_map/ppermute | solution.py:349
  42.3 10.8 %collective-permute-start.12 = (bf16[2,128,256]{2,1,0:T(8,128)(2,1)S(1)}, bf16[2,128,256]{2,1,0:T(8,128)(2,1)S(1)}, u32[]{:S(2)}, u32[]{:S(2)}) collective-permute-start(bf16[2,128,256]{2,1,0:T(8,128)(2,1)S(1)} %get-tuple-element.90), channel_id=1, source_target_pairs={{0,1},{1,2},{2,3},{3,4},{4,5},{5,6},{6,7},{8,9},{9,10},{10,11},{11... | collective-permute-start | bytes 393224 | tf_op jit(solution)/shard_map/ppermute | solution.py:349
  46.9 7.5 %collective-permute-start.8 = (bf16[2,16,1152]{2,1,0:T(8,128)(2,1)S(1)}, bf16[2,16,1152]{2,1,0:T(8,128)(2,1)S(1)}, u32[]{:S(2)}, u32[]{:S(2)}) collective-permute-start(bf16[2,16,1152]{2,1,0:T(8,128)(2,1)S(1)} %get-tuple-element.98), channel_id=1, source_target_pairs={{0,2},{1,3},{2,4},{3,5},{4,6},{5,7},{6,0},{7,1},{8,10},{9,11},{10,... | collective-permute-start | bytes 221192 | tf_op jit(solution)/shard_map/ppermute | solution.py:462
  48.5 5.9 %collective-permute-start.10 = (bf16[2,16,1152]{2,1,0:T(8,128)(2,1)S(1)}, bf16[2,16,1152]{2,1,0:T(8,128)(2,1)S(1)}, u32[]{:S(2)}, u32[]{:S(2)}) collective-permute-start(bf16[2,16,1152]{2,1,0:T(8,128)(2,1)S(1)} %get-tuple-element.99), channel_id=1, source_target_pairs={{0,6},{1,7},{2,0},{3,1},{4,2},{5,3},{6,4},{7,5},{8,14},{9,15},{10,... | collective-permute-start | bytes 221192 | tf_op jit(solution)/shard_map/ppermute | solution.py:462
  50.8 6.4 %collective-permute-start.9 = (bf16[2,16,1152]{2,1,0:T(8,128)(2,1)S(1)}, bf16[2,16,1152]{2,1,0:T(8,128)(2,1)S(1)}, u32[]{:S(2)}, u32[]{:S(2)}) collective-permute-start(bf16[2,16,1152]{2,1,0:T(8,128)(2,1)S(1)} %get-tuple-element.100), channel_id=1, source_target_pairs={{0,4},{1,5},{2,6},{3,7},{4,0},{5,1},{6,2},{7,3},{8,12},{9,13},{10,... | collective-permute-start | bytes 221192 | tf_op jit(solution)/shard_map/ppermute | solution.py:462
  54.3 2.9 %collective-permute-start.15 = (bf16[8,16,1152]{2,1,0:T(8,128)(2,1)S(1)}, bf16[8,16,1152]{2,1,0:T(8,128)(2,1)S(1)}, u32[]{:S(2)}, u32[]{:S(2)}) collective-permute-start(bf16[8,16,1152]{2,1,0:T(8,128)(2,1)S(1)} %get-tuple-element.87), channel_id=1, source_target_pairs={{0,8},{8,0},{1,9},{9,1},{2,10},{10,2},{3,11},{11,3},{4,12},{12,4},... | collective-permute-start | bytes 884744 | tf_op jit(solution)/shard_map/ppermute | solution.py:353
  57.3 6.2 %collective-permute-start.16 = (bf16[80,1152]{1,0:T(8,128)(2,1)S(1)}, bf16[80,1152]{1,0:T(8,128)(2,1)S(1)}, u32[]{:S(2)}, u32[]{:S(2)}) collective-permute-start(bf16[80,1152]{1,0:T(8,128)(2,1)S(1)} %pad_maximum_fusion.2), channel_id=1, source_target_pairs={{0,1},{1,0},{2,3},{3,2},{4,5},{5,4},{6,7},{7,6},{8,9},{9,8},{10,11... | collective-permute-start | bytes 552968 | tf_op jit(solution)/shard_map/ppermute | solution.py:458
  63.7 7.9 %collective-permute-start.17 = (bf16[48,1152]{1,0:T(8,128)(2,1)S(1)}, bf16[48,1152]{1,0:T(8,128)(2,1)S(1)}, u32[]{:S(2)}, u32[]{:S(2)}) collective-permute-start(bf16[48,1152]{1,0:T(8,128)(2,1)S(1)} %get-tuple-element.91), channel_id=1, source_target_pairs={{0,2},{1,3},{2,4},{3,5},{4,6},{5,7},{6,0},{7,1},{8,10},{9,11},{10,... | collective-permute-start | bytes 331784 | tf_op jit(solution)/shard_map/ppermute | solution.py:462
  63.8 10.4 %collective-permute-start.18 = (bf16[48,1152]{1,0:T(8,128)(2,1)S(1)}, bf16[48,1152]{1,0:T(8,128)(2,1)S(1)}, u32[]{:S(2)}, u32[]{:S(2)}) collective-permute-start(bf16[48,1152]{1,0:T(8,128)(2,1)S(1)} %get-tuple-element.92), channel_id=1, source_target_pairs={{0,4},{1,5},{2,6},{3,7},{4,0},{5,1},{6,2},{7,3},{8,12},{9,13},{10,... | collective-permute-start | bytes 331784 | tf_op jit(solution)/shard_map/ppermute | solution.py:462
  67.2 7.1 %collective-permute-start.19 = (bf16[48,1152]{1,0:T(8,128)(2,1)S(1)}, bf16[48,1152]{1,0:T(8,128)(2,1)S(1)}, u32[]{:S(2)}, u32[]{:S(2)}) collective-permute-start(bf16[48,1152]{1,0:T(8,128)(2,1)S(1)} %get-tuple-element.93), channel_id=1, source_target_pairs={{0,6},{1,7},{2,0},{3,1},{4,2},{5,3},{6,4},{7,5},{8,14},{9,15},{10,... | collective-permute-start | bytes 331784 | tf_op jit(solution)/shard_map/ppermute | solution.py:462
  74.4 1.6 %collective-permute-start.20 = (f32[64,1152]{1,0:T(8,128)S(1)}, f32[64,1152]{1,0:T(8,128)S(1)}, u32[]{:S(2)}, u32[]{:S(2)}) collective-permute-start(f32[64,1152]{1,0:T(8,128)S(1)} %pad_maximum_fusion.1), channel_id=1, source_target_pairs={{0,8},{8,0},{1,9},{9,1},{2,10},{10,2},{3,11},{11,3},{4,12},{12,4},... | collective-permute-start | bytes 884744 | tf_op jit(solution)/shard_map/ppermute | solution.py:353

commit v6 on v5

--- a/solution.py
+++ b/solution.py
@@ -14,13 +14,14 @@
 VMEM_LIMIT = 20 * 1024 * 1024
 
 
-def vmem_call(body, out_shape, n_in, scratch=(), scalars=0):
+def vmem_call(body, out_shape, n_in, scratch=(), scalars=0, in_hbm=0):
     spec = pl.BlockSpec(memory_space=pltpu.VMEM)
     scalar = pl.BlockSpec(memory_space=pltpu.SMEM)
+    hbm = pl.BlockSpec(memory_space=pltpu.HBM)
     return pl.pallas_call(
         body,
         out_shape=out_shape,
-        in_specs=[scalar] * scalars + [spec] * n_in,
+        in_specs=[scalar] * scalars + [hbm] * in_hbm + [spec] * n_in,
         out_specs=jax.tree.map(lambda _: spec, out_shape),
         scratch_shapes=list(scratch),
         compiler_params=pltpu.CompilerParams(vmem_limit_bytes=VMEM_LIMIT),
@@ -60,14 +61,29 @@
                 vp_ref[rest // 4, start : start + channels, h * half : (h + 1) * half] = taps[c]
 
 
-def split_body(vol_ref, tgt_ref, vp_ref, tp_ref, wide_ref, tall_ref):
+def edge_body(vol_ref, edge_ref, half_ref, sem):
+    channels, rows, cols, depth = vol_ref.shape
+    count = half_ref.shape[2]
+    copy = pltpu.make_async_copy(vol_ref.at[:, :, cols - count :], half_ref, sem)
+    copy.start()
+    channel = lax.broadcasted_iota(jnp.int32, (channels, channels * count), 0)
+    source = lax.broadcasted_iota(jnp.int32, (channels, channels * count), 1)
+    last = jnp.where(source == channel * count + count - 1, 1.0, 0.0).astype(BF16)
+    copy.wait()
+    for row in range(rows):
+        plane = half_ref[:, row].astype(F32).reshape(channels * count, depth).astype(BF16)
+        edge_ref[row] = jnp.dot(last, plane, preferred_element_type=F32).astype(BF16)
+
+
+def split_body(vol_ref, vp_ref, last_ref, wide_ref):
     channels, rows, cols, depth = vol_ref.shape
     pairs = cols // 4
-    half = depth // 2
     pick = selection(depth)
     for row in range(rows):
         slot = row % 2
         plane = vol_ref[:, row].reshape(channels * cols, depth)
+        if row == rows - 1:
+            last_ref[...] = plane
         spread(plane, pick, wide_ref.at[slot])
         for col in range(cols):
             values = [
@@ -75,7 +91,10 @@
                 for k in range(3)
             ]
             put_column(vp_ref, values, channels, row + 1, col, pairs)
-    outs, orows, ocols, _ = tgt_ref.shape
+
+
+def target_body(tgt_ref, tp_ref, tall_ref):
+    outs, orows, ocols, half = tgt_ref.shape
     for row in range(orows):
         slot = row % 2
         tall_ref[slot] = tgt_ref[:, row].astype(F32).reshape(outs * ocols, half)
@@ -85,19 +104,21 @@
 
 
 def preact_body(own_ref, hrow_ref, hcol_ref, w_ref, vp_ref, h_ref, hl_ref, hr_ref, slope_ref, wide_ref):
-    channels, cols, depth = hrow_ref.shape
-    rows_ext = hcol_ref.shape[0]
+    rows_in, channels, depth = hcol_ref.shape
+    size = hrow_ref.shape[0] - channels
+    cols = size // channels
     orows, pairs, _, _ = h_ref.shape
     vp_ref[:, 9 * channels :] = own_ref[:, 9 * channels :]
     pick = selection(depth)
-    spread(hrow_ref[...].reshape(channels * cols, depth), pick, wide_ref)
+    spread(hrow_ref[:size], pick, wide_ref)
     for col in range(cols):
         values = [
             wide_ref[k, pl.ds(col, channels, stride=cols), :].astype(BF16) for k in range(3)
         ]
         put_column(vp_ref, values, channels, 0, col, pairs)
-    for row in range(rows_ext):
-        values = jnp.dot(hcol_ref[row], pick, preferred_element_type=F32).astype(BF16)
+    for row in range(rows_in + 1):
+        plane = hrow_ref[size:] if row == 0 else hcol_ref[row - 1]
+        values = jnp.dot(plane, pick, preferred_element_type=F32).astype(BF16)
         put_column(vp_ref, thirds(values), channels, row, -1, pairs)
     plane = 9 * channels
     for i in range(orows):
@@ -214,22 +235,18 @@
 
 
 def outer_body(
-    scale, step, slab_ref, hs_ref, hl_ref, hr_ref, ol_ref, or_ref, w2_ref, tp_ref, dg_ref,
-    pred_ref, rs_ref, mine_ref, send_ref, other_ref, edge_ref,
+    scale, step, hs_ref, hl_ref, hr_ref, ol_ref, or_ref, w2_ref, wg_ref, tp_ref, g_ref,
+    pred_ref, res_ref, edge_ref, gown_ref, ghalo_ref, gother_ref, gedge_ref, rs_ref,
 ):
     orows, pairs, depth, lanes = hs_ref.shape
     mid = depth // 6
     outs = w2_ref.shape[0]
+    block = 3 * outs
     ends = (0, pairs - 1)
     for r in range(orows):
         for k, (own, other) in enumerate(((hl_ref, ol_ref), (hr_ref, or_ref))):
             put_window(edge_ref, (r, k), own[r], 0, step)
             put_window(edge_ref, (r, k), other[r], 3 * mid, step)
-
-    def taps(r, m, b):
-        x = m - 1 + b
-        return edge_ref.at[r, 0] if x < 0 else edge_ref.at[r, 1] if x == pairs else hs_ref.at[r, x]
-
     for r in range(orows):
         for k, m in enumerate(ends):
             edge = edge_ref[r, k]
@@ -240,6 +257,37 @@
             out = jnp.dot(w_edge, edge, preferred_element_type=F32)
             out = out + jnp.dot(w_near, near, preferred_element_type=F32)
             put_residual(out, tp_ref[r, m], scale, step, pred_ref, rs_ref, (r, k))
+            res_ref[r, k] = rs_ref[r, k, outs : 2 * outs]
+    for r in range(orows):
+        for x in range(pairs + 2):
+            parts = [g_ref[r, x - 1]] if 0 < x <= pairs else []
+            for k, m in enumerate(ends):
+                tap = m - (x - 2)
+                if 0 <= tap < 3:
+                    weights = wg_ref[:, tap * block : (tap + 1) * block]
+                    parts.append(jnp.dot(weights, rs_ref[r, k], preferred_element_type=F32))
+            grad = added(parts)
+            apart = grad[mid:].astype(BF16)
+            if 0 < x <= pairs:
+                gother_ref[r, x - 1] = apart
+            else:
+                gedge_ref[x // (pairs + 1), r] = apart
+            if x == 0:
+                ghalo_ref[0, r] = grad[:mid]
+            elif x == pairs + 1:
+                ghalo_ref[1, r] = grad[:mid]
+            else:
+                gown_ref[r, x - 1] = grad[:mid]
+
+
+def dilated_grad_body(slab_ref, res_ref, hs_ref, edge_ref, dg_ref, mine_ref, send_ref, other_ref):
+    orows, pairs, depth, _ = hs_ref.shape
+    mid = depth // 6
+
+    def taps(r, m, b):
+        x = m - 1 + b
+        return edge_ref.at[r, 0] if x < 0 else edge_ref.at[r, 1] if x == pairs else hs_ref.at[r, x]
+
     for b in range(3):
         columns = slice(b * 3 * mid, (b + 1) * 3 * mid)
         for src in range(2):
@@ -247,11 +295,10 @@
             at = (b * 2 + src) * 3 * mid
             total = dg_ref[:, at : at + 3 * mid] + added(
                 lax.dot_general(
-                    rs_ref[r, k, outs : 2 * outs], taps(r, m, b)[rows], NT,
-                    preferred_element_type=F32,
+                    res_ref[r, k], taps(r, m, b)[rows], NT, preferred_element_type=F32
                 )
                 for r in range(orows)
-                for k, m in enumerate(ends)
+                for k, m in enumerate((0, pairs - 1))
             )
             if src == 0:
                 split_rows(slab_ref, total, mine_ref, send_ref, columns)
@@ -260,27 +307,6 @@
                 other_ref[:, :, columns] = total.reshape(strips, count, 3 * mid).astype(BF16)
 
 
-def hidden_grad_body(rs_ref, wg_ref, g_ref, gown_ref, ghalo_ref, gother_ref):
-    orows, _, block, lanes = rs_ref.shape
-    pairs, mid = gown_ref.shape[1:3]
-    for r in range(orows):
-        for x in range(pairs + 2):
-            parts = [g_ref[r, x - 1]] if 0 < x <= pairs else []
-            for k, m in enumerate((0, pairs - 1)):
-                tap = m - (x - 2)
-                if 0 <= tap < 3:
-                    weights = wg_ref[:, tap * block : (tap + 1) * block]
-                    parts.append(jnp.dot(weights, rs_ref[r, k], preferred_element_type=F32))
-            grad = added(parts)
-            gother_ref[x, r] = grad[mid:].astype(BF16)
-            if x == 0:
-                ghalo_ref[0, r] = grad[:mid]
-            elif x == pairs + 1:
-                ghalo_ref[1, r] = grad[:mid]
-            else:
-                gown_ref[r, x - 1] = grad[:mid]
-
-
 def split_rows(slab_ref, total, mine_ref, send_ref, columns):
     strips, rows, _ = mine_ref.shape
     parts = total.reshape(strips, 2, rows, total.shape[1])
@@ -294,7 +320,7 @@
     plane = vp_ref.shape[1] // (2 * orows + 1)
 
     def part(i, m):
-        grad = gown_ref[i, m] + gx_ref[m + 1, i].astype(F32)
+        grad = gown_ref[i, m] + gx_ref[i, m].astype(F32)
         if m in extra:
             grad = grad + extra[m][i].astype(F32)
         pg = (grad * slope_ref[i, m]).astype(BF16)
@@ -365,7 +391,14 @@
     groups = strips // 2
     place, parity = strip // 2, strip % 2
     scalars = (slab == 0, slab, parity, 1 - parity, *((place + d) % groups for d in range(groups)))
-    target, scalars = lax.optimization_barrier((target, scalars))
+    edge = vmem_call(
+        edge_body,
+        sds((rows_in, channels, depth), BF16),
+        0,
+        [VMEM((channels, rows_in, min(8, cols_in), depth), BF16), pltpu.SemaphoreType.DMA(())],
+        in_hbm=1,
+    )(volume)
+    edge, scalars = lax.optimization_barrier((edge, scalars))
     first, slab, parity, other_parity, *places = scalars
     slab_id = slab.reshape(1).astype(jnp.int32)
     step = 2
@@ -373,9 +406,18 @@
     cells = orows * ocols * half * lax.axis_size("slab") * strips
     scale = 1.0 / math.sqrt(cells)
 
-    lower = shift_along(volume[:, -1], "slab", 1)
-    last = jnp.concatenate([lower[None, :, -1, :], volume[:, :, -1, :].transpose(1, 0, 2)], axis=0)
-    left = shift_along(last, "strip", 1)
+    left = shift_along(edge, "strip", 1)
+    vp, plane = vmem_call(
+        split_body,
+        (
+            sds((pairs, (rows_in + 1) * 9 * channels, lanes), BF16),
+            sds((channels * cols_in, depth), BF16),
+        ),
+        1,
+        [VMEM((2, 3, channels * cols_in, half), F32)],
+    )(volume)
+    left, vp, plane = lax.optimization_barrier((left, vp, plane))
+    lower = shift_along(jnp.concatenate([plane, left[-1]], axis=0), "slab", 1)
 
     w2, wg, ws = vmem_call(
         weights_body,
@@ -387,15 +429,12 @@
         2,
         scalars=1,
     )(slab_id, dilated_weight, strided_weight.T)
-    vp, tp = vmem_call(
-        split_body,
-        (
-            sds((pairs, (rows_in + 1) * 9 * channels, lanes), BF16),
-            sds((orows, pairs, outs, lanes), BF16),
-        ),
-        2,
-        [VMEM((2, 3, channels * cols_in, half), F32), VMEM((2, outs * ocols, half), F32)],
-    )(volume, target)
+    tp = vmem_call(
+        target_body,
+        sds((orows, pairs, outs, lanes), BF16),
+        1,
+        [VMEM((2, outs * ocols, half), F32)],
+    )(target)
     vp, hidden, hid_l, hid_r, slope = vmem_call(
         preact_body,
         (
@@ -435,21 +474,40 @@
     other_left = swap(from_left)
     other_right = swap(from_right)
 
-    rows = outs // strips
-    half_rows = rows // 2
-    pred_out, residual, mine, send, apart = vmem_call(
+    pred_out, residual, edges, gown, ghalo, gother, gedge = vmem_call(
         outer,
         (
             sds((orows, 2, outs, lanes), BF16),
-            sds((orows, 2, 3 * outs, lanes), BF16),
+            sds((orows, 2, outs, lanes), BF16),
+            sds((orows, 2, 6 * mid, lanes), BF16),
+            sds((orows, pairs, mid, lanes), F32),
+            sds((2, orows, mid, lanes), F32),
+            sds((orows, pairs, mid, lanes), BF16),
+            sds((2, orows, mid, lanes), BF16),
+        ),
+        9,
+        [VMEM((orows, 2, 3 * outs, lanes), BF16)],
+    )(hs, from_left, from_right, other_left, other_right, w2, wg, tp, g_in)
+
+    gx_edge = swap(gedge)
+    gx = swap(gother)
+    to_left = (ghalo[0] + gx_edge[0].astype(F32)).astype(BF16)
+    to_right = (ghalo[1] + gx_edge[1].astype(F32)).astype(BF16)
+    grad_l = shift_along(to_right, "strip", 1)
+    grad_r = shift_along(to_left, "strip", -1)
+
+    rows = outs // strips
+    half_rows = rows // 2
+    mine, send, apart = vmem_call(
+        dilated_grad_body,
+        (
             sds((strips, half_rows, 9 * mid), F32),
             sds((strips, half_rows, 9 * mid), BF16),
             sds((strips, rows, 9 * mid), BF16),
         ),
-        8,
-        [VMEM((orows, 2, 6 * mid, lanes), BF16)],
+        4,
         scalars=1,
-    )(slab_id, hs, from_left, from_right, other_left, other_right, w2, tp, dg_in)
+    )(slab_id, residual, hs, edges, dg_in)
 
     def pick(array, index, dim):
         return lax.dynamic_index_in_dim(array, index, dim, False, allow_negative_indices=False)
@@ -473,23 +531,6 @@
     apart = apart.reshape(groups, 2, rows, 9 * mid)
     apart_got = pair_swap(pick(apart, other_parity, 1))
     dg_own = (mine + swap(send).astype(F32)).astype(BF16)
-
-    send, residual = lax.optimization_barrier((send, residual))
-    gown, ghalo, gother = vmem_call(
-        hidden_grad_body,
-        (
-            sds((orows, pairs, mid, lanes), F32),
-            sds((2, orows, mid, lanes), F32),
-            sds((pairs + 2, orows, mid, lanes), BF16),
-        ),
-        3,
-    )(residual, wg, g_in)
-
-    gx = swap(gother)
-    to_left = (ghalo[0] + gx[0].astype(F32)).astype(BF16)
-    to_right = (ghalo[1] + gx[-1].astype(F32)).astype(BF16)
-    grad_l = shift_along(to_right, "strip", 1)
-    grad_r = shift_along(to_left, "strip", -1)
 
     prediction = vmem_call(
         prediction_body,

time: 77.8 us -> 76.8 us (0.987)
  local copies, waits for them, and re-layouts: 2.99 us -> 1.77 us
  waiting for transfers between devices: 19.3 us -> 18.5 us
    slice x2 -> x0, local copies, waits for them, and re-layouts: 1.52 us -> none  [the longest x1 1.24 us: local(): lower = shift_along(volume[:, -1], 'slab', 1)]
    pallas_call x2 -> x4, Pallas kernels: 4.48 us -> 5.47 us  [the longest x1 2.71 us: local(): vmem_call(outer, (sds((orows, 2, outs, lanes), BF16), sds((orows, 2, outs...]
    ppermute x6, waiting for transfers between devices: 3.18 us -> 2.29 us  [shift_along(): return lax.ppermute(value, axis, pairs)]
    unnamed x14 -> x10, local copies, waits for them, and re-layouts: 1.02 us -> 1.6 us
    ppermute x7 -> x8, starting transfers between devices: 1.46 us -> 1.77 us  [swap(): return lax.ppermute(value, 'slab', [(0, 1), (1, 0)])]
    ppermute x7 -> x8, waiting for transfers between devices: 2.6 us -> 2.61 us  [swap(): return lax.ppermute(value, 'slab', [(0, 1), (1, 0)])]
  transfers between devices with their start and end apart: 21 -> 22, of which waited for: 10 -> 10; matrix products, arithmetic and copies ran while one was open for 1% -> 0% of each run, Pallas kernels for 19% -> 19%
where the time goes in v6:
time: 76.8 us; the launch traced here: 76.5 us
  starting transfers between devices  33 us (43%)
  Pallas kernels  20.1 us (26%)
  waiting for transfers between devices  18.5 us (24%)
  other arithmetic  2.04 us (3%)
  local copies, waits for them, and re-layouts  1.77 us (2%)
  between operations  1.18 us (2%)
    ppermute x6, starting transfers between devices, shift_along(): return lax.ppermute(value, axis, pairs)  17.4 us
    ppermute x6, starting transfers between devices, far_swap(): lax.ppermute(pick(chunks, places[d], 0).astype(BF16), 'strip', [(i, (i +...  9.48 us
    ppermute x6, waiting for transfers between devices, far_swap(): lax.ppermute(pick(chunks, places[d], 0).astype(BF16), 'strip', [(i, (i +...  8.48 us
    ppermute x2, waiting for transfers between devices, pair_swap(): return lax.ppermute(value, 'strip', [(i, i ^ 1) for i in range(strips)])  5.11 us
    pallas_call x1, Pallas kernels, local(): vmem_call(inner, (sds((orows, pairs, 6 * mid, lanes), BF16), sds((orows,...  4.41 us
    ppermute x2, starting transfers between devices, pair_swap(): return lax.ppermute(value, 'strip', [(i, i ^ 1) for i in range(strips)])  4.36 us
    pallas_call x1, Pallas kernels, local(): vmem_call(split_body, (sds((pairs, (rows_in + 1) * 9 * channels, lanes),...  3.54 us
    pallas_call x1, Pallas kernels, local(): vmem_call(outer, (sds((orows, 2, outs, lanes), BF16), sds((orows, 2, outs...  2.71 us
  transfers between devices with their start and end apart: 22, of which 10 were waited for; matrix products, arithmetic and copies ran while one was open for 0% of the time, Pallas kernels for 19%

profile of v6, /device:TPU:0, one launch (start us, length us, event | category | flops | bytes accessed | tf_op | source)
XLA Modules:
  0.0 76.5 jit_solution(4484269992459027925)
XLA Ops:
  0.7 1.6 %copy-done = bf16[64,4,16,256]{3,2,1,0:T(8,128)(2,1)S(1)} copy-done((bf16[64,4,16,256]{3,2,1,0:T(8,128)(2,1)S(1)}, bf16[64,4,16,256]{3,2,1,0:T(8,128)(2,1)}, u32[]{:S(2)}) %copy-start) | copy-done | bytes 2097176
  2.3 0.4 shard_map.67
  2.7 0.0 copy-start.4
  2.8 0.0 copy-start.2
  2.8 5.1 %collective-permute-start = (bf16[4,64,256]{2,1,0:T(8,128)(2,1)S(1)}, bf16[4,64,256]{2,1,0:T(8,128)(2,1)S(1)}, u32[]{:S(2)}, u32[]{:S(2)}) collective-permute-start(bf16[4,64,256]{2,1,0:T(8,128)(2,1)S(1)} %shard_map.67), channel_id=1, source_target_pairs={{0,1},{1,2},{2,3},{3,4},{4,5},{5,6},{6,7},{8,9},{9,10},{10,11},{11... | collective-permute-start | bytes 393224 | tf_op jit(solution)/shard_map/ppermute | solution.py:375
  7.9 3.5 %shard_map.68 = (bf16[4,2880,256]{2,1,0:T(8,128)(2,1)S(1)}, bf16[1024,256]{1,0:T(8,128)(2,1)S(1)}) custom-call(bf16[64,4,16,256]{3,2,1,0:T(8,128)(2,1)S(1)} %copy-done.1), custom_call_target="tpu_custom_call" | custom-call | tf_op jit(solution)/shard_map/pallas_call | solution.py:410
  11.5 0.0 collective-permute-done.hcol_ref
  11.5 1.5 %collective-permute-start.1 = (bf16[1088,256]{1,0:T(8,128)(2,1)S(1)}, bf16[1088,256]{1,0:T(8,128)(2,1)S(1)}, u32[]{:S(2)}, u32[]{:S(2)}) collective-permute-start(bf16[1088,256]{1,0:T(8,128)(2,1)S(1)} %pad_maximum_fusion), channel_id=1, source_target_pairs={{0,8},{1,9},{2,10},{3,11},{4,12},{5,13},{6,14},{7,15},{16,24},{17,... | collective-permute-start | bytes 1671176 | tf_op jit(solution)/shard_map/ppermute | solution.py:375
  13.1 0.5 shard_map.69
  13.6 1.0 %collective-permute-done.1.hrow_ref = bf16[1088,256]{1,0:T(8,128)(2,1)S(1)} collective-permute-done((bf16[1088,256]{1,0:T(8,128)(2,1)S(1)}, bf16[1088,256]{1,0:T(8,128)(2,1)S(1)}, u32[]{:S(2)}, u32[]{:S(2)}) %collective-permute-start.1) | collective-permute-done | bytes 557088 | tf_op jit(solution)/shard_map/ppermute | solution.py:375
  14.6 2.2 %shard_map.70 = (bf16[4,2880,256]{2,1,0:T(8,128)(2,1)S(1)}, bf16[2,4,128,256]{3,2,1,0:T(8,128)(2,1)S(1)}, bf16[2,128,256]{2,1,0:T(8,128)(2,1)S(1)}, bf16[2,128,2...) custom-call(bf16[4,2880,256]{2,1,0:T(8,128)(2,1)S(1)} %get-tuple-element.54.own_ref, ...), custom_call_target="tpu_custom_call" | custom-call | tf_op jit(solution)/shard_map/pallas_call | solution.py:438
  16.7 0.4 collective-permute-start.4
  17.2 3.4 %collective-permute-start.2 = (bf16[2,128,256]{2,1,0:T(8,128)(2,1)S(1)}, bf16[2,128,256]{2,1,0:T(8,128)(2,1)S(1)}, u32[]{:S(2)}, u32[]{:S(2)}) collective-permute-start(bf16[2,128,256]{2,1,0:T(8,128)(2,1)S(1)} %get-tuple-element.58), channel_id=1, source_target_pairs={{0,1},{1,2},{2,3},{3,4},{4,5},{5,6},{6,7},{8,9},{9,10},{10,11},{11... | collective-permute-start | bytes 393224 | tf_op jit(solution)/shard_map/ppermute | solution.py:375
  20.6 1.5 %collective-permute-start.3 = (bf16[2,128,256]{2,1,0:T(8,128)(2,1)S(1)}, bf16[2,128,256]{2,1,0:T(8,128)(2,1)S(1)}, u32[]{:S(2)}, u32[]{:S(2)}) collective-permute-start(bf16[2,128,256]{2,1,0:T(8,128)(2,1)S(1)} %get-tuple-element.59), channel_id=1, source_target_pairs={{1,0},{2,1},{3,2},{4,3},{5,4},{6,5},{7,6},{9,8},{10,9},{11,10},{12... | collective-permute-start | bytes 393224 | tf_op jit(solution)/shard_map/ppermute | solution.py:375
  22.1 0.5 shard_map.71.refs_4_.refs_7_
  22.6 0.0 collective-permute-done.4.refs_1_
  22.7 4.4 %shard_map.72 = (bf16[2,4,768,256]{3,2,1,0:T(8,128)(2,1)S(1)}, bf16[2,2,256,256]{3,2,1,0:T(8,128)(2,1)S(1)}, f32[256,2304]{1,0:T(8,128)S(1)}, f32[2,4,256,256]{3,2,1,0:T(8,128)S(1)}) custom-call(bf16[2,4,128,256]{3,2,1,0:T(8,128)(2,1)S(1)} %get-tuple-element.60.refs_0_, bf16[2,4,128,256]{3,2,1,0:T(8,128)(2,1)S(1)} %collective-permute-done.4.refs_1_, ...), custom_call_target="tpu_custom_call" | custom-call | tf_op jit(solution)/shard_map/pallas_call | solution.py:461
  27.1 0.0 collective-permute-done.2.refs_1_
  27.1 1.3 %collective-permute-done.3.refs_2_ = bf16[2,128,256]{2,1,0:T(8,128)(2,1)S(1)} collective-permute-done((bf16[2,128,256]{2,1,0:T(8,128)(2,1)S(1)}, bf16[2,128,256]{2,1,0:T(8,128)(2,1)S(1)}, u32[]{:S(2)}, u32[]{:S(2)}) %collective-permute-start.3) | collective-permute-done | bytes 131104 | tf_op jit(solution)/shard_map/ppermute | solution.py:375
  28.4 0.0 collective-permute-start.5
  28.4 0.5 collective-permute-start.6
  28.9 0.8 %collective-permute-done.5.refs_3_ = bf16[2,128,256]{2,1,0:T(8,128)(2,1)S(1)} collective-permute-done((bf16[2,128,256]{2,1,0:T(8,128)(2,1)S(1)}, bf16[2,128,256]{2,1,0:T(8,128)(2,1)S(1)}, u32[]{:S(2)}, u32[]{:S(2)}) %collective-permute-start.5) | collective-permute-done | bytes 131104 | tf_op jit(solution)/shard_map/ppermute | solution.py:379
  29.7 0.2 collective-permute-done.6.refs_4_
  29.9 2.7 %shard_map.73 = (bf16[2,2,256,256]{3,2,1,0:T(8,128)(2,1)S(1)}, bf16[2,2,256,256]{3,2,1,0:T(8,128)(2,1)S(1)}, bf16[2,2,768,256]{3,2,1,0:T(8,128)(2,1)S(1)}, f32[2...) custom-call(bf16[2,4,768,256]{3,2,1,0:T(8,128)(2,1)S(1)} %get-tuple-, ...), custom_call_target="tpu_custom_call" | custom-call | tf_op jit(solution)/shard_map/pallas_call | solution.py:477
  32.6 0.4 collective-permute-start.12
  33.0 1.8 %shard_map.74 = (f32[8,16,1152]{2,1,0:T(8,128)S(1)}, bf16[8,16,1152]{2,1,0:T(8,128)(2,1)S(1)}, bf16[8,32,1152]{2,1,0:T(8,128)(2,1)S(1)}) custom-call(s32[1]{0:T(128)} %bitcast.slab_ref, bf16[2,2,256,256]{3,2,1,0:T(8,128)(2,1)S(1)} %get-tuple-element.68.res_ref, bf16[2,4,768,256]{3,2,1,0:T(8,128)(2,1)S(1)} %get-tuple-element.64.refs_0_.hs_ref, ...), custom_call_target="tpu_custom_call" | custom-call | tf_op jit(solution)/shard_map/pallas_call | solution.py:501
  34.9 0.2 collective-permute-start.7
  35.1 2.7 %collective-permute-start.15 = (bf16[4,32,1152]{2,1,0:T(8,128)(2,1)S(1)}, bf16[4,32,1152]{2,1,0:T(8,128)(2,1)S(1)}, u32[]{:S(2)}, u32[]{:S(2)}) collective-permute-start(bf16[4,32,1152]{2,1,0:T(8,128)(2,1)S(1)} %dynamic-slice_bitcast_fusion), channel_id=1, source_target_pairs={{0,1},{1,0},{2,3},{3,2},{4,5},{5,4},{6,7},{7,6},{8,9},{9,8},{10,11... | collective-permute-start | bytes 884744 | tf_op jit(solution)/shard_map/ppermute | solution.py:516
  37.8 0.0 collective-permute-start.11
  37.9 1.6 %shard_map.75 = bf16[256,2,8,128]{3,2,1,0:T(8,128)(2,1)} custom-call(bf16[2,2,256,256]{3,2,1,0:T(8,128)(2,1)S(1)} %get-tuple-element.73.inner_ref, bf16[2,2,256,256]{3,2,1,0:T(8,128)(2,1)S(1)} %get-tuple-element.74.outer_ref), custom_call_target="tpu_custom_call" | custom-call | tf_op jit(solution)/shard_map/pallas_call | solution.py:535
  39.5 0.0 collective-permute-done.12
  39.5 0.1 fusion.14
  39.6 1.3 %collective-permute-start.14 = (bf16[2,128,256]{2,1,0:T(8,128)(2,1)S(1)}, bf16[2,128,256]{2,1,0:T(8,128)(2,1)S(1)}, u32[]{:S(2)}, u32[]{:S(2)}) collective-permute-start(bf16[2,128,256]{2,1,0:T(8,128)(2,1)S(1)} %get-tuple-element.100), channel_id=1, source_target_pairs={{1,0},{2,1},{3,2},{4,3},{5,4},{6,5},{7,6},{9,8},{10,9},{11,10},{12... | collective-permute-start | bytes 393224 | tf_op jit(solution)/shard_map/ppermute | solution.py:375
  40.9 4.6 %collective-permute-start.13 = (bf16[2,128,256]{2,1,0:T(8,128)(2,1)S(1)}, bf16[2,128,256]{2,1,0:T(8,128)(2,1)S(1)}, u32[]{:S(2)}, u32[]{:S(2)}) collective-permute-start(bf16[2,128,256]{2,1,0:T(8,128)(2,1)S(1)} %get-tuple-element.101), channel_id=1, source_target_pairs={{0,1},{1,2},{2,3},{3,4},{4,5},{5,6},{6,7},{8,9},{9,10},{10,11},{11... | collective-permute-start | bytes 393224 | tf_op jit(solution)/shard_map/ppermute | solution.py:375
  45.5 0.0 collective-permute-done.7
  45.5 0.1 add_convert_fusion.1
  45.6 1.6 %collective-permute-start.8 = (bf16[2,16,1152]{2,1,0:T(8,128)(2,1)S(1)}, bf16[2,16,1152]{2,1,0:T(8,128)(2,1)S(1)}, u32[]{:S(2)}, u32[]{:S(2)}) collective-permute-start(bf16[2,16,1152]{2,1,0:T(8,128)(2,1)S(1)} %get-tuple-element.106), channel_id=1, source_target_pairs={{0,2},{1,3},{2,4},{3,5},{4,6},{5,7},{6,0},{7,1},{8,10},{9,11},{10,... | collective-permute-start | bytes 221192 | tf_op jit(solution)/shard_map/ppermute | solution.py:520
  47.2 0.8 %collective-permute-done.15 = bf16[4,32,1152]{2,1,0:T(8,128)(2,1)S(1)} collective-permute-done((bf16[4,32,1152]{2,1,0:T(8,128)(2,1)S(1)}, bf16[4,32,1152]{2,1,0:T(8,128)(2,1)S(1)}, u32[]{:S(2)}, u32[]{:S(2)}) %collective-permute-start.15) | collective-permute-done | bytes 294944 | tf_op jit(solution)/shard_map/ppermute | solution.py:516
  48.0 2.3 %collective-permute-start.10 = (bf16[2,16,1152]{2,1,0:T(8,128)(2,1)S(1)}, bf16[2,16,1152]{2,1,0:T(8,128)(2,1)S(1)}, u32[]{:S(2)}, u32[]{:S(2)}) collective-permute-start(bf16[2,16,1152]{2,1,0:T(8,128)(2,1)S(1)} %get-tuple-element.107), channel_id=1, source_target_pairs={{0,6},{1,7},{2,0},{3,1},{4,2},{5,3},{6,4},{7,5},{8,14},{9,15},{10,... | collective-permute-start | bytes 221192 | tf_op jit(solution)/shard_map/ppermute | solution.py:520
  50.3 0.0 collective-permute-done.11.gx_ref
  50.3 0.6 collective-permute-start.9
  50.9 1.2 %shard_map.76.sum_ref = f32[128,1728]{1,0:T(8,128)S(1)} custom-call(f32[2,4,128,256]{3,2,1,0:T(8,128)S(1)} %get-tuple-element.83.gown_ref, bf16[2,4,128,256]{3,2,1,0:T(8,128)(2,1)S(1)} %collective-permute-done.11.gx_ref, f32[2,4,128,256]{3,2,1,0:T(8,128)S(1)} %get-tuple-element.89.slope_ref, bf16[4,2880,256]{2,1,0:T(8,128)(2,1)S(1)} %get-tuple-element.90.vp_ref), custom_call_target="tpu_custom_call" | custom-call | tf_op jit(solution)/shard_map/pallas_call | solution.py:541
  52.0 0.0 collective-permute-done.14.gr_ref
  52.0 0.0 collective-permute-done.13.gl_ref
  52.0 1.2 %shard_map.77 = (f32[8,16,1152]{2,1,0:T(8,128)S(1)}, bf16[8,16,1152]{2,1,0:T(8,128)(2,1)S(1)}) custom-call(s32[1]{0:T(128)} %bitcast.slab_ref, f32[2,4,128,256]{3,2,1,0:T(8,128)S(1)} %get-tuple-element.83.gown_ref, bf16[2,4,128,256]{3,2,1,0:T(8,128)(2,1)S(1)} %collective-permute-done.11.gx_ref, bf16[2,128,256]{2,1,0:T(8,128)(2,1)S(1)} %collective-permute-done.13.gl_ref, ...), custom_call_target="tpu_custom_call" | custom-call | tf_op jit(solution)/shard_map/pallas_call | solution.py:549
  53.2 0.1 collective-permute-start.16
  53.3 0.0 collective-permute-done.10
  53.3 2.9 %collective-permute-done.9 = bf16[2,16,1152]{2,1,0:T(8,128)(2,1)S(1)} collective-permute-done((bf16[2,16,1152]{2,1,0:T(8,128)(2,1)S(1)}, bf16[2,16,1152]{2,1,0:T(8,128)(2,1)S(1)}, u32[]{:S(2)}, u32[]{:S(2)}) %collective-permute-start.9) | collective-permute-done | bytes 73760 | tf_op jit(solution)/shard_map/ppermute | solution.py:520
  56.3 0.1 add_convert_fusion
  56.4 1.7 %collective-permute-start.17 = (bf16[80,1152]{1,0:T(8,128)(2,1)S(1)}, bf16[80,1152]{1,0:T(8,128)(2,1)S(1)}, u32[]{:S(2)}, u32[]{:S(2)}) collective-permute-start(bf16[80,1152]{1,0:T(8,128)(2,1)S(1)} %pad_maximum_fusion.3), channel_id=1, source_target_pairs={{0,1},{1,0},{2,3},{3,2},{4,5},{5,4},{6,7},{7,6},{8,9},{9,8},{10,11... | collective-permute-start | bytes 552968 | tf_op jit(solution)/shard_map/ppermute | solution.py:516
  58.1 0.1 convert_add_fusion
  58.2 4.3 %collective-permute-done.17 = bf16[80,1152]{1,0:T(8,128)(2,1)S(1)} collective-permute-done((bf16[80,1152]{1,0:T(8,128)(2,1)S(1)}, bf16[80,1152]{1,0:T(8,128)(2,1)S(1)}, u32[]{:S(2)}, u32[]{:S(2)}) %collective-permute-start.17) | collective-permute-done | bytes 184352 | tf_op jit(solution)/shard_map/ppermute | solution.py:516
  62.5 0.1 fusion.16
  62.6 1.6 %collective-permute-start.18 = (bf16[48,1152]{1,0:T(8,128)(2,1)S(1)}, bf16[48,1152]{1,0:T(8,128)(2,1)S(1)}, u32[]{:S(2)}, u32[]{:S(2)}) collective-permute-start(bf16[48,1152]{1,0:T(8,128)(2,1)S(1)} %get-tuple-element.97), channel_id=1, source_target_pairs={{0,2},{1,3},{2,4},{3,5},{4,6},{5,7},{6,0},{7,1},{8,10},{9,11},{10,... | collective-permute-start | bytes 331784 | tf_op jit(solution)/shard_map/ppermute | solution.py:520
  64.2 2.2 %collective-permute-start.19 = (bf16[48,1152]{1,0:T(8,128)(2,1)S(1)}, bf16[48,1152]{1,0:T(8,128)(2,1)S(1)}, u32[]{:S(2)}, u32[]{:S(2)}) collective-permute-start(bf16[48,1152]{1,0:T(8,128)(2,1)S(1)} %get-tuple-element.98), channel_id=1, source_target_pairs={{0,4},{1,5},{2,6},{3,7},{4,0},{5,1},{6,2},{7,3},{8,12},{9,13},{10,... | collective-permute-start | bytes 331784 | tf_op jit(solution)/shard_map/ppermute | solution.py:520
  66.4 1.2 %collective-permute-start.20 = (bf16[48,1152]{1,0:T(8,128)(2,1)S(1)}, bf16[48,1152]{1,0:T(8,128)(2,1)S(1)}, u32[]{:S(2)}, u32[]{:S(2)}) collective-permute-start(bf16[48,1152]{1,0:T(8,128)(2,1)S(1)} %get-tuple-element.99), channel_id=1, source_target_pairs={{0,6},{1,7},{2,0},{3,1},{4,2},{5,3},{6,4},{7,5},{8,14},{9,15},{10,... | collective-permute-start | bytes 331784 | tf_op jit(solution)/shard_map/ppermute | solution.py:520
  67.6 2.8 %collective-permute-done.18 = bf16[48,1152]{1,0:T(8,128)(2,1)S(1)} collective-permute-done((bf16[48,1152]{1,0:T(8,128)(2,1)S(1)}, bf16[48,1152]{1,0:T(8,128)(2,1)S(1)}, u32[]{:S(2)}, u32[]{:S(2)}) %collective-permute-start.18) | collective-permute-done | bytes 110624 | tf_op jit(solution)/shard_map/ppermute | solution.py:520
  70.4 2.8 %collective-permute-done.19 = bf16[48,1152]{1,0:T(8,128)(2,1)S(1)} collective-permute-done((bf16[48,1152]{1,0:T(8,128)(2,1)S(1)}, bf16[48,1152]{1,0:T(8,128)(2,1)S(1)}, u32[]{:S(2)}, u32[]{:S(2)}) %collective-permute-start.19) | collective-permute-done | bytes 110624 | tf_op jit(solution)/shard_map/ppermute | solution.py:520
  73.2 0.0 collective-permute-done.20
  73.2 0.1 fusion.6
  73.3 0.1 collective-permute-start.21
  73.4 1.6 %collective-permute-done.21 = f32[64,1152]{1,0:T(8,128)S(1)} collective-permute-done((f32[64,1152]{1,0:T(8,128)S(1)}, f32[64,1152]{1,0:T(8,128)S(1)}, u32[]{:S(2)}, u32[]{:S(2)}) %collective-permute-start.21) | collective-permute-done | bytes 294944 | tf_op jit(solution)/shard_map/ppermute | solution.py:379
  75.1 0.7 pad_maximum_fusion.4
  75.7 0.8 %pad_maximum_fusion.1 = f32[32,3456]{1,0:T(8,128)} fusion(f32[32,1152]{1,0:T(8,128)S(1)} %slice.61, f32[16,1152]{1,0:T(8,128)S(1)} %slice.60, f32[16,1152]{1,0:T(8,128)S(1)} %get-tuple-element.104, f32[32,1152]{1,0:T(8,128)S(1)} %slice.58), kind=kLoop, calls=%fused_computation.12 | loop fusion | flops 331776 | bytes 884736 | tf_op jit(solution)/shard_map/concatenate | solution.py:574
  (28 shorter events, 0.4 us)
Async XLA Ops:
  0.7 1.6 %copy-start = (bf16[64,4,16,256]{3,2,1,0:T(8,128)(2,1)S(1)}, bf16[64,4,16,256]{3,2,1,0:T(8,128)(2,1)}, u32[]{:S(2)}) copy-start(bf16[64,4,16,256]{3,2,1,0:T(8,128)(2,1)} %vol_ref.3) | copy-start | bytes 6291460
  2.3 5.6 %copy-start.1 = (bf16[64,4,16,256]{3,2,1,0:T(8,128)(2,1)S(1)}, bf16[64,4,16,256]{3,2,1,0:T(8,128)(2,1)}, u32[]{:S(2)}) copy-start(bf16[64,4,16,256]{3,2,1,0:T(8,128)(2,1)} %vol_ref.3) | copy-start | bytes 6291460
  2.7 10.3 %copy-start.4 = (bf16[128,1728]{0,1:T(8,128)(2,1)S(1)}, bf16[128,1728]{0,1:T(8,128)(2,1)}, u32[]{:S(2)}) copy-start(bf16[128,1728]{0,1:T(8,128)(2,1)} %param.6) | copy-start | bytes 1327108
  2.8 10.3 %copy-start.2 = (bf16[256,3456]{1,0:T(8,128)(2,1)S(1)}, bf16[256,3456]{1,0:T(8,128)(2,1)}, u32[]{:S(2)}) copy-start(bf16[256,3456]{1,0:T(8,128)(2,1)} %wd_ref.1) | copy-start | bytes 5308420
  2.8 8.7 %collective-permute-start = (bf16[4,64,256]{2,1,0:T(8,128)(2,1)S(1)}, bf16[4,64,256]{2,1,0:T(8,128)(2,1)S(1)}, u32[]{:S(2)}, u32[]{:S(2)}) collective-permute-start(bf16[4,64,256]{2,1,0:T(8,128)(2,1)S(1)} %shard_map.67), channel_id=1, source_target_pairs={{0,1},{1,2},{2,3},{3,4},{4,5},{5,6},{6,7},{8,9},{9,10},{10,11},{11... | collective-permute-start | bytes 393224 | tf_op jit(solution)/shard_map/ppermute | solution.py:375
  11.5 3.0 %collective-permute-start.1 = (bf16[1088,256]{1,0:T(8,128)(2,1)S(1)}, bf16[1088,256]{1,0:T(8,128)(2,1)S(1)}, u32[]{:S(2)}, u32[]{:S(2)}) collective-permute-start(bf16[1088,256]{1,0:T(8,128)(2,1)S(1)} %pad_maximum_fusion), channel_id=1, source_target_pairs={{0,8},{1,9},{2,10},{3,11},{4,12},{5,13},{6,14},{7,15},{16,24},{17,... | collective-permute-start | bytes 1671176 | tf_op jit(solution)/shard_map/ppermute | solution.py:375
  14.6 7.5 %copy-start.3 = (bf16[256,2,8,128]{3,2,1,0:T(8,128)(2,1)S(1)}, bf16[256,2,8,128]{3,2,1,0:T(8,128)(2,1)}, u32[]{:S(2)}) copy-start(bf16[256,2,8,128]{3,2,1,0:T(8,128)(2,1)} %tgt_ref.1) | copy-start | bytes 3145732
  16.7 5.9 %collective-permute-start.4 = (bf16[2,4,128,256]{3,2,1,0:T(8,128)(2,1)S(1)}, bf16[2,4,128,256]{3,2,1,0:T(8,128)(2,1)S(1)}, u32[]{:S(2)}, u32[]{:S(2)}) collective-permute-start(bf16[2,4,128,256]{3,2,1,0:T(8,128)(2,1)S(1)} %get-tuple-element.60.refs_0_), channel_id=1, source_target_pairs={{0,8},{8,0},{1,9},{9,1},{2,10},{10,2},{3,11},{11,3},{4,12},{12,4},... | collective-permute-start | bytes 1572872 | tf_op jit(solution)/shard_map/ppermute | solution.py:379
  17.2 9.9 %collective-permute-start.2 = (bf16[2,128,256]{2,1,0:T(8,128)(2,1)S(1)}, bf16[2,128,256]{2,1,0:T(8,128)(2,1)S(1)}, u32[]{:S(2)}, u32[]{:S(2)}) collective-permute-start(bf16[2,128,256]{2,1,0:T(8,128)(2,1)S(1)} %get-tuple-element.58), channel_id=1, source_target_pairs={{0,1},{1,2},{2,3},{3,4},{4,5},{5,6},{6,7},{8,9},{9,10},{10,11},{11... | collective-permute-start | bytes 393224 | tf_op jit(solution)/shard_map/ppermute | solution.py:375
  20.6 7.8 %collective-permute-start.3 = (bf16[2,128,256]{2,1,0:T(8,128)(2,1)S(1)}, bf16[2,128,256]{2,1,0:T(8,128)(2,1)S(1)}, u32[]{:S(2)}, u32[]{:S(2)}) collective-permute-start(bf16[2,128,256]{2,1,0:T(8,128)(2,1)S(1)} %get-tuple-element.59), channel_id=1, source_target_pairs={{1,0},{2,1},{3,2},{4,3},{5,4},{6,5},{7,6},{9,8},{10,9},{11,10},{12... | collective-permute-start | bytes 393224 | tf_op jit(solution)/shard_map/ppermute | solution.py:375
  28.4 1.3 %collective-permute-start.5 = (bf16[2,128,256]{2,1,0:T(8,128)(2,1)S(1)}, bf16[2,128,256]{2,1,0:T(8,128)(2,1)S(1)}, u32[]{:S(2)}, u32[]{:S(2)}) collective-permute-start(bf16[2,128,256]{2,1,0:T(8,128)(2,1)S(1)} %collective-permute-done.2.refs_1_), channel_id=1, source_target_pairs={{0,8},{8,0},{1,9},{9,1},{2,10},{10,2},{3,11},{11,3},{4,12},{12,4},... | collective-permute-start | bytes 393224 | tf_op jit(solution)/shard_map/ppermute | solution.py:379
  28.4 1.5 %collective-permute-start.6 = (bf16[2,128,256]{2,1,0:T(8,128)(2,1)S(1)}, bf16[2,128,256]{2,1,0:T(8,128)(2,1)S(1)}, u32[]{:S(2)}, u32[]{:S(2)}) collective-permute-start(bf16[2,128,256]{2,1,0:T(8,128)(2,1)S(1)} %collective-permute-done.3.refs_2_), channel_id=1, source_target_pairs={{0,8},{8,0},{1,9},{9,1},{2,10},{10,2},{3,11},{11,3},{4,12},{12,4},... | collective-permute-start | bytes 393224 | tf_op jit(solution)/shard_map/ppermute | solution.py:379
  32.6 6.9 %collective-permute-start.12 = (bf16[2,2,128,256]{3,2,1,0:T(8,128)(2,1)S(1)}, bf16[2,2,128,256]{3,2,1,0:T(8,128)(2,1)S(1)}, u32[]{:S(2)}, u32[]{:S(2)}) collective-permute-start(bf16[2,2,128,256]{3,2,1,0:T(8,128)(2,1)S(1)} %get-tuple-element.86), channel_id=1, source_target_pairs={{0,8},{8,0},{1,9},{9,1},{2,10},{10,2},{3,11},{11,3},{4,12},{12,4},... | collective-permute-start | bytes 786440 | tf_op jit(solution)/shard_map/ppermute | solution.py:379
  34.9 10.6 %collective-permute-start.7 = (bf16[8,16,1152]{2,1,0:T(8,128)(2,1)S(1)}, bf16[8,16,1152]{2,1,0:T(8,128)(2,1)S(1)}, u32[]{:S(2)}, u32[]{:S(2)}) collective-permute-start(bf16[8,16,1152]{2,1,0:T(8,128)(2,1)S(1)} %get-tuple-element.72), channel_id=1, source_target_pairs={{0,8},{8,0},{1,9},{9,1},{2,10},{10,2},{3,11},{11,3},{4,12},{12,4},... | collective-permute-start | bytes 884744 | tf_op jit(solution)/shard_map/ppermute | solution.py:379
  35.1 12.9 %collective-permute-start.15 = (bf16[4,32,1152]{2,1,0:T(8,128)(2,1)S(1)}, bf16[4,32,1152]{2,1,0:T(8,128)(2,1)S(1)}, u32[]{:S(2)}, u32[]{:S(2)}) collective-permute-start(bf16[4,32,1152]{2,1,0:T(8,128)(2,1)S(1)} %dynamic-slice_bitcast_fusion), channel_id=1, source_target_pairs={{0,1},{1,0},{2,3},{3,2},{4,5},{5,4},{6,7},{7,6},{8,9},{9,8},{10,11... | collective-permute-start | bytes 884744 | tf_op jit(solution)/shard_map/ppermute | solution.py:516
  37.8 12.4 %collective-permute-start.11 = (bf16[2,4,128,256]{3,2,1,0:T(8,128)(2,1)S(1)}, bf16[2,4,128,256]{3,2,1,0:T(8,128)(2,1)S(1)}, u32[]{:S(2)}, u32[]{:S(2)}) collective-permute-start(bf16[2,4,128,256]{3,2,1,0:T(8,128)(2,1)S(1)} %get-tuple-element.84), channel_id=1, source_target_pairs={{0,8},{8,0},{1,9},{9,1},{2,10},{10,2},{3,11},{11,3},{4,12},{12,4},... | collective-permute-start | bytes 1572872 | tf_op jit(solution)/shard_map/ppermute | solution.py:379
  39.6 12.4 %collective-permute-start.14 = (bf16[2,128,256]{2,1,0:T(8,128)(2,1)S(1)}, bf16[2,128,256]{2,1,0:T(8,128)(2,1)S(1)}, u32[]{:S(2)}, u32[]{:S(2)}) collective-permute-start(bf16[2,128,256]{2,1,0:T(8,128)(2,1)S(1)} %get-tuple-element.100), channel_id=1, source_target_pairs={{1,0},{2,1},{3,2},{4,3},{5,4},{6,5},{7,6},{9,8},{10,9},{11,10},{12... | collective-permute-start | bytes 393224 | tf_op jit(solution)/shard_map/ppermute | solution.py:375
  40.9 11.1 %collective-permute-start.13 = (bf16[2,128,256]{2,1,0:T(8,128)(2,1)S(1)}, bf16[2,128,256]{2,1,0:T(8,128)(2,1)S(1)}, u32[]{:S(2)}, u32[]{:S(2)}) collective-permute-start(bf16[2,128,256]{2,1,0:T(8,128)(2,1)S(1)} %get-tuple-element.101), channel_id=1, source_target_pairs={{0,1},{1,2},{2,3},{3,4},{4,5},{5,6},{6,7},{8,9},{9,10},{10,11},{11... | collective-permute-start | bytes 393224 | tf_op jit(solution)/shard_map/ppermute | solution.py:375
  45.6 7.7 %collective-permute-start.8 = (bf16[2,16,1152]{2,1,0:T(8,128)(2,1)S(1)}, bf16[2,16,1152]{2,1,0:T(8,128)(2,1)S(1)}, u32[]{:S(2)}, u32[]{:S(2)}) collective-permute-start(bf16[2,16,1152]{2,1,0:T(8,128)(2,1)S(1)} %get-tuple-element.106), channel_id=1, source_target_pairs={{0,2},{1,3},{2,4},{3,5},{4,6},{5,7},{6,0},{7,1},{8,10},{9,11},{10,... | collective-permute-start | bytes 221192 | tf_op jit(solution)/shard_map/ppermute | solution.py:520
  48.0 5.3 %collective-permute-start.10 = (bf16[2,16,1152]{2,1,0:T(8,128)(2,1)S(1)}, bf16[2,16,1152]{2,1,0:T(8,128)(2,1)S(1)}, u32[]{:S(2)}, u32[]{:S(2)}) collective-permute-start(bf16[2,16,1152]{2,1,0:T(8,128)(2,1)S(1)} %get-tuple-element.107), channel_id=1, source_target_pairs={{0,6},{1,7},{2,0},{3,1},{4,2},{5,3},{6,4},{7,5},{8,14},{9,15},{10,... | collective-permute-start | bytes 221192 | tf_op jit(solution)/shard_map/ppermute | solution.py:520
  50.3 6.0 %collective-permute-start.9 = (bf16[2,16,1152]{2,1,0:T(8,128)(2,1)S(1)}, bf16[2,16,1152]{2,1,0:T(8,128)(2,1)S(1)}, u32[]{:S(2)}, u32[]{:S(2)}) collective-permute-start(bf16[2,16,1152]{2,1,0:T(8,128)(2,1)S(1)} %get-tuple-element.108), channel_id=1, source_target_pairs={{0,4},{1,5},{2,6},{3,7},{4,0},{5,1},{6,2},{7,3},{8,12},{9,13},{10,... | collective-permute-start | bytes 221192 | tf_op jit(solution)/shard_map/ppermute | solution.py:520
  53.2 3.1 %collective-permute-start.16 = (bf16[8,16,1152]{2,1,0:T(8,128)(2,1)S(1)}, bf16[8,16,1152]{2,1,0:T(8,128)(2,1)S(1)}, u32[]{:S(2)}, u32[]{:S(2)}) collective-permute-start(bf16[8,16,1152]{2,1,0:T(8,128)(2,1)S(1)} %get-tuple-element.95), channel_id=1, source_target_pairs={{0,8},{8,0},{1,9},{9,1},{2,10},{10,2},{3,11},{11,3},{4,12},{12,4},... | collective-permute-start | bytes 884744 | tf_op jit(solution)/shard_map/ppermute | solution.py:379
  56.4 6.0 %collective-permute-start.17 = (bf16[80,1152]{1,0:T(8,128)(2,1)S(1)}, bf16[80,1152]{1,0:T(8,128)(2,1)S(1)}, u32[]{:S(2)}, u32[]{:S(2)}) collective-permute-start(bf16[80,1152]{1,0:T(8,128)(2,1)S(1)} %pad_maximum_fusion.3), channel_id=1, source_target_pairs={{0,1},{1,0},{2,3},{3,2},{4,5},{5,4},{6,7},{7,6},{8,9},{9,8},{10,11... | collective-permute-start | bytes 552968 | tf_op jit(solution)/shard_map/ppermute | solution.py:516
  62.6 7.8 %collective-permute-start.18 = (bf16[48,1152]{1,0:T(8,128)(2,1)S(1)}, bf16[48,1152]{1,0:T(8,128)(2,1)S(1)}, u32[]{:S(2)}, u32[]{:S(2)}) collective-permute-start(bf16[48,1152]{1,0:T(8,128)(2,1)S(1)} %get-tuple-element.97), channel_id=1, source_target_pairs={{0,2},{1,3},{2,4},{3,5},{4,6},{5,7},{6,0},{7,1},{8,10},{9,11},{10,... | collective-permute-start | bytes 331784 | tf_op jit(solution)/shard_map/ppermute | solution.py:520
  64.2 9.0 %collective-permute-start.19 = (bf16[48,1152]{1,0:T(8,128)(2,1)S(1)}, bf16[48,1152]{1,0:T(8,128)(2,1)S(1)}, u32[]{:S(2)}, u32[]{:S(2)}) collective-permute-start(bf16[48,1152]{1,0:T(8,128)(2,1)S(1)} %get-tuple-element.98), channel_id=1, source_target_pairs={{0,4},{1,5},{2,6},{3,7},{4,0},{5,1},{6,2},{7,3},{8,12},{9,13},{10,... | collective-permute-start | bytes 331784 | tf_op jit(solution)/shard_map/ppermute | solution.py:520
  66.4 6.8 %collective-permute-start.20 = (bf16[48,1152]{1,0:T(8,128)(2,1)S(1)}, bf16[48,1152]{1,0:T(8,128)(2,1)S(1)}, u32[]{:S(2)}, u32[]{:S(2)}) collective-permute-start(bf16[48,1152]{1,0:T(8,128)(2,1)S(1)} %get-tuple-element.99), channel_id=1, source_target_pairs={{0,6},{1,7},{2,0},{3,1},{4,2},{5,3},{6,4},{7,5},{8,14},{9,15},{10,... | collective-permute-start | bytes 331784 | tf_op jit(solution)/shard_map/ppermute | solution.py:520
  73.3 1.6 %collective-permute-start.21 = (f32[64,1152]{1,0:T(8,128)S(1)}, f32[64,1152]{1,0:T(8,128)S(1)}, u32[]{:S(2)}, u32[]{:S(2)}) collective-permute-start(f32[64,1152]{1,0:T(8,128)S(1)} %pad_maximum_fusion.2), channel_id=1, source_target_pairs={{0,8},{8,0},{1,9},{9,1},{2,10},{10,2},{3,11},{11,3},{4,12},{12,4},... | collective-permute-start | bytes 884744 | tf_op jit(solution)/shard_map/ppermute | solution.py:379

commit v7 on v6

--- a/solution.py
+++ b/solution.py
@@ -532,26 +532,27 @@
     apart_got = pair_swap(pick(apart, other_parity, 1))
     dg_own = (mine + swap(send).astype(F32)).astype(BF16)
 
+    mid_rows = mid // strips
+    width = 9 * mid
+    assert width < 27 * channels <= 2 * width
+    dg_own, gx = lax.optimization_barrier((dg_own, gx))
+    dg_own = dg_own.reshape(groups, 2, half_rows, 9 * mid)
+    own_got = far_swap(dg_own)
+    sg_in = vmem_call(strided_inner_body, sds((mid, 27 * channels), F32), 4)(gown, gx, slope, vp)
+    grad_l, grad_r, sg_in = lax.optimization_barrier((grad_l, grad_r, sg_in))
+    smine, ssend = vmem_call(
+        strided_grad_body,
+        (sds((strips, mid_rows, width), F32), sds((strips, mid_rows, width), BF16)),
+        7,
+        scalars=1,
+    )(slab_id, gown, gx, grad_l, grad_r, slope, vp, sg_in)
+    pred_out, ssend = lax.optimization_barrier((pred_out, ssend))
     prediction = vmem_call(
         prediction_body,
         sds((outs, orows, ocols, half), BF16),
         2,
         [VMEM((2, outs * ocols, half), F32)],
     )(pred_in, pred_out)
-    sg_in = vmem_call(strided_inner_body, sds((mid, 27 * channels), F32), 4)(gown, gx, slope, vp)
-    mid_rows = mid // strips
-    width = 9 * mid
-    assert width < 27 * channels <= 2 * width
-    dg_own, prediction = lax.optimization_barrier((dg_own, prediction))
-    dg_own = dg_own.reshape(groups, 2, half_rows, 9 * mid)
-    own_got = far_swap(dg_own)
-    grad_l, grad_r, apart_got, sg_in = lax.optimization_barrier((grad_l, grad_r, apart_got, sg_in))
-    smine, ssend = vmem_call(
-        strided_grad_body,
-        (sds((strips, mid_rows, width), F32), sds((strips, mid_rows, width), BF16)),
-        7,
-        scalars=1,
-    )(slab_id, gown, gx, grad_l, grad_r, slope, vp, sg_in)
     sg = (smine + swap(ssend).astype(F32)).astype(BF16).reshape(groups, 2, mid_rows, width)
     own = far_sum(dg_own, own_got)
     sent = jnp.concatenate(
@@ -561,6 +562,7 @@
         ],
         axis=0,
     )
+    sent, apart_got = lax.optimization_barrier((sent, apart_got))
     got = pair_swap(sent).astype(F32)
     own = pick(own, parity, 0) + got[groups * mid_rows :]
     sg = pick(sg, parity, 1).astype(F32) + got[: groups * mid_rows].reshape(groups, mid_rows, width)

time: 76.8 us -> 75.9 us (0.988)
  waiting for transfers between devices: 18.5 us -> 16 us
  starting transfers between devices: 33 us -> 34.5 us
    ppermute x6, waiting for transfers between devices: 8.48 us -> 5.77 us  [far_swap(): lax.ppermute(pick(chunks, places[d], 0).astype(BF16), 'strip', [(i, (i +...]
    ppermute x2, waiting for transfers between devices: 5.11 us -> 6.73 us  [pair_swap(): return lax.ppermute(value, 'strip', [(i, i ^ 1) for i in range(strips)])]
    ppermute x8, waiting for transfers between devices: 2.61 us -> 1.19 us  [swap(): return lax.ppermute(value, 'slab', [(0, 1), (1, 0)])]
    ppermute x6, starting transfers between devices: 9.48 us -> 10.8 us  [far_swap(): lax.ppermute(pick(chunks, places[d], 0).astype(BF16), 'strip', [(i, (i +...]
  transfers between devices with their start and end apart: 22 -> 22, of which waited for: 10 -> 10; matrix products, arithmetic and copies ran while one was open for 0% -> 1% of each run, Pallas kernels for 19% -> 20%
where the time goes in v7:
time: 75.9 us; the launch traced here: 75.6 us
  starting transfers between devices  34.5 us (45%)
  Pallas kernels  20.1 us (26%)
  waiting for transfers between devices  16 us (21%)
  other arithmetic  2.03 us (3%)
  local copies, waits for them, and re-layouts  1.77 us (2%)
  between operations  1.17 us (2%)
    ppermute x6, starting transfers between devices, shift_along(): return lax.ppermute(value, axis, pairs)  18 us
    ppermute x6, starting transfers between devices, far_swap(): lax.ppermute(pick(chunks, places[d], 0).astype(BF16), 'strip', [(i, (i +...  10.8 us
    ppermute x2, waiting for transfers between devices, pair_swap(): return lax.ppermute(value, 'strip', [(i, i ^ 1) for i in range(strips)])  6.73 us
    ppermute x6, waiting for transfers between devices, far_swap(): lax.ppermute(pick(chunks, places[d], 0).astype(BF16), 'strip', [(i, (i +...  5.77 us
    pallas_call x1, Pallas kernels, local(): vmem_call(inner, (sds((orows, pairs, 6 * mid, lanes), BF16), sds((orows,...  4.41 us
    ppermute x2, starting transfers between devices, pair_swap(): return lax.ppermute(value, 'strip', [(i, i ^ 1) for i in range(strips)])  3.7 us
    pallas_call x1, Pallas kernels, local(): vmem_call(split_body, (sds((pairs, (rows_in + 1) * 9 * channels, lanes),...  3.54 us
    pallas_call x1, Pallas kernels, local(): vmem_call(outer, (sds((orows, 2, outs, lanes), BF16), sds((orows, 2, outs...  2.71 us
  transfers between devices with their start and end apart: 22, of which 10 were waited for; matrix products, arithmetic and copies ran while one was open for 1% of the time, Pallas kernels for 20%

profile of v7, /device:TPU:0, one launch (start us, length us, event | category | flops | bytes accessed | tf_op | source)
XLA Modules:
  0.0 75.6 jit_solution(7318183400994993185)
XLA Ops:
  0.7 1.6 %copy-done = bf16[64,4,16,256]{3,2,1,0:T(8,128)(2,1)S(1)} copy-done((bf16[64,4,16,256]{3,2,1,0:T(8,128)(2,1)S(1)}, bf16[64,4,16,256]{3,2,1,0:T(8,128)(2,1)}, u32[]{:S(2)}) %copy-start) | copy-done | bytes 2097176
  2.3 0.4 shard_map.67
  2.7 0.0 copy-start.4
  2.8 0.0 copy-start.2
  2.8 5.1 %collective-permute-start = (bf16[4,64,256]{2,1,0:T(8,128)(2,1)S(1)}, bf16[4,64,256]{2,1,0:T(8,128)(2,1)S(1)}, u32[]{:S(2)}, u32[]{:S(2)}) collective-permute-start(bf16[4,64,256]{2,1,0:T(8,128)(2,1)S(1)} %shard_map.67), channel_id=1, source_target_pairs={{0,1},{1,2},{2,3},{3,4},{4,5},{5,6},{6,7},{8,9},{9,10},{10,11},{11... | collective-permute-start | bytes 393224 | tf_op jit(solution)/shard_map/ppermute | solution.py:375
  7.9 3.5 %shard_map.68 = (bf16[4,2880,256]{2,1,0:T(8,128)(2,1)S(1)}, bf16[1024,256]{1,0:T(8,128)(2,1)S(1)}) custom-call(bf16[64,4,16,256]{3,2,1,0:T(8,128)(2,1)S(1)} %copy-done.1), custom_call_target="tpu_custom_call" | custom-call | tf_op jit(solution)/shard_map/pallas_call | solution.py:410
  11.5 0.0 collective-permute-done.hcol_ref
  11.5 1.5 %collective-permute-start.1 = (bf16[1088,256]{1,0:T(8,128)(2,1)S(1)}, bf16[1088,256]{1,0:T(8,128)(2,1)S(1)}, u32[]{:S(2)}, u32[]{:S(2)}) collective-permute-start(bf16[1088,256]{1,0:T(8,128)(2,1)S(1)} %pad_maximum_fusion), channel_id=1, source_target_pairs={{0,8},{1,9},{2,10},{3,11},{4,12},{5,13},{6,14},{7,15},{16,24},{17,... | collective-permute-start | bytes 1671176 | tf_op jit(solution)/shard_map/ppermute | solution.py:375
  13.1 0.5 shard_map.69
  13.6 1.0 %collective-permute-done.1.hrow_ref = bf16[1088,256]{1,0:T(8,128)(2,1)S(1)} collective-permute-done((bf16[1088,256]{1,0:T(8,128)(2,1)S(1)}, bf16[1088,256]{1,0:T(8,128)(2,1)S(1)}, u32[]{:S(2)}, u32[]{:S(2)}) %collective-permute-start.1) | collective-permute-done | bytes 557088 | tf_op jit(solution)/shard_map/ppermute | solution.py:375
  14.6 2.2 %shard_map.70 = (bf16[4,2880,256]{2,1,0:T(8,128)(2,1)S(1)}, bf16[2,4,128,256]{3,2,1,0:T(8,128)(2,1)S(1)}, bf16[2,128,256]{2,1,0:T(8,128)(2,1)S(1)}, bf16[2,128,2...) custom-call(bf16[4,2880,256]{2,1,0:T(8,128)(2,1)S(1)} %get-tuple-element.56.own_ref, ...), custom_call_target="tpu_custom_call" | custom-call | tf_op jit(solution)/shard_map/pallas_call | solution.py:438
  16.7 0.4 collective-permute-start.2
  17.2 3.4 %collective-permute-start.3 = (bf16[2,128,256]{2,1,0:T(8,128)(2,1)S(1)}, bf16[2,128,256]{2,1,0:T(8,128)(2,1)S(1)}, u32[]{:S(2)}, u32[]{:S(2)}) collective-permute-start(bf16[2,128,256]{2,1,0:T(8,128)(2,1)S(1)} %get-tuple-element.65), channel_id=1, source_target_pairs={{0,1},{1,2},{2,3},{3,4},{4,5},{5,6},{6,7},{8,9},{9,10},{10,11},{11... | collective-permute-start | bytes 393224 | tf_op jit(solution)/shard_map/ppermute | solution.py:375
  20.6 1.5 %collective-permute-start.4 = (bf16[2,128,256]{2,1,0:T(8,128)(2,1)S(1)}, bf16[2,128,256]{2,1,0:T(8,128)(2,1)S(1)}, u32[]{:S(2)}, u32[]{:S(2)}) collective-permute-start(bf16[2,128,256]{2,1,0:T(8,128)(2,1)S(1)} %get-tuple-element.66), channel_id=1, source_target_pairs={{1,0},{2,1},{3,2},{4,3},{5,4},{6,5},{7,6},{9,8},{10,9},{11,10},{12... | collective-permute-start | bytes 393224 | tf_op jit(solution)/shard_map/ppermute | solution.py:375
  22.1 0.5 shard_map.71.refs_4_.refs_7_
  22.6 0.0 collective-permute-done.2.refs_1_
  22.7 4.4 %shard_map.72 = (bf16[2,4,768,256]{3,2,1,0:T(8,128)(2,1)S(1)}, bf16[2,2,256,256]{3,2,1,0:T(8,128)(2,1)S(1)}, f32[256,2304]{1,0:T(8,128)S(1)}, f32[2,4,256,256]{3,2,1,0:T(8,128)S(1)}) custom-call(bf16[2,4,128,256]{3,2,1,0:T(8,128)(2,1)S(1)} %get-tuple-element.61.refs_0_, bf16[2,4,128,256]{3,2,1,0:T(8,128)(2,1)S(1)} %collective-permute-done.2.refs_1_, ...), custom_call_target="tpu_custom_call" | custom-call | tf_op jit(solution)/shard_map/pallas_call | solution.py:461
  27.1 0.0 collective-permute-done.3.refs_1_
  27.1 1.3 %collective-permute-done.4.refs_2_ = bf16[2,128,256]{2,1,0:T(8,128)(2,1)S(1)} collective-permute-done((bf16[2,128,256]{2,1,0:T(8,128)(2,1)S(1)}, bf16[2,128,256]{2,1,0:T(8,128)(2,1)S(1)}, u32[]{:S(2)}, u32[]{:S(2)}) %collective-permute-start.4) | collective-permute-done | bytes 131104 | tf_op jit(solution)/shard_map/ppermute | solution.py:375
  28.4 0.0 collective-permute-start.5
  28.4 0.5 collective-permute-start.6
  28.9 0.8 %collective-permute-done.5.refs_3_ = bf16[2,128,256]{2,1,0:T(8,128)(2,1)S(1)} collective-permute-done((bf16[2,128,256]{2,1,0:T(8,128)(2,1)S(1)}, bf16[2,128,256]{2,1,0:T(8,128)(2,1)S(1)}, u32[]{:S(2)}, u32[]{:S(2)}) %collective-permute-start.5) | collective-permute-done | bytes 131104 | tf_op jit(solution)/shard_map/ppermute | solution.py:379
  29.7 0.2 collective-permute-done.6.refs_4_
  29.9 2.7 %shard_map.73 = (bf16[2,2,256,256]{3,2,1,0:T(8,128)(2,1)S(1)}, bf16[2,2,256,256]{3,2,1,0:T(8,128)(2,1)S(1)}, bf16[2,2,768,256]{3,2,1,0:T(8,128)(2,1)S(1)}, f32[2...) custom-call(bf16[2,4,768,256]{3,2,1,0:T(8,128)(2,1)S(1)} %get-tuple-, ...), custom_call_target="tpu_custom_call" | custom-call | tf_op jit(solution)/shard_map/pallas_call | solution.py:477
  32.6 0.4 collective-permute-start.9
  33.0 1.8 %shard_map.74 = (f32[8,16,1152]{2,1,0:T(8,128)S(1)}, bf16[8,16,1152]{2,1,0:T(8,128)(2,1)S(1)}, bf16[8,32,1152]{2,1,0:T(8,128)(2,1)S(1)}) custom-call(s32[1]{0:T(128)} %bitcast.1.slab_ref, bf16[2,2,256,256]{3,2,1,0:T(8,128)(2,1)S(1)} %get-tuple-element.74.res_ref, bf16[2,4,768,256]{3,2,1,0:T(8,128)(2,1)S(1)} %get-tuple-element.68.refs_0_.hs_ref, ...), custom_call_target="tpu_custom_call" | custom-call | tf_op jit(solution)/shard_map/pallas_call | solution.py:501
  34.9 0.2 collective-permute-start.7
  35.1 0.3 collective-permute-start.8
  35.4 0.0 collective-permute-done.9
  35.4 0.1 fusion.14
  35.5 1.3 %collective-permute-start.11 = (bf16[2,128,256]{2,1,0:T(8,128)(2,1)S(1)}, bf16[2,128,256]{2,1,0:T(8,128)(2,1)S(1)}, u32[]{:S(2)}, u32[]{:S(2)}) collective-permute-start(bf16[2,128,256]{2,1,0:T(8,128)(2,1)S(1)} %get-tuple-element.106), channel_id=1, source_target_pairs={{1,0},{2,1},{3,2},{4,3},{5,4},{6,5},{7,6},{9,8},{10,9},{11,10},{12... | collective-permute-start | bytes 393224 | tf_op jit(solution)/shard_map/ppermute | solution.py:375
  36.8 5.2 %collective-permute-start.10 = (bf16[2,128,256]{2,1,0:T(8,128)(2,1)S(1)}, bf16[2,128,256]{2,1,0:T(8,128)(2,1)S(1)}, u32[]{:S(2)}, u32[]{:S(2)}) collective-permute-start(bf16[2,128,256]{2,1,0:T(8,128)(2,1)S(1)} %get-tuple-element.107), channel_id=1, source_target_pairs={{0,1},{1,2},{2,3},{3,4},{4,5},{5,6},{6,7},{8,9},{9,10},{10,11},{11... | collective-permute-start | bytes 393224 | tf_op jit(solution)/shard_map/ppermute | solution.py:375
  42.0 0.0 collective-permute-done.7
  42.0 0.1 add_convert_fusion.1
  42.1 2.6 %collective-permute-start.12 = (bf16[2,16,1152]{2,1,0:T(8,128)(2,1)S(1)}, bf16[2,16,1152]{2,1,0:T(8,128)(2,1)S(1)}, u32[]{:S(2)}, u32[]{:S(2)}) collective-permute-start(bf16[2,16,1152]{2,1,0:T(8,128)(2,1)S(1)} %get-tuple-element.112), channel_id=1, source_target_pairs={{0,2},{1,3},{2,4},{3,5},{4,6},{5,7},{6,0},{7,1},{8,10},{9,11},{10,... | collective-permute-start | bytes 221192 | tf_op jit(solution)/shard_map/ppermute | solution.py:520
  44.7 2.1 %collective-permute-start.14 = (bf16[2,16,1152]{2,1,0:T(8,128)(2,1)S(1)}, bf16[2,16,1152]{2,1,0:T(8,128)(2,1)S(1)}, u32[]{:S(2)}, u32[]{:S(2)}) collective-permute-start(bf16[2,16,1152]{2,1,0:T(8,128)(2,1)S(1)} %get-tuple-element.113), channel_id=1, source_target_pairs={{0,6},{1,7},{2,0},{3,1},{4,2},{5,3},{6,4},{7,5},{8,14},{9,15},{10,... | collective-permute-start | bytes 221192 | tf_op jit(solution)/shard_map/ppermute | solution.py:520
  46.8 0.9 %collective-permute-start.13 = (bf16[2,16,1152]{2,1,0:T(8,128)(2,1)S(1)}, bf16[2,16,1152]{2,1,0:T(8,128)(2,1)S(1)}, u32[]{:S(2)}, u32[]{:S(2)}) collective-permute-start(bf16[2,16,1152]{2,1,0:T(8,128)(2,1)S(1)} %get-tuple-element.114), channel_id=1, source_target_pairs={{0,4},{1,5},{2,6},{3,7},{4,0},{5,1},{6,2},{7,3},{8,12},{9,13},{10,... | collective-permute-start | bytes 221192 | tf_op jit(solution)/shard_map/ppermute | solution.py:520
  47.8 1.2 %shard_map.75.sum_ref = f32[128,1728]{1,0:T(8,128)S(1)} custom-call(f32[2,4,128,256]{3,2,1,0:T(8,128)S(1)} %get-tuple-element.73.gown_ref, bf16[2,4,128,256]{3,2,1,0:T(8,128)(2,1)S(1)} %collective-permute-done.8.gx_ref, f32[2,4,128,256]{3,2,1,0:T(8,128)S(1)} %get-tuple-element.83.slope_ref, bf16[4,2880,256]{2,1,0:T(8,128)(2,1)S(1)} %get-tuple-element.84.vp_ref), custom_call_target="tpu_custom_call" | custom-call | tf_op jit(solution)/shard_map/pallas_call | solution.py:541
  49.0 0.0 collective-permute-done.11.gr_ref
  49.0 2.0 %collective-permute-start.16 = (bf16[4,32,1152]{2,1,0:T(8,128)(2,1)S(1)}, bf16[4,32,1152]{2,1,0:T(8,128)(2,1)S(1)}, u32[]{:S(2)}, u32[]{:S(2)}) collective-permute-start(bf16[4,32,1152]{2,1,0:T(8,128)(2,1)S(1)} %dynamic-slice_bitcast_fusion), channel_id=1, source_target_pairs={{0,1},{1,0},{2,3},{3,2},{4,5},{5,4},{6,7},{7,6},{8,9},{9,8},{10,11... | collective-permute-start | bytes 884744 | tf_op jit(solution)/shard_map/ppermute | solution.py:516
  51.0 1.2 %shard_map.76 = (f32[8,16,1152]{2,1,0:T(8,128)S(1)}, bf16[8,16,1152]{2,1,0:T(8,128)(2,1)S(1)}) custom-call(s32[1]{0:T(128)} %bitcast.1.slab_ref, f32[2,4,128,256]{3,2,1,0:T(8,128)S(1)} %get-tuple-element.73.gown_ref, bf16[2,4,128,256]{3,2,1,0:T(8,128)(2,1)S(1)} %collective-permute-done.8.gx_ref, bf16[2,128,256]{2,1,0:T(8,128)(2,1)S(1)} %collective-permute-done.10.gl_ref, ...), custom_call_target="tpu_custom_call" | custom-call | tf_op jit(solution)/shard_map/pallas_call | solution.py:543
  52.1 0.1 collective-permute-start.15
  52.2 0.0 collective-permute-done.12
  52.2 0.0 collective-permute-done.14
  52.2 1.3 %collective-permute-done.13 = bf16[2,16,1152]{2,1,0:T(8,128)(2,1)S(1)} collective-permute-done((bf16[2,16,1152]{2,1,0:T(8,128)(2,1)S(1)}, bf16[2,16,1152]{2,1,0:T(8,128)(2,1)S(1)}, u32[]{:S(2)}, u32[]{:S(2)}) %collective-permute-start.13) | collective-permute-done | bytes 73760 | tf_op jit(solution)/shard_map/ppermute | solution.py:520
  53.6 0.1 collective-permute-done.15
  53.8 0.1 add_convert_fusion
  53.9 3.0 %collective-permute-done.16 = bf16[4,32,1152]{2,1,0:T(8,128)(2,1)S(1)} collective-permute-done((bf16[4,32,1152]{2,1,0:T(8,128)(2,1)S(1)}, bf16[4,32,1152]{2,1,0:T(8,128)(2,1)S(1)}, u32[]{:S(2)}, u32[]{:S(2)}) %collective-permute-start.16) | collective-permute-done | bytes 294944 | tf_op jit(solution)/shard_map/ppermute | solution.py:516
  56.9 1.7 %collective-permute-start.17 = (bf16[80,1152]{1,0:T(8,128)(2,1)S(1)}, bf16[80,1152]{1,0:T(8,128)(2,1)S(1)}, u32[]{:S(2)}, u32[]{:S(2)}) collective-permute-start(bf16[80,1152]{1,0:T(8,128)(2,1)S(1)} %pad_maximum_fusion.3), channel_id=1, source_target_pairs={{0,1},{1,0},{2,3},{3,2},{4,5},{5,4},{6,7},{7,6},{8,9},{9,8},{10,11... | collective-permute-start | bytes 552968 | tf_op jit(solution)/shard_map/ppermute | solution.py:516
  58.6 0.1 convert_add_fusion
  58.7 3.7 %collective-permute-done.17 = bf16[80,1152]{1,0:T(8,128)(2,1)S(1)} collective-permute-done((bf16[80,1152]{1,0:T(8,128)(2,1)S(1)}, bf16[80,1152]{1,0:T(8,128)(2,1)S(1)}, u32[]{:S(2)}, u32[]{:S(2)}) %collective-permute-start.17) | collective-permute-done | bytes 184352 | tf_op jit(solution)/shard_map/ppermute | solution.py:516
  62.5 0.1 fusion.16
  62.6 1.5 %collective-permute-start.18 = (bf16[48,1152]{1,0:T(8,128)(2,1)S(1)}, bf16[48,1152]{1,0:T(8,128)(2,1)S(1)}, u32[]{:S(2)}, u32[]{:S(2)}) collective-permute-start(bf16[48,1152]{1,0:T(8,128)(2,1)S(1)} %get-tuple-element.103), channel_id=1, source_target_pairs={{0,2},{1,3},{2,4},{3,5},{4,6},{5,7},{6,0},{7,1},{8,10},{9,11},{10,... | collective-permute-start | bytes 331784 | tf_op jit(solution)/shard_map/ppermute | solution.py:520
  64.1 0.9 %collective-permute-start.19 = (bf16[48,1152]{1,0:T(8,128)(2,1)S(1)}, bf16[48,1152]{1,0:T(8,128)(2,1)S(1)}, u32[]{:S(2)}, u32[]{:S(2)}) collective-permute-start(bf16[48,1152]{1,0:T(8,128)(2,1)S(1)} %get-tuple-element.104), channel_id=1, source_target_pairs={{0,4},{1,5},{2,6},{3,7},{4,0},{5,1},{6,2},{7,3},{8,12},{9,13},{10,... | collective-permute-start | bytes 331784 | tf_op jit(solution)/shard_map/ppermute | solution.py:520
  64.9 2.8 %collective-permute-start.20 = (bf16[48,1152]{1,0:T(8,128)(2,1)S(1)}, bf16[48,1152]{1,0:T(8,128)(2,1)S(1)}, u32[]{:S(2)}, u32[]{:S(2)}) collective-permute-start(bf16[48,1152]{1,0:T(8,128)(2,1)S(1)} %get-tuple-element.105), channel_id=1, source_target_pairs={{0,6},{1,7},{2,0},{3,1},{4,2},{5,3},{6,4},{7,5},{8,14},{9,15},{10,... | collective-permute-start | bytes 331784 | tf_op jit(solution)/shard_map/ppermute | solution.py:520
  67.7 1.6 %collective-permute-done.18 = bf16[48,1152]{1,0:T(8,128)(2,1)S(1)} collective-permute-done((bf16[48,1152]{1,0:T(8,128)(2,1)S(1)}, bf16[48,1152]{1,0:T(8,128)(2,1)S(1)}, u32[]{:S(2)}, u32[]{:S(2)}) %collective-permute-start.18) | collective-permute-done | bytes 110624 | tf_op jit(solution)/shard_map/ppermute | solution.py:520
  69.3 2.8 %collective-permute-done.19 = bf16[48,1152]{1,0:T(8,128)(2,1)S(1)} collective-permute-done((bf16[48,1152]{1,0:T(8,128)(2,1)S(1)}, bf16[48,1152]{1,0:T(8,128)(2,1)S(1)}, u32[]{:S(2)}, u32[]{:S(2)}) %collective-permute-start.19) | collective-permute-done | bytes 110624 | tf_op jit(solution)/shard_map/ppermute | solution.py:520
  72.2 0.0 collective-permute-done.20
  72.2 0.1 fusion.6
  72.3 0.1 collective-permute-start.21
  72.3 1.6 %shard_map.77 = bf16[256,2,8,128]{3,2,1,0:T(8,128)(2,1)} custom-call(bf16[2,2,256,256]{3,2,1,0:T(8,128)(2,1)S(1)} %get-tuple-element.64.inner_ref, bf16[2,2,256,256]{3,2,1,0:T(8,128)(2,1)S(1)} %get-tuple-element.89.outer_ref), custom_call_target="tpu_custom_call" | custom-call | tf_op jit(solution)/shard_map/pallas_call | solution.py:550
  74.0 0.0 collective-permute-done.21
  74.1 0.7 pad_maximum_fusion.4
  74.8 0.8 %pad_maximum_fusion.1 = f32[32,3456]{1,0:T(8,128)} fusion(f32[32,1152]{1,0:T(8,128)S(1)} %slice.61, f32[16,1152]{1,0:T(8,128)S(1)} %slice.60, f32[16,1152]{1,0:T(8,128)S(1)} %get-tuple-element.110, f32[32,1152]{1,0:T(8,128)S(1)} %slice.58), kind=kLoop, calls=%fused_computation.12 | loop fusion | flops 331776 | bytes 884736 | tf_op jit(solution)/shard_map/concatenate | solution.py:576
  (28 shorter events, 0.4 us)
Async XLA Ops:
  0.7 1.6 %copy-start = (bf16[64,4,16,256]{3,2,1,0:T(8,128)(2,1)S(1)}, bf16[64,4,16,256]{3,2,1,0:T(8,128)(2,1)}, u32[]{:S(2)}) copy-start(bf16[64,4,16,256]{3,2,1,0:T(8,128)(2,1)} %vol_ref.3) | copy-start | bytes 6291460
  2.3 5.6 %copy-start.1 = (bf16[64,4,16,256]{3,2,1,0:T(8,128)(2,1)S(1)}, bf16[64,4,16,256]{3,2,1,0:T(8,128)(2,1)}, u32[]{:S(2)}) copy-start(bf16[64,4,16,256]{3,2,1,0:T(8,128)(2,1)} %vol_ref.3) | copy-start | bytes 6291460
  2.7 10.3 %copy-start.4 = (bf16[128,1728]{0,1:T(8,128)(2,1)S(1)}, bf16[128,1728]{0,1:T(8,128)(2,1)}, u32[]{:S(2)}) copy-start(bf16[128,1728]{0,1:T(8,128)(2,1)} %param.6) | copy-start | bytes 1327108
  2.8 10.3 %copy-start.2 = (bf16[256,3456]{1,0:T(8,128)(2,1)S(1)}, bf16[256,3456]{1,0:T(8,128)(2,1)}, u32[]{:S(2)}) copy-start(bf16[256,3456]{1,0:T(8,128)(2,1)} %wd_ref.1) | copy-start | bytes 5308420
  2.8 8.7 %collective-permute-start = (bf16[4,64,256]{2,1,0:T(8,128)(2,1)S(1)}, bf16[4,64,256]{2,1,0:T(8,128)(2,1)S(1)}, u32[]{:S(2)}, u32[]{:S(2)}) collective-permute-start(bf16[4,64,256]{2,1,0:T(8,128)(2,1)S(1)} %shard_map.67), channel_id=1, source_target_pairs={{0,1},{1,2},{2,3},{3,4},{4,5},{5,6},{6,7},{8,9},{9,10},{10,11},{11... | collective-permute-start | bytes 393224 | tf_op jit(solution)/shard_map/ppermute | solution.py:375
  11.5 3.0 %collective-permute-start.1 = (bf16[1088,256]{1,0:T(8,128)(2,1)S(1)}, bf16[1088,256]{1,0:T(8,128)(2,1)S(1)}, u32[]{:S(2)}, u32[]{:S(2)}) collective-permute-start(bf16[1088,256]{1,0:T(8,128)(2,1)S(1)} %pad_maximum_fusion), channel_id=1, source_target_pairs={{0,8},{1,9},{2,10},{3,11},{4,12},{5,13},{6,14},{7,15},{16,24},{17,... | collective-permute-start | bytes 1671176 | tf_op jit(solution)/shard_map/ppermute | solution.py:375
  14.6 7.5 %copy-start.3 = (bf16[256,2,8,128]{3,2,1,0:T(8,128)(2,1)S(1)}, bf16[256,2,8,128]{3,2,1,0:T(8,128)(2,1)}, u32[]{:S(2)}) copy-start(bf16[256,2,8,128]{3,2,1,0:T(8,128)(2,1)} %tgt_ref.1) | copy-start | bytes 3145732
  16.7 5.9 %collective-permute-start.2 = (bf16[2,4,128,256]{3,2,1,0:T(8,128)(2,1)S(1)}, bf16[2,4,128,256]{3,2,1,0:T(8,128)(2,1)S(1)}, u32[]{:S(2)}, u32[]{:S(2)}) collective-permute-start(bf16[2,4,128,256]{3,2,1,0:T(8,128)(2,1)S(1)} %get-tuple-element.61.refs_0_), channel_id=1, source_target_pairs={{0,8},{8,0},{1,9},{9,1},{2,10},{10,2},{3,11},{11,3},{4,12},{12,4},... | collective-permute-start | bytes 1572872 | tf_op jit(solution)/shard_map/ppermute | solution.py:379
  17.2 9.9 %collective-permute-start.3 = (bf16[2,128,256]{2,1,0:T(8,128)(2,1)S(1)}, bf16[2,128,256]{2,1,0:T(8,128)(2,1)S(1)}, u32[]{:S(2)}, u32[]{:S(2)}) collective-permute-start(bf16[2,128,256]{2,1,0:T(8,128)(2,1)S(1)} %get-tuple-element.65), channel_id=1, source_target_pairs={{0,1},{1,2},{2,3},{3,4},{4,5},{5,6},{6,7},{8,9},{9,10},{10,11},{11... | collective-permute-start | bytes 393224 | tf_op jit(solution)/shard_map/ppermute | solution.py:375
  20.6 7.8 %collective-permute-start.4 = (bf16[2,128,256]{2,1,0:T(8,128)(2,1)S(1)}, bf16[2,128,256]{2,1,0:T(8,128)(2,1)S(1)}, u32[]{:S(2)}, u32[]{:S(2)}) collective-permute-start(bf16[2,128,256]{2,1,0:T(8,128)(2,1)S(1)} %get-tuple-element.66), channel_id=1, source_target_pairs={{1,0},{2,1},{3,2},{4,3},{5,4},{6,5},{7,6},{9,8},{10,9},{11,10},{12... | collective-permute-start | bytes 393224 | tf_op jit(solution)/shard_map/ppermute | solution.py:375
  28.4 1.3 %collective-permute-start.5 = (bf16[2,128,256]{2,1,0:T(8,128)(2,1)S(1)}, bf16[2,128,256]{2,1,0:T(8,128)(2,1)S(1)}, u32[]{:S(2)}, u32[]{:S(2)}) collective-permute-start(bf16[2,128,256]{2,1,0:T(8,128)(2,1)S(1)} %collective-permute-done.3.refs_1_), channel_id=1, source_target_pairs={{0,8},{8,0},{1,9},{9,1},{2,10},{10,2},{3,11},{11,3},{4,12},{12,4},... | collective-permute-start | bytes 393224 | tf_op jit(solution)/shard_map/ppermute | solution.py:379
  28.4 1.5 %collective-permute-start.6 = (bf16[2,128,256]{2,1,0:T(8,128)(2,1)S(1)}, bf16[2,128,256]{2,1,0:T(8,128)(2,1)S(1)}, u32[]{:S(2)}, u32[]{:S(2)}) collective-permute-start(bf16[2,128,256]{2,1,0:T(8,128)(2,1)S(1)} %collective-permute-done.4.refs_2_), channel_id=1, source_target_pairs={{0,8},{8,0},{1,9},{9,1},{2,10},{10,2},{3,11},{11,3},{4,12},{12,4},... | collective-permute-start | bytes 393224 | tf_op jit(solution)/shard_map/ppermute | solution.py:379
  32.6 2.8 %collective-permute-start.9 = (bf16[2,2,128,256]{3,2,1,0:T(8,128)(2,1)S(1)}, bf16[2,2,128,256]{3,2,1,0:T(8,128)(2,1)S(1)}, u32[]{:S(2)}, u32[]{:S(2)}) collective-permute-start(bf16[2,2,128,256]{3,2,1,0:T(8,128)(2,1)S(1)} %get-tuple-element.82), channel_id=1, source_target_pairs={{0,8},{8,0},{1,9},{9,1},{2,10},{10,2},{3,11},{11,3},{4,12},{12,4},... | collective-permute-start | bytes 786440 | tf_op jit(solution)/shard_map/ppermute | solution.py:379
  34.9 7.1 %collective-permute-start.7 = (bf16[8,16,1152]{2,1,0:T(8,128)(2,1)S(1)}, bf16[8,16,1152]{2,1,0:T(8,128)(2,1)S(1)}, u32[]{:S(2)}, u32[]{:S(2)}) collective-permute-start(bf16[8,16,1152]{2,1,0:T(8,128)(2,1)S(1)} %get-tuple-element.78), channel_id=1, source_target_pairs={{0,8},{8,0},{1,9},{9,1},{2,10},{10,2},{3,11},{11,3},{4,12},{12,4},... | collective-permute-start | bytes 884744 | tf_op jit(solution)/shard_map/ppermute | solution.py:379
  35.1 7.0 %collective-permute-start.8 = (bf16[2,4,128,256]{3,2,1,0:T(8,128)(2,1)S(1)}, bf16[2,4,128,256]{3,2,1,0:T(8,128)(2,1)S(1)}, u32[]{:S(2)}, u32[]{:S(2)}) collective-permute-start(bf16[2,4,128,256]{3,2,1,0:T(8,128)(2,1)S(1)} %get-tuple-element.79), channel_id=1, source_target_pairs={{0,8},{8,0},{1,9},{9,1},{2,10},{10,2},{3,11},{11,3},{4,12},{12,4},... | collective-permute-start | bytes 1572872 | tf_op jit(solution)/shard_map/ppermute | solution.py:379
  35.5 13.5 %collective-permute-start.11 = (bf16[2,128,256]{2,1,0:T(8,128)(2,1)S(1)}, bf16[2,128,256]{2,1,0:T(8,128)(2,1)S(1)}, u32[]{:S(2)}, u32[]{:S(2)}) collective-permute-start(bf16[2,128,256]{2,1,0:T(8,128)(2,1)S(1)} %get-tuple-element.106), channel_id=1, source_target_pairs={{1,0},{2,1},{3,2},{4,3},{5,4},{6,5},{7,6},{9,8},{10,9},{11,10},{12... | collective-permute-start | bytes 393224 | tf_op jit(solution)/shard_map/ppermute | solution.py:375
  36.8 14.2 %collective-permute-start.10 = (bf16[2,128,256]{2,1,0:T(8,128)(2,1)S(1)}, bf16[2,128,256]{2,1,0:T(8,128)(2,1)S(1)}, u32[]{:S(2)}, u32[]{:S(2)}) collective-permute-start(bf16[2,128,256]{2,1,0:T(8,128)(2,1)S(1)} %get-tuple-element.107), channel_id=1, source_target_pairs={{0,1},{1,2},{2,3},{3,4},{4,5},{5,6},{6,7},{8,9},{9,10},{10,11},{11... | collective-permute-start | bytes 393224 | tf_op jit(solution)/shard_map/ppermute | solution.py:375
  42.1 10.1 %collective-permute-start.12 = (bf16[2,16,1152]{2,1,0:T(8,128)(2,1)S(1)}, bf16[2,16,1152]{2,1,0:T(8,128)(2,1)S(1)}, u32[]{:S(2)}, u32[]{:S(2)}) collective-permute-start(bf16[2,16,1152]{2,1,0:T(8,128)(2,1)S(1)} %get-tuple-element.112), channel_id=1, source_target_pairs={{0,2},{1,3},{2,4},{3,5},{4,6},{5,7},{6,0},{7,1},{8,10},{9,11},{10,... | collective-permute-start | bytes 221192 | tf_op jit(solution)/shard_map/ppermute | solution.py:520
  44.7 7.5 %collective-permute-start.14 = (bf16[2,16,1152]{2,1,0:T(8,128)(2,1)S(1)}, bf16[2,16,1152]{2,1,0:T(8,128)(2,1)S(1)}, u32[]{:S(2)}, u32[]{:S(2)}) collective-permute-start(bf16[2,16,1152]{2,1,0:T(8,128)(2,1)S(1)} %get-tuple-element.113), channel_id=1, source_target_pairs={{0,6},{1,7},{2,0},{3,1},{4,2},{5,3},{6,4},{7,5},{8,14},{9,15},{10,... | collective-permute-start | bytes 221192 | tf_op jit(solution)/shard_map/ppermute | solution.py:520
  46.8 6.7 %collective-permute-start.13 = (bf16[2,16,1152]{2,1,0:T(8,128)(2,1)S(1)}, bf16[2,16,1152]{2,1,0:T(8,128)(2,1)S(1)}, u32[]{:S(2)}, u32[]{:S(2)}) collective-permute-start(bf16[2,16,1152]{2,1,0:T(8,128)(2,1)S(1)} %get-tuple-element.114), channel_id=1, source_target_pairs={{0,4},{1,5},{2,6},{3,7},{4,0},{5,1},{6,2},{7,3},{8,12},{9,13},{10,... | collective-permute-start | bytes 221192 | tf_op jit(solution)/shard_map/ppermute | solution.py:520
  49.0 7.9 %collective-permute-start.16 = (bf16[4,32,1152]{2,1,0:T(8,128)(2,1)S(1)}, bf16[4,32,1152]{2,1,0:T(8,128)(2,1)S(1)}, u32[]{:S(2)}, u32[]{:S(2)}) collective-permute-start(bf16[4,32,1152]{2,1,0:T(8,128)(2,1)S(1)} %dynamic-slice_bitcast_fusion), channel_id=1, source_target_pairs={{0,1},{1,0},{2,3},{3,2},{4,5},{5,4},{6,7},{7,6},{8,9},{9,8},{10,11... | collective-permute-start | bytes 884744 | tf_op jit(solution)/shard_map/ppermute | solution.py:516
  52.1 1.6 %collective-permute-start.15 = (bf16[8,16,1152]{2,1,0:T(8,128)(2,1)S(1)}, bf16[8,16,1152]{2,1,0:T(8,128)(2,1)S(1)}, u32[]{:S(2)}, u32[]{:S(2)}) collective-permute-start(bf16[8,16,1152]{2,1,0:T(8,128)(2,1)S(1)} %get-tuple-element.98), channel_id=1, source_target_pairs={{0,8},{8,0},{1,9},{9,1},{2,10},{10,2},{3,11},{11,3},{4,12},{12,4},... | collective-permute-start | bytes 884744 | tf_op jit(solution)/shard_map/ppermute | solution.py:379
  56.9 5.5 %collective-permute-start.17 = (bf16[80,1152]{1,0:T(8,128)(2,1)S(1)}, bf16[80,1152]{1,0:T(8,128)(2,1)S(1)}, u32[]{:S(2)}, u32[]{:S(2)}) collective-permute-start(bf16[80,1152]{1,0:T(8,128)(2,1)S(1)} %pad_maximum_fusion.3), channel_id=1, source_target_pairs={{0,1},{1,0},{2,3},{3,2},{4,5},{5,4},{6,7},{7,6},{8,9},{9,8},{10,11... | collective-permute-start | bytes 552968 | tf_op jit(solution)/shard_map/ppermute | solution.py:516
  62.6 6.8 %collective-permute-start.18 = (bf16[48,1152]{1,0:T(8,128)(2,1)S(1)}, bf16[48,1152]{1,0:T(8,128)(2,1)S(1)}, u32[]{:S(2)}, u32[]{:S(2)}) collective-permute-start(bf16[48,1152]{1,0:T(8,128)(2,1)S(1)} %get-tuple-element.103), channel_id=1, source_target_pairs={{0,2},{1,3},{2,4},{3,5},{4,6},{5,7},{6,0},{7,1},{8,10},{9,11},{10,... | collective-permute-start | bytes 331784 | tf_op jit(solution)/shard_map/ppermute | solution.py:520
  64.1 8.1 %collective-permute-start.19 = (bf16[48,1152]{1,0:T(8,128)(2,1)S(1)}, bf16[48,1152]{1,0:T(8,128)(2,1)S(1)}, u32[]{:S(2)}, u32[]{:S(2)}) collective-permute-start(bf16[48,1152]{1,0:T(8,128)(2,1)S(1)} %get-tuple-element.104), channel_id=1, source_target_pairs={{0,4},{1,5},{2,6},{3,7},{4,0},{5,1},{6,2},{7,3},{8,12},{9,13},{10,... | collective-permute-start | bytes 331784 | tf_op jit(solution)/shard_map/ppermute | solution.py:520
  64.9 7.3 %collective-permute-start.20 = (bf16[48,1152]{1,0:T(8,128)(2,1)S(1)}, bf16[48,1152]{1,0:T(8,128)(2,1)S(1)}, u32[]{:S(2)}, u32[]{:S(2)}) collective-permute-start(bf16[48,1152]{1,0:T(8,128)(2,1)S(1)} %get-tuple-element.105), channel_id=1, source_target_pairs={{0,6},{1,7},{2,0},{3,1},{4,2},{5,3},{6,4},{7,5},{8,14},{9,15},{10,... | collective-permute-start | bytes 331784 | tf_op jit(solution)/shard_map/ppermute | solution.py:520
  72.3 1.7 %collective-permute-start.21 = (f32[64,1152]{1,0:T(8,128)S(1)}, f32[64,1152]{1,0:T(8,128)S(1)}, u32[]{:S(2)}, u32[]{:S(2)}) collective-permute-start(f32[64,1152]{1,0:T(8,128)S(1)} %pad_maximum_fusion.2), channel_id=1, source_target_pairs={{0,8},{8,0},{1,9},{9,1},{2,10},{10,2},{3,11},{11,3},{4,12},{12,4},... | collective-permute-start | bytes 884744 | tf_op jit(solution)/shard_map/ppermute | solution.py:379
